TPU v7x, 32 devices: a whole 2x2x4 slice. The times are simulated.
32 devices in a mesh: dp: 8 (over y, x, core), seq: 4 (over z).
Axes of the slice: x: 2, y: 2, z: 4, core: 2. Of those that a mesh axis runs over, the one named last changes fastest.
Arguments:
- tokens: bfloat16 [32, 1024, 1024], P('dp', 'seq'), may hold values from -6 to 6
- prefix_len: int32 [32], P('dp'), may hold values from 102 to 960, as said below
- norm1_gain: bfloat16 [1024], P(('dp', 'seq')), may hold values from 0.5 to 1.5
- query_weight: bfloat16 [1024, 512], P(('dp', 'seq')), may hold values from -0.1875 to 0.1875
- key_weight: bfloat16 [1024, 512], P(('dp', 'seq')), may hold values from -0.1875 to 0.1875
- value_weight: bfloat16 [1024, 1024], P(('dp', 'seq')), may hold values from -0.1875 to 0.1875
- gate_weight: bfloat16 [1024, 1024], P(('dp', 'seq')), may hold values from -0.1875 to 0.1875
- decay_down: bfloat16 [1024, 16], P(('dp', 'seq')), may hold values from -0.1875 to 0.1875
- decay_up: bfloat16 [16, 512], P(None, ('dp', 'seq')), may hold values from -1.5 to 1.5
- decay_bias: bfloat16 [512], P(('dp', 'seq')), may hold values from 0 to 10
- group_gain: bfloat16 [256], P(('dp', 'seq')), may hold values from 0.5 to 1.5
- out_weight: bfloat16 [1024, 1024], P(('dp', 'seq')), may hold values from -0.25 to 0.25
- norm2_gain: bfloat16 [1024], P(('dp', 'seq')), may hold values from 0.5 to 1.5
- ffn_gate: bfloat16 [1024, 2816], P(('dp', 'seq')), may hold values from -0.1875 to 0.1875
- ffn_up: bfloat16 [1024, 2816], P(('dp', 'seq')), may hold values from -0.1875 to 0.1875
- ffn_down: bfloat16 [2816, 1024], P(None, ('dp', 'seq')), may hold values from -0.21875 to 0.21875
- out_grad: bfloat16 [32, 1024, 1024], P('dp', 'seq'), may hold values from -6 to 6
Outputs:
- layer_out: bfloat16 [32, 1024, 1024], P('dp', 'seq')
- tokens_grad: float32 [32, 1024, 1024], P('dp', 'seq')
- norm1_gain_grad: float32 [1024], P(('dp', 'seq'))
- query_weight_grad: float32 [1024, 512], P(('dp', 'seq'))
- key_weight_grad: float32 [1024, 512], P(('dp', 'seq'))
- value_weight_grad: float32 [1024, 1024], P(('dp', 'seq'))
- gate_weight_grad: float32 [1024, 1024], P(('dp', 'seq'))
- decay_down_grad: float32 [1024, 16], P(('dp', 'seq'))
- decay_up_grad: float32 [16, 512], P(None, ('dp', 'seq'))
- decay_bias_grad: float32 [512], P(('dp', 'seq'))
- group_gain_grad: float32 [256], P(('dp', 'seq'))
- out_weight_grad: float32 [1024, 1024], P(('dp', 'seq'))
- norm2_gain_grad: float32 [1024], P(('dp', 'seq'))
- ffn_gate_grad: float32 [1024, 2816], P(('dp', 'seq'))
- ffn_up_grad: float32 [1024, 2816], P(('dp', 'seq'))
- ffn_down_grad: float32 [2816, 1024], P(None, ('dp', 'seq'))
Inputs may be any that keep to these rules, and one draw needn't show every extreme that they name: `prefix_len`: some sequence has a prefix of exactly 960 tokens.
All inputs are finite; a program needn't handle non-finite values.
Results may differ from a plain program's by a relative error of at most 0.033.
Values may be sent and summed in bfloat16 or wider, within the bound.
A program may use at most 256 MiB of HBM per device.

v0:
```python
from functools import partial

import jax
import jax.numpy as jnp
from jax import lax
from jax.sharding import PartitionSpec as P

KEYS = 512
VALS = 1024
HEADS = 4
SPAN = 64
HEAD_K = 128
HEAD_V = 256


norm_eps = 1e-05


def entering(part, axis, combine, identity):
    place = lax.axis_index(axis)
    gathered = jax.tree.map(lambda a: lax.all_gather(a, axis), part)
    state = jax.tree.map(lambda a, e: jnp.zeros_like(a) + jnp.asarray(e, a.dtype), part, identity)

    def entering_one(lap, state):
        return combine(
            state, jax.tree.map(lambda a: lax.dynamic_index_in_dim(a, lap, 0, False), gathered)
        )

    return lax.fori_loop(0, place, entering_one, state)


def carried_in(x, axis, join, neutral):
    count = lax.axis_size(axis)
    place = lax.axis_index(axis)
    ahead = count - 1 - place
    gathered = jax.tree.map(
        lambda a, kind: lax.all_gather(a.astype(kind), axis),
        x,
        jax.tree.map(lambda a: jnp.bfloat16 if a.dtype == jnp.float32 else a.dtype, x),
    )
    state = jax.tree.map(lambda a, e: jnp.zeros_like(a) + jnp.asarray(e, a.dtype), x, neutral)

    def carried_one(lap, state):
        source = count - 1 - lap
        return join(
            state,
            jax.tree.map(
                lambda a, own: lax.dynamic_index_in_dim(a, source, 0, False).astype(own.dtype),
                gathered,
                x,
            ),
        )

    return lax.fori_loop(0, ahead, carried_one, state)


def precise_summation(pattern, *operands):
    return jnp.einsum(
        pattern, *operands, precision=lax.Precision.HIGHEST, preferred_element_type=jnp.float32
    )


def project(inputs, weight):
    return jnp.einsum("std,de->ste", inputs, weight, preferred_element_type=jnp.float32)


def back_project(gradient, weight):
    return jnp.einsum("ste,de->std", gradient, weight, preferred_element_type=jnp.float32)


def weight_grad(inputs, gradient):
    return jnp.einsum("std,ste->de", inputs, gradient, preferred_element_type=jnp.float32)


def rms_scale(values):
    return lax.rsqrt(jnp.mean(values * values, axis=-1, keepdims=True) + norm_eps)


def rms_back(grad_unit, unit_rows, scale_rows):
    return scale_rows * (
        grad_unit - unit_rows * jnp.mean(grad_unit * unit_rows, axis=-1, keepdims=True)
    )


def silu_slope(values):
    logistic = jax.nn.sigmoid(values)
    return logistic * (1.0 + values * (1.0 - logistic))


def chain_combine(earlier, later):
    return (earlier[0] + later[0], jnp.exp(later[0])[..., None] * earlier[1] + later[1])


def lower_ones(extent):
    indices = jnp.arange(extent)
    return (indices[:, None] >= indices[None, :]).astype(jnp.float32)


def local_states(key_matrix, valued, decays):
    seq_count, tok_count, head_count, key_width = key_matrix.shape
    blocks = tok_count // SPAN
    key_blocks = key_matrix.reshape(seq_count, blocks, SPAN, head_count, key_width)
    value_blocks = valued.reshape(seq_count, blocks, SPAN, head_count, valued.shape[-1])
    decay_blocks = decays.reshape(seq_count, blocks, SPAN, head_count, key_width)
    cumulative_decay = precise_summation("ij,snjhk->snihk", lower_ones(SPAN), decay_blocks)
    running_totals = cumulative_decay[:, :, -1]
    shares = precise_summation(
        "snjhk,snjhv->snhkv",
        key_blocks * jnp.exp(running_totals[:, :, None] - cumulative_decay),
        value_blocks,
    )
    carried_state = jnp.zeros_like(shares[:, 0])
    starts = []
    for number in range(blocks):
        starts.append(carried_state)
        carried_state = (
            jnp.exp(running_totals[:, number])[..., None] * carried_state + shares[:, number]
        )
    return (
        jnp.sum(running_totals, axis=1),
        carried_state,
        jnp.stack(starts, axis=1),
        cumulative_decay,
        running_totals,
    )


def local_outputs(
    queries,
    key_matrix,
    valued,
    incoming,
    starts,
    cumulative_decay,
    running_totals,
    end_local=None,
    is_owner=None,
):
    seq_count, tok_count, head_count, key_width = queries.shape
    val_width = valued.shape[-1]
    blocks = tok_count // SPAN
    query_blocks = queries.reshape(seq_count, blocks, SPAN, head_count, key_width)
    key_blocks = key_matrix.reshape(seq_count, blocks, SPAN, head_count, key_width)
    value_blocks = valued.reshape(seq_count, blocks, SPAN, head_count, val_width)
    before = jnp.cumsum(running_totals, axis=1) - running_totals
    block_states = jnp.exp(before)[..., None] * incoming[:, None] + starts
    query_input = query_blocks * jnp.exp(cumulative_decay)
    key_in = key_blocks * jnp.exp(-cumulative_decay)
    attention_scores = precise_summation("snihk,snjhk->snhij", query_input, key_in) * lower_ones(
        SPAN
    )
    causal = precise_summation(
        "snhij,snjhv->snihv", attention_scores, value_blocks
    ) + precise_summation("snihk,snhkv->snihv", query_input, block_states)
    causal = causal.reshape(seq_count, tok_count, head_count, val_width)
    position_cum = (cumulative_decay + before[:, :, None]).reshape(
        seq_count, tok_count, head_count, key_width
    )
    places = jnp.arange(tok_count)
    select = (places[None, :] == end_local[:, None]).astype(jnp.float32)
    end_cum = precise_summation("st,sthk->shk", select, position_cum)
    keep_mask = (places[None, :] <= end_local[:, None]) & is_owner[:, None]
    exponent = jnp.where(keep_mask[:, :, None, None], end_cum[:, None] - position_cum, 0.0)
    weight_bundle = jnp.exp(exponent) * keep_mask.astype(jnp.float32)[:, :, None, None]
    partial_state = precise_summation("sthk,sthv->shkv", key_matrix * weight_bundle, valued)
    owner_weight = is_owner.astype(jnp.float32)[:, None, None, None]
    partial_state = partial_state + owner_weight * jnp.exp(end_cum)[..., None] * incoming
    return (causal, partial_state)


def chain_forward(total_dev, state_dev):
    identity = (jnp.zeros_like(total_dev), jnp.zeros_like(state_dev))
    return entering((total_dev, state_dev), "seq", chain_combine, identity)[1]


def chain_backward(total_dev, grad_in):
    identity = (jnp.zeros_like(total_dev), jnp.zeros_like(grad_in))
    return carried_in((total_dev, grad_in), "seq", chain_combine, identity)[1]


def ffn_owners(terms):
    return (
        lax.psum_scatter(terms[0], ("dp", "seq"), scatter_dimension=0, tiled=True),
        lax.psum_scatter(terms[1], ("dp", "seq"), scatter_dimension=0, tiled=True),
        lax.psum_scatter(terms[2], ("dp", "seq"), scatter_dimension=0, tiled=True),
        lax.psum_scatter(terms[3], ("dp", "seq"), scatter_dimension=1, tiled=True),
    )


def mixer_owners(terms):
    return (
        lax.psum_scatter(terms[0], ("dp", "seq"), scatter_dimension=0, tiled=True),
        lax.psum_scatter(terms[1], ("dp", "seq"), scatter_dimension=0, tiled=True),
        lax.psum_scatter(terms[2], ("dp", "seq"), scatter_dimension=0, tiled=True),
        lax.psum_scatter(terms[3], ("dp", "seq"), scatter_dimension=0, tiled=True),
        lax.psum_scatter(terms[4], ("dp", "seq"), scatter_dimension=0, tiled=True),
        lax.psum_scatter(terms[5], ("dp", "seq"), scatter_dimension=0, tiled=True),
        lax.psum_scatter(terms[6], ("dp", "seq"), scatter_dimension=1, tiled=True),
        lax.psum_scatter(terms[7], ("dp", "seq"), scatter_dimension=0, tiled=True),
        lax.psum_scatter(terms[8], ("dp", "seq"), scatter_dimension=0, tiled=True),
        lax.psum_scatter(terms[9], ("dp", "seq"), scatter_dimension=0, tiled=True),
    )


def local(
    tokens,
    prefix_len,
    norm1_gain,
    query_weight,
    key_weight,
    value_weight,
    gate_weight,
    decay_down,
    decay_up,
    decay_bias,
    group_gain,
    out_weight,
    norm2_gain,
    ffn_gate,
    ffn_up,
    ffn_down,
    out_grad,
):
    mixer_full = (
        lax.all_gather(norm1_gain, ("dp", "seq"), axis=0, tiled=True),
        lax.all_gather(query_weight, ("dp", "seq"), axis=0, tiled=True),
        lax.all_gather(key_weight, ("dp", "seq"), axis=0, tiled=True),
        lax.all_gather(value_weight, ("dp", "seq"), axis=0, tiled=True),
        lax.all_gather(gate_weight, ("dp", "seq"), axis=0, tiled=True),
        lax.all_gather(decay_down, ("dp", "seq"), axis=0, tiled=True),
        lax.all_gather(decay_up, ("dp", "seq"), axis=1, tiled=True),
        lax.all_gather(decay_bias, ("dp", "seq"), axis=0, tiled=True),
        lax.all_gather(group_gain, ("dp", "seq"), axis=0, tiled=True),
        lax.all_gather(out_weight, ("dp", "seq"), axis=0, tiled=True),
    )
    (
        gain_one,
        weight_q,
        weight_k,
        weight_v,
        weight_g,
        weight_down,
        weight_up,
        bias_full,
        gain_group,
        weight_o,
    ) = mixer_full
    seq_count, tok_count, feature_count = tokens.shape
    resid_in = tokens.astype(jnp.float32)
    scale_one = rms_scale(resid_in)
    unit_one = resid_in * scale_one
    normed = (unit_one * gain_one.astype(jnp.float32)).astype(jnp.bfloat16)
    queries = project(normed, weight_q).astype(jnp.bfloat16)
    key_matrix = project(normed, weight_k).astype(jnp.bfloat16)
    value_matrix = project(normed, weight_v).astype(jnp.bfloat16)
    gate_out = project(normed, weight_g)
    lowrank = project(normed, weight_down).astype(jnp.bfloat16)
    logits = project(lowrank, weight_up) + bias_full.astype(jnp.float32)
    decays = jax.nn.log_sigmoid(logits) / 16.0
    query_heads = queries.astype(jnp.float32).reshape(seq_count, tok_count, HEADS, HEAD_K)
    key_heads = key_matrix.astype(jnp.float32).reshape(seq_count, tok_count, HEADS, HEAD_K)
    value_heads = value_matrix.astype(jnp.float32).reshape(seq_count, tok_count, HEADS, HEAD_V)
    decay_heads = decays.reshape(seq_count, tok_count, HEADS, HEAD_K)
    seg_start = lax.axis_index("seq") * tok_count
    places = seg_start + jnp.arange(tok_count)
    in_prefix = (places[None, :] < prefix_len[:, None]).astype(jnp.float32)[:, :, None, None]
    end_local = prefix_len - 1 - seg_start
    is_owner = (end_local >= 0) & (end_local < tok_count)
    local_out, pull_states = jax.vjp(local_states, key_heads, value_heads, decay_heads)
    total_dev, state_dev, starts, cumulative_decay, running_totals = local_out
    incoming = chain_forward(total_dev, state_dev)
    outputs_of = partial(local_outputs, end_local=end_local, is_owner=is_owner)
    (causal, partial_state), pull_outputs = jax.vjp(
        outputs_of,
        query_heads,
        key_heads,
        value_heads,
        incoming,
        starts,
        cumulative_decay,
        running_totals,
    )
    prefix_carry_state = lax.psum(partial_state.astype(jnp.bfloat16), "seq").astype(jnp.float32)
    prefix_output = precise_summation("sthk,shkv->sthv", query_heads, prefix_carry_state)
    mixed_heads = in_prefix * prefix_output + (1.0 - in_prefix) * causal
    scale_group = rms_scale(mixed_heads)
    unit_group = mixed_heads * scale_group
    normed_group = unit_group * gain_group.astype(jnp.float32)
    swish_gate = jax.nn.silu(gate_out).reshape(seq_count, tok_count, HEADS, HEAD_V)
    gated_rows = (
        (normed_group * swish_gate).reshape(seq_count, tok_count, VALS).astype(jnp.bfloat16)
    )
    branch = project(gated_rows, weight_o)
    resid_mid = resid_in + branch
    ffn_full = (
        lax.all_gather(norm2_gain, ("dp", "seq"), axis=0, tiled=True),
        lax.all_gather(ffn_gate, ("dp", "seq"), axis=0, tiled=True),
        lax.all_gather(ffn_up, ("dp", "seq"), axis=0, tiled=True),
        lax.all_gather(ffn_down, ("dp", "seq"), axis=1, tiled=True),
    )
    gain_two, weight_gate, weight_upper, weight_lower = ffn_full
    scale_two = rms_scale(resid_mid)
    unit_two = resid_mid * scale_two
    normed_two = (unit_two * gain_two.astype(jnp.float32)).astype(jnp.bfloat16)
    gate_part = project(normed_two, weight_gate)
    up_part = project(normed_two, weight_upper)
    gate_act = jax.nn.silu(gate_part)
    hidden = (gate_act * up_part).astype(jnp.bfloat16)
    ffn_out = project(hidden, weight_lower)
    layer_out = (resid_mid + ffn_out).astype(jnp.bfloat16)
    ffn_back = (
        lax.all_gather(norm2_gain, ("dp", "seq"), axis=0, tiled=True),
        lax.all_gather(ffn_gate, ("dp", "seq"), axis=0, tiled=True),
        lax.all_gather(ffn_up, ("dp", "seq"), axis=0, tiled=True),
        lax.all_gather(ffn_down, ("dp", "seq"), axis=1, tiled=True),
    )
    back_gain_two, back_gate, back_upper, back_lower = ffn_back
    grad_out = out_grad.astype(jnp.float32)
    grad_hidden = back_project(out_grad, back_lower)
    lower_grad = weight_grad(hidden, out_grad)
    grad_gate = (grad_hidden * up_part * silu_slope(gate_part)).astype(jnp.bfloat16)
    grad_up = (grad_hidden * gate_act).astype(jnp.bfloat16)
    gate_w_grad = weight_grad(normed_two, grad_gate)
    up_w_grad = weight_grad(normed_two, grad_up)
    grad_normed_two = back_project(grad_gate, back_gate) + back_project(grad_up, back_upper)
    gain_two_grad = jnp.sum(grad_normed_two * unit_two, axis=(0, 1))
    grad_mid = grad_out + rms_back(
        grad_normed_two * back_gain_two.astype(jnp.float32), unit_two, scale_two
    )
    ffn_grads = ffn_owners((gain_two_grad, gate_w_grad, up_w_grad, lower_grad))
    mixer_back = (
        lax.all_gather(norm1_gain, ("dp", "seq"), axis=0, tiled=True),
        lax.all_gather(query_weight, ("dp", "seq"), axis=0, tiled=True),
        lax.all_gather(key_weight, ("dp", "seq"), axis=0, tiled=True),
        lax.all_gather(value_weight, ("dp", "seq"), axis=0, tiled=True),
        lax.all_gather(gate_weight, ("dp", "seq"), axis=0, tiled=True),
        lax.all_gather(decay_down, ("dp", "seq"), axis=0, tiled=True),
        lax.all_gather(decay_up, ("dp", "seq"), axis=1, tiled=True),
        lax.all_gather(decay_bias, ("dp", "seq"), axis=0, tiled=True),
        lax.all_gather(group_gain, ("dp", "seq"), axis=0, tiled=True),
        lax.all_gather(out_weight, ("dp", "seq"), axis=0, tiled=True),
    )
    (
        back_gain_one,
        back_q,
        back_k,
        back_v,
        back_g,
        back_down,
        back_up,
        unused_bias,
        back_group,
        back_o,
    ) = mixer_back
    grad_branch = grad_mid.astype(jnp.bfloat16)
    out_w_grad = weight_grad(gated_rows, grad_branch)
    grad_gated = back_project(grad_branch, back_o).reshape(seq_count, tok_count, HEADS, HEAD_V)
    grad_normed_group = grad_gated * swish_gate
    grad_swish = (grad_gated * normed_group).reshape(seq_count, tok_count, VALS)
    grad_gate_out = (grad_swish * silu_slope(gate_out)).astype(jnp.bfloat16)
    group_grad = jnp.sum(grad_normed_group * unit_group, axis=(0, 1, 2))
    grad_mixed = rms_back(
        grad_normed_group * back_group.astype(jnp.float32), unit_group, scale_group
    )
    grad_prefix = grad_mixed * in_prefix
    grad_causal = grad_mixed - grad_prefix
    grad_query_pre = precise_summation("sthv,shkv->sthk", grad_prefix, prefix_carry_state)
    prefix_term = precise_summation("sthk,sthv->shkv", query_heads, grad_prefix)
    grad_state = lax.psum(prefix_term.astype(jnp.bfloat16), "seq").astype(jnp.float32)
    grad_q_local, grad_k_local, grad_v_local, grad_in, grad_starts, grad_cum, grad_tot = (
        pull_outputs((grad_causal, grad_state))
    )
    grad_end = chain_backward(total_dev, grad_in)
    grad_total = jnp.sum(incoming * grad_end, axis=-1) * jnp.exp(total_dev)
    grad_k_chain, grad_v_chain, grad_decay = pull_states(
        (grad_total, grad_end, grad_starts, grad_cum, grad_tot)
    )
    grad_q = (
        (grad_query_pre + grad_q_local).reshape(seq_count, tok_count, KEYS).astype(jnp.bfloat16)
    )
    grad_k = (grad_k_local + grad_k_chain).reshape(seq_count, tok_count, KEYS).astype(jnp.bfloat16)
    grad_v = (grad_v_local + grad_v_chain).reshape(seq_count, tok_count, VALS).astype(jnp.bfloat16)
    grad_logits = (
        grad_decay.reshape(seq_count, tok_count, KEYS) * jax.nn.sigmoid(-logits) / 16.0
    ).astype(jnp.bfloat16)
    bias_grad = jnp.sum(grad_logits.astype(jnp.float32), axis=(0, 1))
    up_rank_grad = weight_grad(lowrank, grad_logits)
    grad_lowrank = back_project(grad_logits, back_up).astype(jnp.bfloat16)
    down_rank_grad = weight_grad(normed, grad_lowrank)
    grad_normed = (
        back_project(grad_q, back_q)
        + back_project(grad_k, back_k)
        + back_project(grad_v, back_v)
        + back_project(grad_gate_out, back_g)
        + back_project(grad_lowrank, back_down)
    )
    gain_one_grad = jnp.sum(grad_normed * unit_one, axis=(0, 1))
    tokens_grad = grad_mid + rms_back(
        grad_normed * back_gain_one.astype(jnp.float32), unit_one, scale_one
    )
    mixer_grads = mixer_owners(
        (
            gain_one_grad,
            weight_grad(normed, grad_q),
            weight_grad(normed, grad_k),
            weight_grad(normed, grad_v),
            weight_grad(normed, grad_gate_out),
            down_rank_grad,
            up_rank_grad,
            bias_grad,
            group_grad,
            out_w_grad,
        )
    )
    return (layer_out, tokens_grad) + tuple(mixer_grads) + tuple(ffn_grads)


def solution(mesh):
    return jax.shard_map(
        local,
        mesh=mesh,
        in_specs=(
            P("dp", "seq", None),
            P("dp"),
            P(("dp", "seq")),
            P(("dp", "seq"), None),
            P(("dp", "seq"), None),
            P(("dp", "seq"), None),
            P(("dp", "seq"), None),
            P(("dp", "seq"), None),
            P(None, ("dp", "seq")),
            P(("dp", "seq")),
            P(("dp", "seq")),
            P(("dp", "seq"), None),
            P(("dp", "seq")),
            P(("dp", "seq"), None),
            P(("dp", "seq"), None),
            P(None, ("dp", "seq")),
            P("dp", "seq", None),
        ),
        out_specs=(
            P("dp", "seq", None),
            P("dp", "seq", None),
            P(("dp", "seq")),
            P(("dp", "seq"), None),
            P(("dp", "seq"), None),
            P(("dp", "seq"), None),
            P(("dp", "seq"), None),
            P(("dp", "seq"), None),
            P(None, ("dp", "seq")),
            P(("dp", "seq")),
            P(("dp", "seq")),
            P(("dp", "seq"), None),
            P(("dp", "seq")),
            P(("dp", "seq"), None),
            P(("dp", "seq"), None),
            P(None, ("dp", "seq")),
        ),
        check_vma=False,
    )
```

profile of v0, /device:TPU:0, one launch (start us, length us, event | category | flops | bytes accessed | tf_op | source)
XLA Modules:
  0.0 2792.0 jit_solution(4527334862062246042)
XLA Ops:
  12.9 42.1 %all-reduce.18 = (bf16[1024]{0:T(1024)(128)(2,1)S(1)}, bf16[512]{0:T(512)(128)(2,1)S(1)}, bf16[256]{0:T(256)(128)(2,1)S(1)}, bf16[1024]{0:T(1024)(128)(2,1)S(1)}) all-reduce(bf16[1024]{0:T(1024)(128)(2,1)S(1)} %dynamic-update-slice, bf16[512]{0:T(512)(128)(2,1)S(1)} %dynamic-update-slice.1, ...), channel_id=1, replica_groups=mesh['dp'=8,'seq'=4] {'dp','seq'}, use_global_device_ids=true, to_apply=%add.9 | all-reduce | flops 2816 | bytes 11264
  57.1 67.1 %all-gather.3 = bf16[32,32,16]{1,2,0:T(8,128)(2,1)S(1)} all-gather(bf16[1,32,16]{1,2,0:T(8,128)(2,1)S(1)} %bitcast.465), channel_id=1, replica_groups=mesh['dp'=8,'seq'=4] {'dp','seq'}, dimensions={0}, use_global_device_ids=true | all-gather | bytes 33792 | tf_op jit(solution)/shard_map/all_gather | solution.py:230
  124.5 64.8 %all_gather.78 = bf16[16,512]{0,1:T(8,128)(2,1)S(1)} all-gather(bf16[16,16]{0,1:T(8,128)(2,1)S(1)} %copy.175), channel_id=1, replica_groups=mesh['dp'=8,'seq'=4] {'dp','seq'}, dimensions={1}, use_global_device_ids=true | all-gather | bytes 16896 | tf_op jit(solution)/shard_map/all_gather | solution.py:231
  229.1 13.4 all-gather
  257.6 118.9 %all-gather.19.cloned.1.call-done = f32[4,4,4,128,256]{4,3,2,1,0:T(8,128)} async-done(((f32[1,4,4,128,256]{4,3,2,1,0:T(8,128)}), f32[4,4,4,128,256]{4,3,2,1,0:T(8,128)}) %all-gather.19.cloned.1.call-update) | async-done | bytes 8388624 | tf_op jit(solution)/shard_map/all_gather | solution.py:21
  394.5 39.4 %all-gather.23.cloned.1.call-done = bf16[1024,1024]{1,0:T(8,128)(2,1)} async-done(((bf16[32,1024]{1,0:T(8,128)(2,1)}), bf16[1024,1024]{1,0:T(8,128)(2,1)}) %all-gather.23.cloned.1.call-update) | async-done | bytes 2097168 | tf_op jit(solution)/shard_map/all_gather | solution.py:229
  452.7 50.2 %all-gather.31.cloned.1.call-done = bf16[2816,1024]{0,1:T(8,128)(2,1)} async-done(((bf16[2816,32]{0,1:T(8,128)(2,1)}), bf16[2816,1024]{0,1:T(8,128)(2,1)}) %all-gather.31.cloned.1.call-update) | async-done | bytes 5767184 | tf_op jit(solution)/shard_map/all_gather | solution.py:299
  502.8 12.1 fusion.17
  532.1 23.9 all-reduce.22.cloned.1.call-done
  564.1 51.1 %all-gather.25.cloned.1.call-done = bf16[1024,1024]{1,0:T(8,128)(2,1)} async-done(((bf16[32,1024]{1,0:T(8,128)(2,1)}), bf16[1024,1024]{1,0:T(8,128)(2,1)}) %all-gather.25.cloned.1.call-update) | async-done | bytes 2097168 | tf_op jit(solution)/shard_map/all_gather | solution.py:234
  624.5 60.2 %all-gather.29.cloned.1.call-done = bf16[1024,2816]{1,0:T(8,128)(2,1)} async-done(((bf16[32,2816]{1,0:T(8,128)(2,1)}), bf16[1024,2816]{1,0:T(8,128)(2,1)}) %all-gather.29.cloned.1.call-update) | async-done | bytes 5767184 | tf_op jit(solution)/shard_map/all_gather | solution.py:298
  684.7 11.8 fusion.23
  696.5 57.6 %all-gather.27.cloned.1.call-done = bf16[1024,2816]{1,0:T(8,128)(2,1)} async-done(((bf16[32,2816]{1,0:T(8,128)(2,1)}), bf16[1024,2816]{1,0:T(8,128)(2,1)}) %all-gather.27.cloned.1.call-update) | async-done | bytes 5767184 | tf_op jit(solution)/shard_map/all_gather | solution.py:297
  754.1 21.9 multiply_convert_fusion.1
  831.9 17.5 multiply_reduce_fusion
  849.4 27.9 %all-reduce.24.cloned.1.call-done = bf16[4,4,128,256]{3,2,1,0:T(8,128)(2,1)} async-done(((bf16[4,4,128,256]{3,2,1,0:T(8,128)(2,1)}), bf16[4,4,128,256]{3,2,1,0:T(8,128)(2,1)}) %all-reduce.24.cloned.1.call-update) | async-done | bytes 1048592 | tf_op jit(solution)/shard_map/psum | solution.py:369
  880.7 13.6 all-gather.2
  918.8 42.1 %all-gather.33.cloned.1.call-done = bf16[16,4,128,256]{3,2,1,0:T(8,128)(2,1)} async-done(((bf16[4,4,128,256]{3,2,1,0:T(8,128)(2,1)}), bf16[16,4,128,256]{3,2,1,0:T(8,128)(2,1)}) %all-gather.33.cloned.1.call-update) | async-done | bytes 4194320 | tf_op jit(solution)/shard_map/all_gather | solution.py:37
  986.3 13.4 fusion.147
  1135.3 11.5 convolution_bitcast_fusion.2
  1147.0 11.6 convolution_bitcast_fusion.1
  1160.2 11.7 convolution_bitcast_fusion
  1198.7 38.1 %all-reduce.17 = (f32[1024]{0:T(1024)S(1)}, f32[512]{0:T(512)S(1)}, f32[256]{0:T(256)S(1)}, f32[1024]{0:T(1024)S(1)}) all-reduce(f32[1024]{0:T(1024)S(1)} %get-tuple-element.153, f32[512]{0:T(512)S(1)} %get-tuple-element.187, f32[256]{0:T(256)S(1)} %copy-done.81, ...), channel_id=5, replica_groups=mesh['dp'=8,'seq'=4] {'dp','seq'}, use_global_device_ids=true, to_apply=%region_27.28.clone | all-reduce | flops 2816 | bytes 22528
  1245.9 60.9 %reduce-scatter.31.cloned.1.call-done = f32[32,16]{1,0:T(8,128)} async-done(((f32[1024,16]{1,0:T(8,128)}), f32[32,16]{1,0:T(8,128)}) %reduce-scatter.31.cloned.1.call-update) | async-done | bytes 2064
  1308.1 145.5 %reduce-scatter.23.cloned.1.call-done = f32[32,1024]{1,0:T(8,128)} async-done(((f32[1024,1024]{1,0:T(8,128)}), f32[32,1024]{1,0:T(8,128)}) %reduce-scatter.23.cloned.1.call-update) | async-done | bytes 131088 | tf_op jit(solution)/shard_map/reduce_scatter | solution.py:201
  1453.6 149.3 %reduce-scatter.21.cloned.1.call-done = f32[32,1024]{1,0:T(8,128)} async-done(((f32[1024,1024]{1,0:T(8,128)}), f32[32,1024]{1,0:T(8,128)}) %reduce-scatter.21.cloned.1.call-update) | async-done | bytes 131088 | tf_op jit(solution)/shard_map/reduce_scatter | solution.py:196
  1602.9 139.0 %reduce-scatter.15.cloned.1.call-done = f32[32,512]{1,0:T(8,128)} async-done(((f32[1024,512]{1,0:T(8,128)}), f32[32,512]{1,0:T(8,128)}) %reduce-scatter.15.cloned.1.call-update) | async-done | bytes 65552 | tf_op jit(solution)/shard_map/reduce_scatter | solution.py:193
  1742.0 139.3 %reduce-scatter.17.cloned.1.call-done = f32[32,512]{1,0:T(8,128)} async-done(((f32[1024,512]{1,0:T(8,128)}), f32[32,512]{1,0:T(8,128)}) %reduce-scatter.17.cloned.1.call-update) | async-done | bytes 65552 | tf_op jit(solution)/shard_map/reduce_scatter | solution.py:194
  1881.3 148.4 %reduce-scatter.19.cloned.1.call-done = f32[32,1024]{1,0:T(8,128)} async-done(((f32[1024,1024]{1,0:T(8,128)}), f32[32,1024]{1,0:T(8,128)}) %reduce-scatter.19.cloned.1.call-update) | async-done | bytes 131088 | tf_op jit(solution)/shard_map/reduce_scatter | solution.py:195
  2029.7 252.5 %reduce-scatter.25.cloned.1.call-done = f32[32,2816]{1,0:T(8,128)} async-done(((f32[1024,2816]{1,0:T(8,128)}), f32[32,2816]{1,0:T(8,128)}) %reduce-scatter.25.cloned.1.call-update) | async-done | bytes 360464 | tf_op jit(solution)/shard_map/reduce_scatter | solution.py:184
  2282.2 251.4 %reduce-scatter.27.cloned.1.call-done = f32[32,2816]{1,0:T(8,128)} async-done(((f32[1024,2816]{1,0:T(8,128)}), f32[32,2816]{1,0:T(8,128)}) %reduce-scatter.27.cloned.1.call-update) | async-done | bytes 360464 | tf_op jit(solution)/shard_map/reduce_scatter | solution.py:185
  2533.6 251.3 %reduce-scatter.29.cloned.1.call-done = f32[2816,32]{0,1:T(8,128)} async-done(((f32[2816,1024]{0,1:T(8,128)}), f32[2816,32]{0,1:T(8,128)}) %reduce-scatter.29.cloned.1.call-update) | async-done | bytes 360464 | tf_op jit(solution)/shard_map/reduce_scatter | solution.py:186
  (371 shorter events, 427.6 us)
Async XLA Ops:
  7.2 182.1 %copy-start.17 = (bf16[4,256,1024]{2,1,0:T(8,128)(2,1)S(1)}, bf16[4,256,1024]{2,1,0:T(8,128)(2,1)}, u32[]{:S(2)}) copy-start(bf16[4,256,1024]{2,1,0:T(8,128)(2,1)} %param.21) | copy-start | bytes 6291460
  7.2 190.2 %all-gather.15.cloned.1.call-start = ((), (), s32[]{:S(2)}) async-start(), calls=%async_computation.10 | async-start | bytes 1081344 | tf_op jit(solution)/shard_map/all_gather | solution.py:227
  7.9 197.4 %all-gather.17.cloned.1.call-start = ((), (), s32[]{:S(2)}) async-start(), calls=%async_computation.11 | async-start | bytes 2162688 | tf_op jit(solution)/shard_map/all_gather | solution.py:228
  8.7 237.5 %all-gather.21.cloned.1.call-start = ((), (), s32[]{:S(2)}) async-start(), calls=%async_computation.14 | async-start | bytes 1081344 | tf_op jit(solution)/shard_map/all_gather | solution.py:226
  9.4 367.0 %all-gather.19.cloned.1.call-start = ((), (), s32[]{:S(2)}) async-start(), calls=%async_computation.12 | async-start | bytes 10485760 | tf_op jit(solution)/shard_map/all_gather | solution.py:21
  55.0 378.9 %copy-start.69 = (f32[1024]{0:T(1024)}, f32[1024]{0:T(1024)S(1)}, u32[]{:S(2)}) copy-start(f32[1024]{0:T(1024)S(1)} %convert_element_type.173) | copy-start | bytes 12292
  57.1 376.8 %copy-start.71 = (f32[4,256]{1,0:T(4,128)}, f32[4,256]{1,0:T(4,128)S(1)}, u32[]{:S(2)}) copy-start(f32[4,256]{1,0:T(4,128)S(1)} %add_rsqrt_fusion.2) | copy-start | bytes 12292
  197.3 187.8 %copy-start.32 = (f32[4,4,1,4,128]{4,2,3,1,0:T(1,128)}, f32[4,4,1,4,128]{4,2,3,1,0:T(1,128)S(1)}, u32[]{:S(2)}) copy-start(f32[4,4,1,4,128]{4,2,3,1,0:T(1,128)S(1)} %slice.36) | copy-start | bytes 98308
  197.3 250.3 %copy-start.53 = (f32[4,4,128]{2,1,0:T(4,128)}, f32[4,4,128]{2,1,0:T(4,128)S(1)}, u32[]{:S(2)}) copy-start(f32[4,4,128]{2,1,0:T(4,128)S(1)} %get-tuple-element.220) | copy-start | bytes 24580
  197.3 250.3 %copy-start.59 = (f32[4,4,128]{2,1,0:T(4,128)}, f32[4,4,128]{2,1,0:T(4,128)S(1)}, u32[]{:S(2)}) copy-start(f32[4,4,128]{2,1,0:T(4,128)S(1)} %get-tuple-element.219) | copy-start | bytes 24580
  197.4 250.3 %copy-start.61 = (f32[4,4,128]{2,1,0:T(4,128)}, f32[4,4,128]{2,1,0:T(4,128)S(1)}, u32[]{:S(2)}) copy-start(f32[4,4,128]{2,1,0:T(4,128)S(1)} %get-tuple-element.221) | copy-start | bytes 24580
  227.8 206.1 %all-gather.23.cloned.1.call-start = ((), (), s32[]{:S(2)}) async-start(), calls=%async_computation.15 | async-start | bytes 2162688 | tf_op jit(solution)/shard_map/all_gather | solution.py:229
  228.4 274.4 %all-gather.31.cloned.1.call-start = ((), (), s32[]{:S(2)}) async-start(), calls=%async_computation.19 | async-start | bytes 5947392 | tf_op jit(solution)/shard_map/all_gather | solution.py:299
  229.0 327.0 %all-reduce.22.cloned.1.call-start = ((), (), s32[]{:S(2)}) async-start(), calls=%async_computation.13 | async-start | bytes 2097152 | tf_op jit(solution)/shard_map/psum | solution.py:283
  243.2 133.5 %copy-start.67 = (f32[4,256]{1,0:T(4,128)}, f32[4,256]{1,0:T(4,128)S(1)}, u32[]{:S(2)}) copy-start(f32[4,256]{1,0:T(4,128)S(1)} %get-tuple-element.226) | copy-start | bytes 12292
  243.2 133.5 %copy-start.75 = (pred[4,256]{1,0:T(4,128)(4,1)}, pred[4,256]{1,0:T(4,128)(4,1)S(1)}, u32[]{:S(2)}) copy-start(pred[4,256]{1,0:T(4,128)(4,1)S(1)} %get-tuple-element.227) | copy-start | bytes 3076
  257.5 119.2 %copy-start.51 = (f32[4,1,4,128]{3,1,2,0:T(1,128)}, f32[4,1,4,128]{3,1,2,0:T(1,128)S(1)}, u32[]{:S(2)}) copy-start(f32[4,1,4,128]{3,1,2,0:T(1,128)S(1)} %fusion.183) | copy-start | bytes 24580
  382.3 232.9 %all-gather.25.cloned.1.call-start = ((), (), s32[]{:S(2)}) async-start(), calls=%async_computation.16 | async-start | bytes 2162688 | tf_op jit(solution)/shard_map/all_gather | solution.py:234
  383.0 301.6 %all-gather.29.cloned.1.call-start = ((), (), s32[]{:S(2)}) async-start(), calls=%async_computation.18 | async-start | bytes 5947392 | tf_op jit(solution)/shard_map/all_gather | solution.py:298
  383.8 370.3 %all-gather.27.cloned.1.call-start = ((), (), s32[]{:S(2)}) async-start(), calls=%async_computation.17 | async-start | bytes 5947392 | tf_op jit(solution)/shard_map/all_gather | solution.py:297
  384.4 492.9 %all-reduce.24.cloned.1.call-start = ((), (), s32[]{:S(2)}) async-start(), calls=%async_computation.20 | async-start | bytes 2097152 | tf_op jit(solution)/shard_map/psum | solution.py:369
  826.4 134.5 %all-gather.33.cloned.1.call-start = ((), (), s32[]{:S(2)}) async-start(), calls=%async_computation.29 | async-start | bytes 5242880 | tf_op jit(solution)/shard_map/all_gather | solution.py:37
  880.6 363.9 %reduce-scatter.33.cloned.1.call-start = ((), (), s32[]{:S(2)}) async-start(), calls=%async_computation.31 | async-start | bytes 270336
  1041.8 264.9 %reduce-scatter.31.cloned.1.call-start = ((), (), s32[]{:S(2)}) async-start(), calls=%async_computation.30 | async-start | bytes 540672
  1045.5 408.2 %reduce-scatter.23.cloned.1.call-start = ((), (), s32[]{:S(2)}) async-start(), calls=%async_computation.25 | async-start | bytes 4325376 | tf_op jit(solution)/shard_map/reduce_scatter | solution.py:201
  1052.7 550.2 %reduce-scatter.21.cloned.1.call-start = ((), (), s32[]{:S(2)}) async-start(), calls=%async_computation.24 | async-start | bytes 4325376 | tf_op jit(solution)/shard_map/reduce_scatter | solution.py:196
  1069.2 672.8 %reduce-scatter.15.cloned.1.call-start = ((), (), s32[]{:S(2)}) async-start(), calls=%async_computation.21 | async-start | bytes 2162688 | tf_op jit(solution)/shard_map/reduce_scatter | solution.py:193
  1084.9 796.4 %reduce-scatter.17.cloned.1.call-start = ((), (), s32[]{:S(2)}) async-start(), calls=%async_computation.22 | async-start | bytes 2162688 | tf_op jit(solution)/shard_map/reduce_scatter | solution.py:194
  1089.7 940.0 %reduce-scatter.19.cloned.1.call-start = ((), (), s32[]{:S(2)}) async-start(), calls=%async_computation.23 | async-start | bytes 4325376 | tf_op jit(solution)/shard_map/reduce_scatter | solution.py:195
  1133.8 1148.5 %reduce-scatter.25.cloned.1.call-start = ((), (), s32[]{:S(2)}) async-start(), calls=%async_computation.26 | async-start | bytes 11894784 | tf_op jit(solution)/shard_map/reduce_scatter | solution.py:184
  1146.9 1386.7 %reduce-scatter.27.cloned.1.call-start = ((), (), s32[]{:S(2)}) async-start(), calls=%async_computation.27 | async-start | bytes 11894784 | tf_op jit(solution)/shard_map/reduce_scatter | solution.py:185
  1158.6 1626.3 %reduce-scatter.29.cloned.1.call-start = ((), (), s32[]{:S(2)}) async-start(), calls=%async_computation.28 | async-start | bytes 11894784 | tf_op jit(solution)/shard_map/reduce_scatter | solution.py:186
  (80 other events, 982.7 us)
Sparse Core Ops, SparseCore 0:
  11.0 56.5 all-gather.14
  70.5 55.5 all-gather.16
  129.1 52.7 all-gather.20
  227.9 148.4 all-gather.18
  379.2 54.6 all-gather.22
  436.6 66.1 all-gather.30
  505.2 50.7 all-reduce.21
  559.3 55.8 all-gather.24
  618.5 66.1 all-gather.28
  687.7 66.2 all-gather.26
  826.5 50.7 all-reduce.23
  880.7 80.1 all-gather.32
  1042.0 131.9 reduce-scatter.32
  1176.2 130.5 reduce-scatter.30
  1309.4 144.1 reduce-scatter.22
  1456.3 146.5 reduce-scatter.20
  1605.6 136.3 reduce-scatter.14
  1744.8 136.5 reduce-scatter.16
  1884.2 145.4 reduce-scatter.18
  2032.5 249.7 reduce-scatter.24
  2285.1 248.4 reduce-scatter.26
  2536.5 248.4 reduce-scatter.28
where the time goes:
time: 2800 us; the launch traced here: 2790 us
  waiting for transfers between devices  2010 us (72%)
  matrix products  327 us (12%)
  blocking collectives  239 us (9%)
  local copies, waits for them, and re-layouts  114 us (4%)
  other arithmetic  80.8 us (3%)
    reduce_scatter x1, waiting for transfers between devices, ffn_owners(): lax.psum_scatter(terms[1], ('dp', 'seq'), scatter_dimension=0, tiled=True)  253 us
    reduce_scatter x1, waiting for transfers between devices, ffn_owners(): lax.psum_scatter(terms[2], ('dp', 'seq'), scatter_dimension=0, tiled=True)  251 us
    reduce_scatter x1, waiting for transfers between devices, ffn_owners(): lax.psum_scatter(terms[3], ('dp', 'seq'), scatter_dimension=1, tiled=True)  251 us
    reduce_scatter x1, waiting for transfers between devices, mixer_owners(): lax.psum_scatter(terms[4], ('dp', 'seq'), scatter_dimension=0, tiled=True)  149 us
    reduce_scatter x1, waiting for transfers between devices, mixer_owners(): lax.psum_scatter(terms[3], ('dp', 'seq'), scatter_dimension=0, tiled=True)  148 us
    reduce_scatter x1, waiting for transfers between devices, mixer_owners(): lax.psum_scatter(terms[9], ('dp', 'seq'), scatter_dimension=0, tiled=True)  146 us
    reduce_scatter x1, waiting for transfers between devices, mixer_owners(): lax.psum_scatter(terms[2], ('dp', 'seq'), scatter_dimension=0, tiled=True)  139 us
    reduce_scatter x1, waiting for transfers between devices, mixer_owners(): lax.psum_scatter(terms[1], ('dp', 'seq'), scatter_dimension=0, tiled=True)  139 us
  transfers between devices with their start and end apart: 22, of which 18 were waited for; matrix products, arithmetic and copies ran while one was open for 12% of the time, Pallas kernels for 0%

commit v1 on v0

v1 whole, which is shorter than its diff:
```python
from functools import partial

import jax
import jax.numpy as jnp
import numpy as np
from jax import lax
from jax.sharding import Mesh
from jax.sharding import PartitionSpec as P

KEYS = 512
VALS = 1024
HEADS = 4
SPAN = 64
HEAD_K = 128
HEAD_V = 256
FF = 2816


norm_eps = 1e-05


def entering(part, axis, combine, identity):
    place = lax.axis_index(axis)
    gathered = jax.tree.map(lambda a: lax.all_gather(a, axis), part)
    state = jax.tree.map(lambda a, e: jnp.zeros_like(a) + jnp.asarray(e, a.dtype), part, identity)

    def entering_one(lap, state):
        return combine(
            state, jax.tree.map(lambda a: lax.dynamic_index_in_dim(a, lap, 0, False), gathered)
        )

    return lax.fori_loop(0, place, entering_one, state)


def carried_in(x, axis, join, neutral):
    count = lax.axis_size(axis)
    place = lax.axis_index(axis)
    ahead = count - 1 - place
    gathered = jax.tree.map(
        lambda a, kind: lax.all_gather(a.astype(kind), axis),
        x,
        jax.tree.map(lambda a: jnp.bfloat16 if a.dtype == jnp.float32 else a.dtype, x),
    )
    state = jax.tree.map(lambda a, e: jnp.zeros_like(a) + jnp.asarray(e, a.dtype), x, neutral)

    def carried_one(lap, state):
        source = count - 1 - lap
        return join(
            state,
            jax.tree.map(
                lambda a, own: lax.dynamic_index_in_dim(a, source, 0, False).astype(own.dtype),
                gathered,
                x,
            ),
        )

    return lax.fori_loop(0, ahead, carried_one, state)


def precise_summation(pattern, *operands):
    return jnp.einsum(
        pattern, *operands, precision=lax.Precision.HIGHEST, preferred_element_type=jnp.float32
    )


def project(inputs, weight):
    return jnp.einsum("std,de->ste", inputs, weight, preferred_element_type=jnp.float32)


def back_project(gradient, weight):
    return jnp.einsum("ste,de->std", gradient, weight, preferred_element_type=jnp.float32)


def weight_grad(inputs, gradient):
    return jnp.einsum("std,ste->de", inputs, gradient, preferred_element_type=jnp.float32)


def rms_scale(values):
    return lax.rsqrt(jnp.mean(values * values, axis=-1, keepdims=True) + norm_eps)


def rms_back(grad_unit, unit_rows, scale_rows):
    return scale_rows * (
        grad_unit - unit_rows * jnp.mean(grad_unit * unit_rows, axis=-1, keepdims=True)
    )


def silu_slope(values):
    logistic = jax.nn.sigmoid(values)
    return logistic * (1.0 + values * (1.0 - logistic))


def chain_combine(earlier, later):
    return (earlier[0] + later[0], jnp.exp(later[0])[..., None] * earlier[1] + later[1])


def lower_ones(extent):
    indices = jnp.arange(extent)
    return (indices[:, None] >= indices[None, :]).astype(jnp.float32)


def local_states(key_matrix, valued, decays):
    seq_count, tok_count, head_count, key_width = key_matrix.shape
    blocks = tok_count // SPAN
    key_blocks = key_matrix.reshape(seq_count, blocks, SPAN, head_count, key_width)
    value_blocks = valued.reshape(seq_count, blocks, SPAN, head_count, valued.shape[-1])
    decay_blocks = decays.reshape(seq_count, blocks, SPAN, head_count, key_width)
    cumulative_decay = precise_summation("ij,snjhk->snihk", lower_ones(SPAN), decay_blocks)
    running_totals = cumulative_decay[:, :, -1]
    shares = precise_summation(
        "snjhk,snjhv->snhkv",
        key_blocks * jnp.exp(running_totals[:, :, None] - cumulative_decay),
        value_blocks,
    )
    carried_state = jnp.zeros_like(shares[:, 0])
    starts = []
    for number in range(blocks):
        starts.append(carried_state)
        carried_state = (
            jnp.exp(running_totals[:, number])[..., None] * carried_state + shares[:, number]
        )
    return (
        jnp.sum(running_totals, axis=1),
        carried_state,
        jnp.stack(starts, axis=1),
        cumulative_decay,
        running_totals,
    )


def local_outputs(
    queries,
    key_matrix,
    valued,
    incoming,
    starts,
    cumulative_decay,
    running_totals,
    end_local=None,
    is_owner=None,
):
    seq_count, tok_count, head_count, key_width = queries.shape
    val_width = valued.shape[-1]
    blocks = tok_count // SPAN
    query_blocks = queries.reshape(seq_count, blocks, SPAN, head_count, key_width)
    key_blocks = key_matrix.reshape(seq_count, blocks, SPAN, head_count, key_width)
    value_blocks = valued.reshape(seq_count, blocks, SPAN, head_count, val_width)
    before = jnp.cumsum(running_totals, axis=1) - running_totals
    block_states = jnp.exp(before)[..., None] * incoming[:, None] + starts
    query_input = query_blocks * jnp.exp(cumulative_decay)
    key_in = key_blocks * jnp.exp(-cumulative_decay)
    attention_scores = precise_summation("snihk,snjhk->snhij", query_input, key_in) * lower_ones(
        SPAN
    )
    causal = precise_summation(
        "snhij,snjhv->snihv", attention_scores, value_blocks
    ) + precise_summation("snihk,snhkv->snihv", query_input, block_states)
    causal = causal.reshape(seq_count, tok_count, head_count, val_width)
    position_cum = (cumulative_decay + before[:, :, None]).reshape(
        seq_count, tok_count, head_count, key_width
    )
    places = jnp.arange(tok_count)
    select = (places[None, :] == end_local[:, None]).astype(jnp.float32)
    end_cum = precise_summation("st,sthk->shk", select, position_cum)
    keep_mask = (places[None, :] <= end_local[:, None]) & is_owner[:, None]
    exponent = jnp.where(keep_mask[:, :, None, None], end_cum[:, None] - position_cum, 0.0)
    weight_bundle = jnp.exp(exponent) * keep_mask.astype(jnp.float32)[:, :, None, None]
    partial_state = precise_summation("sthk,sthv->shkv", key_matrix * weight_bundle, valued)
    owner_weight = is_owner.astype(jnp.float32)[:, None, None, None]
    partial_state = partial_state + owner_weight * jnp.exp(end_cum)[..., None] * incoming
    return (causal, partial_state)


def chain_forward(total_dev, state_dev, seq):
    identity = (jnp.zeros_like(total_dev), jnp.zeros_like(state_dev))
    return entering((total_dev, state_dev), seq, chain_combine, identity)[1]


def chain_backward(total_dev, grad_in, seq):
    identity = (jnp.zeros_like(total_dev), jnp.zeros_like(grad_in))
    return carried_in((total_dev, grad_in), seq, chain_combine, identity)[1]


EXTRA = 128


def physical_axes(mesh):
    shape = mesh.devices.shape
    names = []
    sizes = []
    for axis, extent in enumerate(shape):
        line = np.moveaxis(mesh.devices, axis, 0).reshape(extent, -1)[:, 0]
        places = [tuple(d.coords) + (d.core_on_chip,) for d in line]
        parts = []
        for dim, label in enumerate(("x", "y", "z", "core")):
            values = [p[dim] for p in places]
            if len(set(values)) > 1:
                step = next(i for i in range(extent) if values[i] != values[0])
                parts.append((step, label, len(set(values))))
        for step, label, size in sorted(parts, reverse=True):
            names.append(label)
            sizes.append(size)
    return tuple(names), tuple(sizes)


def pack_mixer(norm1_gain, norm2_gain, query, key, value, gate, down, up, bias, group, out):
    rows = query.shape[0]
    small = jnp.zeros((rows, EXTRA), query.dtype)
    small = small.at[:, :16].set(down)
    small = small.at[:, 16].set(norm1_gain)
    small = small.at[:, 17].set(norm2_gain)
    small = small.at[: bias.shape[0], 18].set(bias)
    small = small.at[: group.shape[0], 19].set(group)
    small = small.at[:, 24:32].set(up.T.reshape(rows, 8))
    return jnp.concatenate([query, key, value, gate, out, small], axis=1)


def unpack_small(small, devices):
    rows = small.shape[0] // devices
    by_device = small.reshape(devices, rows, EXTRA)
    down = small[:, :16]
    gain_one = small[:, 16]
    gain_two = small[:, 17]
    bias = by_device[:, : KEYS // devices, 18].reshape(KEYS)
    group = by_device[:, : HEAD_V // devices, 19].reshape(HEAD_V)
    up = small[:, 24:32].reshape(KEYS, 16).T
    return down, gain_one, gain_two, bias, group, up


def pack_small_grads(down, gain_one, gain_two, bias, group, up, devices):
    rows = gain_one.shape[0] // devices

    def column(vector):
        parts = vector.reshape(devices, -1)
        parts = jnp.pad(parts, ((0, 0), (0, rows - parts.shape[1])))
        return parts.reshape(devices * rows, 1)

    pieces = [
        down,
        gain_one[:, None],
        gain_two[:, None],
        column(bias),
        column(group),
        jnp.zeros((rows * devices, 4), jnp.float32),
        up.T.reshape(rows * devices, 8),
        jnp.zeros((rows * devices, EXTRA - 32), jnp.float32),
    ]
    return jnp.concatenate(pieces, axis=1)


def reduce_to_owner(total, names, sizes):
    rows = total.shape[0]
    width = total.shape[1]
    devices = int(np.prod(sizes))
    if "core" in names:
        at = names.index("core")
        before = int(np.prod(sizes[:at], initial=1))
        after = rows // before // sizes[at]
        shaped = total.reshape(before, sizes[at], after, width)
        core = lax.axis_index("core")
        kept = lax.dynamic_index_in_dim(shaped, core, 1, False)
        given = lax.dynamic_index_in_dim(shaped, 1 - core, 1, False)
        taken = lax.ppermute(given, "core", [(0, 1), (1, 0)])
        total = (kept + taken).reshape(rows // sizes[at], width)
    rest = tuple(n for n in names if n != "core")
    return lax.psum_scatter(total, rest, scatter_dimension=0, tiled=True)


def local(
    names,
    sizes,
    seq,
    tokens,
    prefix_len,
    norm1_gain,
    query_weight,
    key_weight,
    value_weight,
    gate_weight,
    decay_down,
    decay_up,
    decay_bias,
    group_gain,
    out_weight,
    norm2_gain,
    ffn_gate,
    ffn_up,
    ffn_down,
    out_grad,
):
    devices = int(np.prod(sizes))
    mixer_full = lax.all_gather(
        pack_mixer(
            norm1_gain,
            norm2_gain,
            query_weight,
            key_weight,
            value_weight,
            gate_weight,
            decay_down,
            decay_up,
            decay_bias,
            group_gain,
            out_weight,
        ),
        names,
        axis=0,
        tiled=True,
    )
    ffn_full = lax.all_gather(
        jnp.concatenate([ffn_gate, ffn_up, ffn_down.T], axis=1), names, axis=0, tiled=True
    )
    weight_q = mixer_full[:, :512]
    weight_k = mixer_full[:, 512:1024]
    weight_v = mixer_full[:, 1024:2048]
    weight_g = mixer_full[:, 2048:3072]
    weight_o = mixer_full[:, 3072:4096]
    weight_down, gain_one, gain_two, bias_full, gain_group, weight_up = unpack_small(
        mixer_full[:, 4096:], devices
    )
    weight_gate = ffn_full[:, :FF]
    weight_upper = ffn_full[:, FF : 2 * FF]
    weight_lower = ffn_full[:, 2 * FF :].T
    seq_count, tok_count, feature_count = tokens.shape
    resid_in = tokens.astype(jnp.float32)
    scale_one = rms_scale(resid_in)
    unit_one = resid_in * scale_one
    normed = (unit_one * gain_one.astype(jnp.float32)).astype(jnp.bfloat16)
    queries = project(normed, weight_q).astype(jnp.bfloat16)
    key_matrix = project(normed, weight_k).astype(jnp.bfloat16)
    value_matrix = project(normed, weight_v).astype(jnp.bfloat16)
    gate_out = project(normed, weight_g)
    lowrank = project(normed, weight_down).astype(jnp.bfloat16)
    logits = project(lowrank, weight_up) + bias_full.astype(jnp.float32)
    decays = jax.nn.log_sigmoid(logits) / 16.0
    query_heads = queries.astype(jnp.float32).reshape(seq_count, tok_count, HEADS, HEAD_K)
    key_heads = key_matrix.astype(jnp.float32).reshape(seq_count, tok_count, HEADS, HEAD_K)
    value_heads = value_matrix.astype(jnp.float32).reshape(seq_count, tok_count, HEADS, HEAD_V)
    decay_heads = decays.reshape(seq_count, tok_count, HEADS, HEAD_K)
    seg_start = lax.axis_index(seq) * tok_count
    places = seg_start + jnp.arange(tok_count)
    in_prefix = (places[None, :] < prefix_len[:, None]).astype(jnp.float32)[:, :, None, None]
    end_local = prefix_len - 1 - seg_start
    is_owner = (end_local >= 0) & (end_local < tok_count)
    local_out, pull_states = jax.vjp(local_states, key_heads, value_heads, decay_heads)
    total_dev, state_dev, starts, cumulative_decay, running_totals = local_out
    incoming = chain_forward(total_dev, state_dev, seq)
    outputs_of = partial(local_outputs, end_local=end_local, is_owner=is_owner)
    (causal, partial_state), pull_outputs = jax.vjp(
        outputs_of,
        query_heads,
        key_heads,
        value_heads,
        incoming,
        starts,
        cumulative_decay,
        running_totals,
    )
    prefix_carry_state = lax.psum(partial_state.astype(jnp.bfloat16), seq).astype(jnp.float32)
    prefix_output = precise_summation("sthk,shkv->sthv", query_heads, prefix_carry_state)
    mixed_heads = in_prefix * prefix_output + (1.0 - in_prefix) * causal
    scale_group = rms_scale(mixed_heads)
    unit_group = mixed_heads * scale_group
    normed_group = unit_group * gain_group.astype(jnp.float32)
    swish_gate = jax.nn.silu(gate_out).reshape(seq_count, tok_count, HEADS, HEAD_V)
    gated_rows = (
        (normed_group * swish_gate).reshape(seq_count, tok_count, VALS).astype(jnp.bfloat16)
    )
    branch = project(gated_rows, weight_o)
    resid_mid = resid_in + branch
    scale_two = rms_scale(resid_mid)
    unit_two = resid_mid * scale_two
    normed_two = (unit_two * gain_two.astype(jnp.float32)).astype(jnp.bfloat16)
    gate_part = project(normed_two, weight_gate)
    up_part = project(normed_two, weight_upper)
    gate_act = jax.nn.silu(gate_part)
    hidden = (gate_act * up_part).astype(jnp.bfloat16)
    ffn_out = project(hidden, weight_lower)
    layer_out = (resid_mid + ffn_out).astype(jnp.bfloat16)
    grad_out = out_grad.astype(jnp.float32)
    grad_hidden = back_project(out_grad, weight_lower)
    lower_grad = weight_grad(out_grad, hidden)
    grad_gate = (grad_hidden * up_part * silu_slope(gate_part)).astype(jnp.bfloat16)
    grad_up = (grad_hidden * gate_act).astype(jnp.bfloat16)
    gate_w_grad = weight_grad(normed_two, grad_gate)
    up_w_grad = weight_grad(normed_two, grad_up)
    grad_normed_two = back_project(grad_gate, weight_gate) + back_project(grad_up, weight_upper)
    gain_two_grad = jnp.sum(grad_normed_two * unit_two, axis=(0, 1))
    grad_mid = grad_out + rms_back(
        grad_normed_two * gain_two.astype(jnp.float32), unit_two, scale_two
    )
    ffn_mine = reduce_to_owner(
        jnp.concatenate([gate_w_grad, up_w_grad, lower_grad], axis=1).astype(jnp.bfloat16),
        names,
        sizes,
    ).astype(jnp.float32)
    grad_branch = grad_mid.astype(jnp.bfloat16)
    out_w_grad = weight_grad(gated_rows, grad_branch)
    grad_gated = back_project(grad_branch, weight_o).reshape(seq_count, tok_count, HEADS, HEAD_V)
    grad_normed_group = grad_gated * swish_gate
    grad_swish = (grad_gated * normed_group).reshape(seq_count, tok_count, VALS)
    grad_gate_out = (grad_swish * silu_slope(gate_out)).astype(jnp.bfloat16)
    group_grad = jnp.sum(grad_normed_group * unit_group, axis=(0, 1, 2))
    grad_mixed = rms_back(
        grad_normed_group * gain_group.astype(jnp.float32), unit_group, scale_group
    )
    grad_prefix = grad_mixed * in_prefix
    grad_causal = grad_mixed - grad_prefix
    grad_query_pre = precise_summation("sthv,shkv->sthk", grad_prefix, prefix_carry_state)
    prefix_term = precise_summation("sthk,sthv->shkv", query_heads, grad_prefix)
    grad_state = lax.psum(prefix_term.astype(jnp.bfloat16), seq).astype(jnp.float32)
    grad_q_local, grad_k_local, grad_v_local, grad_in, grad_starts, grad_cum, grad_tot = (
        pull_outputs((grad_causal, grad_state))
    )
    grad_end = chain_backward(total_dev, grad_in, seq)
    grad_total = jnp.sum(incoming * grad_end, axis=-1) * jnp.exp(total_dev)
    grad_k_chain, grad_v_chain, grad_decay = pull_states(
        (grad_total, grad_end, grad_starts, grad_cum, grad_tot)
    )
    grad_q = (
        (grad_query_pre + grad_q_local).reshape(seq_count, tok_count, KEYS).astype(jnp.bfloat16)
    )
    grad_k = (grad_k_local + grad_k_chain).reshape(seq_count, tok_count, KEYS).astype(jnp.bfloat16)
    grad_v = (grad_v_local + grad_v_chain).reshape(seq_count, tok_count, VALS).astype(jnp.bfloat16)
    grad_logits = (
        grad_decay.reshape(seq_count, tok_count, KEYS) * jax.nn.sigmoid(-logits) / 16.0
    ).astype(jnp.bfloat16)
    bias_grad = jnp.sum(grad_logits.astype(jnp.float32), axis=(0, 1))
    up_rank_grad = weight_grad(lowrank, grad_logits)
    grad_lowrank = back_project(grad_logits, weight_up).astype(jnp.bfloat16)
    down_rank_grad = weight_grad(normed, grad_lowrank)
    grad_normed = (
        back_project(grad_q, weight_q)
        + back_project(grad_k, weight_k)
        + back_project(grad_v, weight_v)
        + back_project(grad_gate_out, weight_g)
        + back_project(grad_lowrank, weight_down)
    )
    gain_one_grad = jnp.sum(grad_normed * unit_one, axis=(0, 1))
    tokens_grad = grad_mid + rms_back(
        grad_normed * gain_one.astype(jnp.float32), unit_one, scale_one
    )
    small_grads = pack_small_grads(
        down_rank_grad, gain_one_grad, gain_two_grad, bias_grad, group_grad, up_rank_grad, devices
    )
    mine = reduce_to_owner(
        jnp.concatenate(
            [
                weight_grad(normed, grad_q),
                weight_grad(normed, grad_k),
                weight_grad(normed, grad_v),
                weight_grad(normed, grad_gate_out),
                out_w_grad,
                small_grads,
            ],
            axis=1,
        ).astype(jnp.bfloat16),
        names,
        sizes,
    ).astype(jnp.float32)
    small = mine[:, 4096:]
    rows = mine.shape[0]
    return (
        layer_out,
        tokens_grad,
        small[:, 16],
        mine[:, :512],
        mine[:, 512:1024],
        mine[:, 1024:2048],
        mine[:, 2048:3072],
        small[:, :16],
        small[:, 24:32].reshape(KEYS // devices, 16).T,
        small[: KEYS // devices, 18],
        small[: HEAD_V // devices, 19],
        mine[:, 3072:4096],
        small[:, 17],
        ffn_mine[:, :FF],
        ffn_mine[:, FF : 2 * FF],
        ffn_mine[:, 2 * FF :].T,
    )


def solution(mesh):
    names, sizes = physical_axes(mesh)
    cut = next(
        i for i in range(len(sizes) + 1) if np.prod(sizes[:i], initial=1) == mesh.shape["dp"]
    )
    dp, seq = names[:cut], names[cut:]
    split = Mesh(mesh.devices.reshape(sizes), names)
    return jax.shard_map(
        partial(local, names, sizes, seq),
        mesh=split,
        in_specs=(
            P(dp, seq, None),
            P(dp),
            P(names),
            P(names, None),
            P(names, None),
            P(names, None),
            P(names, None),
            P(names, None),
            P(None, names),
            P(names),
            P(names),
            P(names, None),
            P(names),
            P(names, None),
            P(names, None),
            P(None, names),
            P(dp, seq, None),
        ),
        out_specs=(
            P(dp, seq, None),
            P(dp, seq, None),
            P(names),
            P(names, None),
            P(names, None),
            P(names, None),
            P(names, None),
            P(names, None),
            P(None, names),
            P(names),
            P(names),
            P(names, None),
            P(names),
            P(names, None),
            P(names, None),
            P(None, names),
        ),
        check_vma=False,
    )
```

time: 2800 us -> 1280 us (0.46)
  waiting for transfers between devices: 2010 us -> 609 us
  blocking collectives: 239 us -> 32.1 us
  local copies, waits for them, and re-layouts: 114 us -> 175 us
  other arithmetic: 80.8 us -> 117 us
    reduce_scatter x8 -> x2, waiting for transfers between devices: 1480 us -> 267 us  [reduce_to_owner(): return lax.psum_scatter(total, rest, scatter_dimension=0, tiled=True)]
    all_gather x2 -> x0, blocking collectives: 132 us -> none  [the longest x1 67.1 us: local(): lax.all_gather(decay_down, ('dp', 'seq'), axis=0, tiled=True)]
    all_gather x8 -> x2, waiting for transfers between devices: 259 us -> 173 us  [the longest x1 93.5 us: local(): lax.all_gather(jnp.concatenate([ffn_gate, ffn_up, ffn_down.T], axis=1), n...]
    unnamed x2 -> x0, blocking collectives: 80.2 us -> none
    unnamed x24 -> x8, waiting for transfers between devices: 66.1 us -> 0.13 us
  transfers between devices with their start and end apart: 22 -> 10, of which waited for: 18 -> 8; matrix products, arithmetic and copies ran while one was open for 12% -> 18% of each run, Pallas kernels for 0% -> 0%
where the time goes in v1:
time: 1280 us; the launch traced here: 1270 us
  waiting for transfers between devices  609 us (48%)
  matrix products  318 us (25%)
  local copies, waits for them, and re-layouts  175 us (14%)
  other arithmetic  117 us (9%)
  blocking collectives  32.1 us (3%)
  between operations  16 us (1%)
    reduce_scatter x2, waiting for transfers between devices, reduce_to_owner(): return lax.psum_scatter(total, rest, scatter_dimension=0, tiled=True)  267 us
    dot_general x21, matrix products, precise_summation(): jnp.einsum(pattern, *operands, precision=lax.Precision.HIGHEST, preferred...  133 us
    all_gather x1, waiting for transfers between devices, entering(): gathered = jax.tree.map(lambda a: lax.all_gather(a, axis), part)  117 us
    all_gather x1, waiting for transfers between devices, local(): lax.all_gather(jnp.concatenate([ffn_gate, ffn_up, ffn_down.T], axis=1), n...  93.5 us
    all_gather x1, waiting for transfers between devices, local(): lax.all_gather(pack_mixer(norm1_gain, norm2_gain, query_weight, key_weigh...  79.1 us
    dot_general x10, matrix products, back_project(): jnp.einsum('ste,de->std', gradient, weight, preferred_element_type=jnp.fl...  67.8 us
    dot_general x10, matrix products, project(): jnp.einsum('std,de->ste', inputs, weight, preferred_element_type=jnp.floa...  66.4 us
    dot_general x10, matrix products, weight_grad(): jnp.einsum('std,ste->de', inputs, gradient, preferred_element_type=jnp.fl...  50.3 us
  transfers between devices with their start and end apart: 10, of which 8 were waited for; matrix products, arithmetic and copies ran while one was open for 18% of the time, Pallas kernels for 0%

profile of v1, /device:TPU:0, one launch (start us, length us, event | category | flops | bytes accessed | tf_op | source)
XLA Modules:
  0.0 1268.2 jit_solution(606898675585786513)
XLA Ops:
  34.6 79.1 %all-gather.8.cloned.1.call-done = bf16[1024,4224]{1,0:T(8,128)(2,1)} async-done(((bf16[32,4224]{1,0:T(8,128)(2,1)}), bf16[1024,4224]{1,0:T(8,128)(2,1)}) %all-gather.8.cloned.1.call-update) | async-done | bytes 8650768 | tf_op jit(solution)/shard_map/all_gather | solution.py:292
  173.2 15.2 %all-gather = f32[16,4,128]{2,1,0:T(4,128)S(1)} all-gather(f32[4,4,128]{2,1,0:T(4,128)S(1)} %get-tuple-element.341), channel_id=2, replica_groups=mesh['y'=2,'x'=2,'core'=2,'z'=4] {'z'}, dimensions={0}, use_global_device_ids=true | all-gather | bytes 40960 | tf_op jit(solution)/shard_map/all_gather | solution.py:24
  189.3 117.3 %all-gather.10.cloned.1.call-done = f32[4,4,4,128,256]{4,3,2,1,0:T(8,128)} async-done(((f32[1,4,4,128,256]{4,3,2,1,0:T(8,128)}), f32[4,4,4,128,256]{4,3,2,1,0:T(8,128)}) %all-gather.10.cloned.1.call-update) | async-done | bytes 8388624 | tf_op jit(solution)/shard_map/all_gather | solution.py:24
  318.9 8.3 fusion.37
  332.6 16.9 %all-gather.2 = bf16[16,4,128]{2,1,0:T(4,128)(2,1)} all-gather(bf16[4,4,128]{2,1,0:T(4,128)(2,1)S(1)} %convert_element_type.266), channel_id=4, replica_groups=mesh['y'=2,'x'=2,'core'=2,'z'=4] {'z'}, dimensions={0}, use_global_device_ids=true | all-gather | bytes 20480 | tf_op jit(solution)/shard_map/all_gather | solution.py:40
  395.3 93.5 %all-gather.12.cloned.1.call-done = bf16[1024,8448]{1,0:T(8,128)(2,1)} async-done(((bf16[32,8448]{1,0:T(8,128)(2,1)}), bf16[1024,8448]{1,0:T(8,128)(2,1)}) %all-gather.12.cloned.1.call-update) | async-done | bytes 17301520 | tf_op jit(solution)/shard_map/all_gather | solution.py:310
  488.8 11.9 fusion.21
  500.7 11.5 fusion.23
  512.2 22.7 %fusion.2 = (bf16[4,256,2816]{2,1,0:T(8,128)(2,1)}, bf16[4,256,2816]{2,1,0:T(8,128)(2,1)}, bf16[4,256,2816]{2,1,0:T(8,128)(2,1)}) fusion(f32[4,256,2816]{2,1,0:T(8,128)} %fusion.21, f32[4,256,2816]{2,1,0:T(8,128)} %fusion.23, bf16[4,256,1024]{2,1,0:T(8,128)(2,1)} %param.49, bf16[1024,8448]{1,0:T(8,128)(2,1)} %all-gather.12.cloned.1.call-done), kind=kOutput, calls=%fused_computation.12 | convolution fusion | flops 5948833792 | bytes 48234496 | tf_op jit(solution)/shard_map/ste,de->std/dot_general | solution.py:71
  534.9 10.0 fusion.20
  544.9 9.1 multiply_reduce_fusion.3
  555.3 7.6 fusion.120
  569.2 11.4 multiply_subtract_fusion
  586.0 17.6 %multiply_reduce_fusion = (f32[4,4,4,128]{3,2,0,1:T(4,128)S(1)}, f32[4,4,128,256]{3,2,1,0:T(8,128)}, f32[4,4,4,128,256]{4,3,2,0,1:T(8,128)}) fusion(f32[4,4,128,256]{3,2,1,0:T(8,128)S(1)} %get-tuple-element.216, f32[4,4,4,256,64]{3,4,1,2,0:T(8,128)} %bitcast.462, f32[4,4,64,4,128]{4,2,3,1,0:T(8,128)} %get-tuple-element.328, f32[4,4,4,128]{3,2,1,0:T(4,128)S(1)} %bitcast.520), kind=kOutput, calls=%fused_computation.19 | convolution fusion | flops 1618468864 | bytes 18939904 | tf_op jit(solution)/shard_map/transpose(jvp(snihk,snhkv->snihv))/dot_general | solution.py:61
  603.7 8.4 fusion.43
  625.9 11.3 fusion.8
  637.2 28.6 %all-reduce.17.cloned.1.call-done = bf16[4,4,128,256]{3,2,1,0:T(8,128)(2,1)} async-done(((bf16[4,4,128,256]{3,2,1,0:T(8,128)(2,1)}), bf16[4,4,128,256]{3,2,1,0:T(8,128)(2,1)}) %all-reduce.17.cloned.1.call-update) | async-done | bytes 1048592 | tf_op jit(solution)/shard_map/psum | solution.py:411
  696.7 7.4 fusion.108
  715.9 8.7 bitcast_convert_fusion.1
  724.6 8.5 bitcast_convert_fusion
  733.0 16.5 %all-gather.14.cloned.1.call-done = bf16[16,4,128,256]{3,2,1,0:T(8,128)(2,1)} async-done(((bf16[4,4,128,256]{3,2,1,0:T(8,128)(2,1)}), bf16[16,4,128,256]{3,2,1,0:T(8,128)(2,1)}) %all-gather.14.cloned.1.call-update) | async-done | bytes 4194320 | tf_op jit(solution)/shard_map/all_gather | solution.py:40
  751.1 12.9 %while.33 = (s32[]{:T(128)}, f32[4,4,128,256]{3,2,1,0:T(8,128)}, s32[]{:T(128)}, bf16[4,4,4,128]{3,2,1,0:T(4,128)(2,1)}, bf16[4,4,4,128,256]{4,3,2,1,0:T(8,128)(...) while((s32[]{:T(128)}, f32[4,4,128,256]{3,2,1,0:T(8,128)}, s32[]{:T(128)}, ...), condition=%wide.region_19.20_spmd, body=%wide.region_18.19_spmd.sunk | while | flops 1574918 | bytes 5263515 | solution.py:57
  764.1 8.0 fusion.63
  784.3 13.8 %fusion.129 = (f32[4,4,4,128]{3,2,1,0:T(4,128)}, f32[4,4,64,4,128]{4,2,3,1,0:T(8,128)}, f32[4,4,64,4,128]{4,2,3,1,0:T(8,128)}, f32[4,4,64,4,128]{4,2,3,1,0:T(8,128)}, f32[4,4,4,128,64]{3,4,2,1,0:T(8,128)}) fusion(f32[4,4,64,4,128]{4,2,3,1,0:T(8,128)S(1)} %copy-done.4, f32[4,4,64,4,128]{4,3,2,1,0:T(4,128)S(1)} %copy-done.6, ...), kind=kOutput, calls=%fused_computation.207 | convolution fusion | flops 1621090304 | bytes 27328512 | tf_op jit(solution)/shard_map/transpose(jvp(snjhk,snjhv->snhkv))/dot_general | solution.py:61
  902.0 13.9 %concatenate.57 = bf16[4,2,128,4224]{3,2,1,0:T(8,128)(2,1)} concatenate(bf16[4,2,128,512]{3,2,1,0:T(8,128)(2,1)} %bitcast_convert_fusion.6, bf16[4,2,128,512]{3,2,1,0:T(8,128)(2,1)} %bitcast_convert_fusion.5, bf16[4,2,128,1024]{3,2,1,0:T(8,128)(2,1)} %bitcast_convert_fusion.4, bf16[4,2,128,1024]{3,2,1,0:T(8,128)(2,1)} %bitcast.511, bf16[4,2,128,1024]{3,2,1,0:T(8,128)(2,1)} %copy.463, ...), dimensions={3} | concatenate | bytes 17301504 | tf_op jit(solution)/shard_map/concatenate | solution.py:447
  920.9 9.4 bitcast_convert_fusion.2
  937.1 7.4 dynamic-slice_bitcast_fusion
  951.4 7.4 collective-permute-done.1
  958.8 9.3 bitcast_add_fusion.1
  968.2 11.8 add_convert_fusion
  982.6 104.5 %reduce-scatter.3.cloned.1.call-done = bf16[32,4224]{1,0:T(8,128)(2,1)} async-done(((bf16[512,4224]{1,0:T(8,128)(2,1)}), bf16[32,4224]{1,0:T(8,128)(2,1)}) %reduce-scatter.3.cloned.1.call-update) | async-done | bytes 270352 | tf_op jit(solution)/shard_map/reduce_scatter | solution.py:266
  1096.1 162.0 %reduce-scatter.5.cloned.1.call-done = bf16[32,8448]{1,0:T(8,128)(2,1)} async-done(((bf16[512,8448]{1,0:T(8,128)(2,1)}), bf16[32,8448]{1,0:T(8,128)(2,1)}) %reduce-scatter.5.cloned.1.call-update) | async-done | bytes 540688 | tf_op jit(solution)/shard_map/reduce_scatter | solution.py:266
  (456 shorter events, 383.0 us)
Async XLA Ops:
  7.2 106.5 %all-gather.8.cloned.1.call-start = ((), (), s32[]{:S(2)}) async-start(), calls=%async_computation.2 | async-start | bytes 8921088 | tf_op jit(solution)/shard_map/all_gather | solution.py:292
  32.3 86.2 %copy-start.21 = (bf16[4,256,1024]{2,1,0:T(8,128)(2,1)S(1)}, bf16[4,256,1024]{2,1,0:T(8,128)(2,1)}, u32[]{:S(2)}) copy-start(bf16[4,256,1024]{2,1,0:T(8,128)(2,1)} %param.33) | copy-start | bytes 6291460
  32.3 274.3 %all-gather.10.cloned.1.call-start = ((), (), s32[]{:S(2)}) async-start(), calls=%async_computation.3 | async-start | bytes 10485760 | tf_op jit(solution)/shard_map/all_gather | solution.py:24
  34.6 127.5 %copy-start.91 = (f32[4,256]{1,0:T(4,128)}, f32[4,256]{1,0:T(4,128)S(1)}, u32[]{:S(2)}) copy-start(f32[4,256]{1,0:T(4,128)S(1)} %add_rsqrt_fusion.2) | copy-start | bytes 12292
  118.5 43.6 %copy-start.89 = (f32[1024]{0:T(1024)}, f32[1024]{0:T(1024)S(1)}, u32[]{:S(2)}) copy-start(f32[1024]{0:T(1024)S(1)} %get-tuple-element.267) | copy-start | bytes 12292
  127.7 39.7 %copy-start.3 = (f32[4,4,64,4,128]{4,2,3,1,0:T(8,128)}, f32[4,4,64,4,128]{4,2,3,1,0:T(8,128)S(1)}, u32[]{:S(2)}) copy-start(f32[4,4,64,4,128]{4,2,3,1,0:T(8,128)S(1)} %fusion.111) | copy-start | bytes 6291460
  127.8 221.8 %copy-start.45 = (f32[4,4,1,4,128]{4,2,3,1,0:T(1,128)}, f32[4,4,1,4,128]{4,2,3,1,0:T(1,128)S(1)}, u32[]{:S(2)}) copy-start(f32[4,4,1,4,128]{4,2,3,1,0:T(1,128)S(1)} %slice.288) | copy-start | bytes 98308
  145.7 210.3 %copy-start.68 = (f32[4,4,128]{2,1,0:T(4,128)}, f32[4,4,128]{2,1,0:T(4,128)S(1)}, u32[]{:S(2)}) copy-start(f32[4,4,128]{2,1,0:T(4,128)S(1)} %get-tuple-element.344) | copy-start | bytes 24580
  157.6 222.4 %all-reduce.15.cloned.1.call-start = ((), (), s32[]{:S(2)}) async-start(), calls=%async_computation.4 | async-start | bytes 2097152 | tf_op jit(solution)/shard_map/psum | solution.py:359
  158.3 30.9 %copy-start.109 = (f32[4]{0:T(128)}, f32[4]{0:T(128)S(1)}, u32[]{:S(2)}) copy-start(f32[4]{0:T(128)S(1)} %fusion.175) | copy-start | bytes 52
  159.0 147.8 %copy-start.87 = (f32[4,256]{1,0:T(4,128)}, f32[4,256]{1,0:T(4,128)S(1)}, u32[]{:S(2)}) copy-start(f32[4,256]{1,0:T(4,128)S(1)} %get-tuple-element.350) | copy-start | bytes 12292
  159.0 147.8 %copy-start.101 = (pred[4,256]{1,0:T(4,128)(4,1)}, pred[4,256]{1,0:T(4,128)(4,1)S(1)}, u32[]{:S(2)}) copy-start(pred[4,256]{1,0:T(4,128)(4,1)S(1)} %get-tuple-element.351) | copy-start | bytes 3076
  167.3 150.3 %copy-start.74 = (f32[4,4,128]{2,1,0:T(4,128)}, f32[4,4,128]{2,1,0:T(4,128)S(1)}, u32[]{:S(2)}) copy-start(f32[4,4,128]{2,1,0:T(4,128)S(1)} %get-tuple-element.341) | copy-start | bytes 24580
  189.2 117.6 %copy-start.66 = (f32[4,1,4,128]{3,1,2,0:T(1,128)}, f32[4,1,4,128]{3,1,2,0:T(1,128)S(1)}, u32[]{:S(2)}) copy-start(f32[4,1,4,128]{3,1,2,0:T(1,128)S(1)} %fusion.163) | copy-start | bytes 24580
  189.3 117.6 %copy-start.83 = (f32[4,4,128]{2,1,0:T(4,128)}, f32[4,4,128]{2,1,0:T(4,128)S(1)}, u32[]{:S(2)}) copy-start(f32[4,4,128]{2,1,0:T(4,128)S(1)} %exponential_multiply_fusion.1) | copy-start | bytes 24580
  312.5 176.3 %all-gather.12.cloned.1.call-start = ((), (), s32[]{:S(2)}) async-start(), calls=%async_computation.5 | async-start | bytes 17842176 | tf_op jit(solution)/shard_map/all_gather | solution.py:310
  313.5 352.4 %all-reduce.17.cloned.1.call-start = ((), (), s32[]{:S(2)}) async-start(), calls=%async_computation.6 | async-start | bytes 2097152 | tf_op jit(solution)/shard_map/psum | solution.py:411
  356.1 13.7 %copy-start.20 = (f32[4,4,4,64,64]{4,3,2,1,0:T(8,128)}, f32[4,4,4,64,64]{4,3,2,1,0:T(8,128)S(1)}, u32[]{:S(2)}) copy-start(f32[4,4,4,64,64]{4,3,2,1,0:T(8,128)S(1)} %fusion.154) | copy-start | bytes 3145732
  586.0 17.6 %copy-start.8 = (f32[4,256,4,256]{3,1,2,0:T(8,128)S(1)}, f32[4,256,4,256]{3,1,2,0:T(8,128)}, u32[]{:S(2)}) copy-start(f32[4,256,4,256]{3,1,2,0:T(8,128)} %copy.249) | copy-start | bytes 12582916
  615.7 133.8 %all-gather.14.cloned.1.call-start = ((), (), s32[]{:S(2)}) async-start(), calls=%async_computation.9 | async-start | bytes 5242880 | tf_op jit(solution)/shard_map/all_gather | solution.py:40
  625.9 39.9 %copy-start.84 = (f32[4,4,128]{2,1,0:T(4,128)S(1)}, f32[4,4,128]{2,1,0:T(4,128)}, u32[]{:S(2)}) copy-start(f32[4,4,128]{2,1,0:T(4,128)} %copy-done.83) | copy-start | bytes 24580
  669.2 417.9 %reduce-scatter.3.cloned.1.call-start = ((), (), s32[]{:S(2)}) async-start(), calls=%async_computation.7 | async-start | bytes 4595712 | tf_op jit(solution)/shard_map/reduce_scatter | solution.py:266
  751.1 12.9 %copy-start.27 = (bf16[4,4,128,256]{3,2,1,0:T(8,128)(2,1)S(1)}, bf16[4,4,128,256]{3,2,1,0:T(8,128)(2,1)}, u32[]{:S(2)}) copy-start(bf16[4,4,128,256]{3,2,1,0:T(8,128)(2,1)} %all-reduce.17.cloned.1.call-done) | copy-start | bytes 3145732
  751.1 12.9 %copy-start.69 = (f32[4,4,128]{2,1,0:T(4,128)S(1)}, f32[4,4,128]{2,1,0:T(4,128)}, u32[]{:S(2)}) copy-start(f32[4,4,128]{2,1,0:T(4,128)} %copy-done.68) | copy-start | bytes 24580
  751.1 12.9 %copy-start.78 = (f32[4,4,128]{2,1,0:T(4,128)S(1)}, f32[4,4,128]{2,1,0:T(4,128)}, u32[]{:S(2)}) copy-start(f32[4,4,128]{2,1,0:T(4,128)} %copy-done.76) | copy-start | bytes 24580
  751.1 12.9 %copy-start.81 = (f32[4,4,128]{2,1,0:T(4,128)S(1)}, f32[4,4,128]{2,1,0:T(4,128)}, u32[]{:S(2)}) copy-start(f32[4,4,128]{2,1,0:T(4,128)} %copy-done.79) | copy-start | bytes 24580
  751.1 12.9 %copy-start.86 = (f32[4,4,128]{2,1,0:T(4,128)S(1)}, f32[4,4,128]{2,1,0:T(4,128)}, u32[]{:S(2)}) copy-start(f32[4,4,128]{2,1,0:T(4,128)} %copy-done.85) | copy-start | bytes 24580
  916.0 14.3 %slice-start = ((s8[5767168]{0:T(1024)(128)(4,1)}), s8[1572864]{0:T(1024)(128)(4,1)S(1)}, s32[]{:S(2)}) async-start(s8[5767168]{0:T(1024)(128)(4,1)} %bitcast.491), calls=%async_computation.10 | async-start | bytes 3145728
  916.0 14.4 %slice-start.2 = ((s8[5767168]{0:T(1024)(128)(4,1)}), s8[4194304]{0:T(1024)(128)(4,1)S(1)}, s32[]{:S(2)}) async-start(s8[5767168]{0:T(1024)(128)(4,1)} %bitcast.494), calls=%async_computation.12 | async-start | bytes 8388608
  920.9 24.5 %collective-permute-start = (bf16[4,128,4224]{2,1,0:T(8,128)(2,1)}, bf16[4,128,4224]{2,1,0:T(8,128)(2,1)}, u32[]{:S(2)}, u32[]{:S(2)}) collective-permute-start(bf16[4,128,4224]{2,1,0:T(8,128)(2,1)} %dynamic-slice_bitcast_fusion.1), channel_id=1, source_target_pairs={{0,4},{4,0},{1,5},{5,1},{2,6},{6,2},{3,7},{7,3},{8,12},{12,8},{9,1... | collective-permute-start | bytes 12976136 | tf_op jit(solution)/shard_map/ppermute | solution.py:263
  944.6 14.3 %collective-permute-start.1 = (bf16[4,128,8448]{2,1,0:T(8,128)(2,1)}, bf16[4,128,8448]{2,1,0:T(8,128)(2,1)}, u32[]{:S(2)}, u32[]{:S(2)}) collective-permute-start(bf16[4,128,8448]{2,1,0:T(8,128)(2,1)} %dynamic-slice_bitcast_fusion), channel_id=1, source_target_pairs={{0,4},{4,0},{1,5},{5,1},{2,6},{6,2},{3,7},{7,3},{8,12},{12,8},{9,1... | collective-permute-start | bytes 25952264 | tf_op jit(solution)/shard_map/ppermute | solution.py:263
  951.4 306.8 %reduce-scatter.5.cloned.1.call-start = ((), (), s32[]{:S(2)}) async-start(), calls=%async_computation.8 | async-start | bytes 9191424 | tf_op jit(solution)/shard_map/reduce_scatter | solution.py:266
  (99 other events, 519.7 us)
Sparse Core Ops, SparseCore 0:
  32.4 81.2 all-gather.7
  157.8 148.7 all-gather.9
  312.6 56.4 all-reduce.14
  372.1 116.6 all-gather.11
  615.8 49.9 all-reduce.16
  669.3 80.1 all-gather.13
  951.5 135.5 reduce-scatter.2
  1093.7 164.4 reduce-scatter.4

commit v2 on v1

--- a/solution.py
+++ b/solution.py
@@ -4,6 +4,8 @@
 import jax.numpy as jnp
 import numpy as np
 from jax import lax
+from jax.experimental import pallas as pl
+from jax.experimental.pallas import tpu as pltpu
 from jax.sharding import Mesh
 from jax.sharding import PartitionSpec as P
 
@@ -19,50 +21,6 @@
 norm_eps = 1e-05
 
 
-def entering(part, axis, combine, identity):
-    place = lax.axis_index(axis)
-    gathered = jax.tree.map(lambda a: lax.all_gather(a, axis), part)
-    state = jax.tree.map(lambda a, e: jnp.zeros_like(a) + jnp.asarray(e, a.dtype), part, identity)
-
-    def entering_one(lap, state):
-        return combine(
-            state, jax.tree.map(lambda a: lax.dynamic_index_in_dim(a, lap, 0, False), gathered)
-        )
-
-    return lax.fori_loop(0, place, entering_one, state)
-
-
-def carried_in(x, axis, join, neutral):
-    count = lax.axis_size(axis)
-    place = lax.axis_index(axis)
-    ahead = count - 1 - place
-    gathered = jax.tree.map(
-        lambda a, kind: lax.all_gather(a.astype(kind), axis),
-        x,
-        jax.tree.map(lambda a: jnp.bfloat16 if a.dtype == jnp.float32 else a.dtype, x),
-    )
-    state = jax.tree.map(lambda a, e: jnp.zeros_like(a) + jnp.asarray(e, a.dtype), x, neutral)
-
-    def carried_one(lap, state):
-        source = count - 1 - lap
-        return join(
-            state,
-            jax.tree.map(
-                lambda a, own: lax.dynamic_index_in_dim(a, source, 0, False).astype(own.dtype),
-                gathered,
-                x,
-            ),
-        )
-
-    return lax.fori_loop(0, ahead, carried_one, state)
-
-
-def precise_summation(pattern, *operands):
-    return jnp.einsum(
-        pattern, *operands, precision=lax.Precision.HIGHEST, preferred_element_type=jnp.float32
-    )
-
-
 def project(inputs, weight):
     return jnp.einsum("std,de->ste", inputs, weight, preferred_element_type=jnp.float32)
 
@@ -90,95 +48,579 @@
     return logistic * (1.0 + values * (1.0 - logistic))
 
 
-def chain_combine(earlier, later):
-    return (earlier[0] + later[0], jnp.exp(later[0])[..., None] * earlier[1] + later[1])
-
-
-def lower_ones(extent):
-    indices = jnp.arange(extent)
-    return (indices[:, None] >= indices[None, :]).astype(jnp.float32)
-
-
-def local_states(key_matrix, valued, decays):
-    seq_count, tok_count, head_count, key_width = key_matrix.shape
-    blocks = tok_count // SPAN
-    key_blocks = key_matrix.reshape(seq_count, blocks, SPAN, head_count, key_width)
-    value_blocks = valued.reshape(seq_count, blocks, SPAN, head_count, valued.shape[-1])
-    decay_blocks = decays.reshape(seq_count, blocks, SPAN, head_count, key_width)
-    cumulative_decay = precise_summation("ij,snjhk->snihk", lower_ones(SPAN), decay_blocks)
-    running_totals = cumulative_decay[:, :, -1]
-    shares = precise_summation(
-        "snjhk,snjhv->snhkv",
-        key_blocks * jnp.exp(running_totals[:, :, None] - cumulative_decay),
-        value_blocks,
-    )
-    carried_state = jnp.zeros_like(shares[:, 0])
-    starts = []
-    for number in range(blocks):
-        starts.append(carried_state)
-        carried_state = (
-            jnp.exp(running_totals[:, number])[..., None] * carried_state + shares[:, number]
+CHUNK = 128
+MESH = pl.DeviceIdType.MESH
+
+
+def nn(a, b):
+    return lax.dot_general(a, b, (((1,), (0,)), ((), ())), preferred_element_type=jnp.float32)
+
+
+def nt(a, b):
+    return lax.dot_general(a, b, (((1,), (1,)), ((), ())), preferred_element_type=jnp.float32)
+
+
+def tn(a, b):
+    return lax.dot_general(a, b, (((0,), (0,)), ((), ())), preferred_element_type=jnp.float32)
+
+
+def low(values):
+    return values.astype(jnp.bfloat16)
+
+
+def wide(values):
+    return values.astype(jnp.float32)
+
+
+def three_way(ones, values):
+    first = low(values)
+    left = values - wide(first)
+    second = low(left)
+    third = low(left - wide(second))
+    return nn(ones, first) + nn(ones, second) + nn(ones, third)
+
+
+def iota(shape, dim):
+    return lax.broadcasted_iota(jnp.int32, shape, dim)
+
+
+def place_on(axes):
+    place = 0
+    for name, size in axes:
+        place = place * size + lax.axis_index(name)
+    return place
+
+
+def device_at(axes, place):
+    where = {}
+    for name, size in reversed(axes):
+        where[name] = lax.rem(place, size)
+        place = lax.div(place, size)
+    return where
+
+
+def line_length(axes):
+    return int(np.prod([size for _, size in axes]))
+
+
+def greet(axes, place, count):
+    barrier = pltpu.get_barrier_semaphore()
+
+    @pl.when(place > 0)
+    def _():
+        pl.semaphore_signal(
+            barrier, inc=1, device_id=device_at(axes, place - 1), device_id_type=MESH
         )
-    return (
-        jnp.sum(running_totals, axis=1),
-        carried_state,
-        jnp.stack(starts, axis=1),
-        cumulative_decay,
-        running_totals,
-    )
-
-
-def local_outputs(
-    queries,
-    key_matrix,
-    valued,
-    incoming,
-    starts,
-    cumulative_decay,
-    running_totals,
-    end_local=None,
-    is_owner=None,
+
+    @pl.when(place < count - 1)
+    def _():
+        pl.semaphore_signal(
+            barrier, inc=1, device_id=device_at(axes, place + 1), device_id_type=MESH
+        )
+
+    @pl.when(jnp.logical_or(place == 0, place == count - 1))
+    def _():
+        pl.semaphore_wait(barrier, 1)
+
+    @pl.when(jnp.logical_and(place > 0, place < count - 1))
+    def _():
+        pl.semaphore_wait(barrier, 2)
+
+
+def send(source, target, send_sem, recv_sem, axes, place):
+    return pltpu.make_async_remote_copy(
+        src_ref=source,
+        dst_ref=target,
+        send_sem=send_sem,
+        recv_sem=recv_sem,
+        device_id=device_at(axes, place),
+        device_id_type=MESH,
+    )
+
+
+def row_places(count):
+    return iota((count, HEAD_K), 0)
+
+
+def prefix_weights(cum, end_local, count):
+    rows = row_places(count)
+    owner = jnp.logical_and(end_local >= 0, end_local < count)
+    end_cum = jnp.sum(jnp.where(rows == end_local, cum, 0.0), axis=0, keepdims=True)
+    keep = jnp.logical_and(rows <= end_local, rows <= jnp.where(owner, count, -1))
+    weights = jnp.where(keep, jnp.exp(jnp.where(keep, end_cum - cum, 0.0)), 0.0)
+    return weights, jnp.exp(end_cum) * jnp.where(owner, 1.0, 0.0)
+
+
+def chunk_parts(cum, chunk):
+    begin = chunk * CHUNK
+    piece = cum[begin : begin + CHUNK]
+    if chunk:
+        piece = piece - cum[begin - 1 : begin]
+    return piece, piece[CHUNK - 1 :], piece[CHUNK // 2 - 1 : CHUNK // 2]
+
+
+def forward_kernel(
+    axes,
+    prefix_ref,
+    q_ref,
+    k_ref,
+    v_ref,
+    decay_ref,
+    mixed_ref,
+    cum_ref,
+    state_ref,
+    prefix_state_ref,
+    kv_ref,
+    part_ref,
+    edge_ref,
+    right_out,
+    right_in,
+    left_out,
+    left_in,
+    right_sent,
+    right_got,
+    left_sent,
+    left_got,
 ):
-    seq_count, tok_count, head_count, key_width = queries.shape
-    val_width = valued.shape[-1]
-    blocks = tok_count // SPAN
-    query_blocks = queries.reshape(seq_count, blocks, SPAN, head_count, key_width)
-    key_blocks = key_matrix.reshape(seq_count, blocks, SPAN, head_count, key_width)
-    value_blocks = valued.reshape(seq_count, blocks, SPAN, head_count, val_width)
-    before = jnp.cumsum(running_totals, axis=1) - running_totals
-    block_states = jnp.exp(before)[..., None] * incoming[:, None] + starts
-    query_input = query_blocks * jnp.exp(cumulative_decay)
-    key_in = key_blocks * jnp.exp(-cumulative_decay)
-    attention_scores = precise_summation("snihk,snjhk->snhij", query_input, key_in) * lower_ones(
-        SPAN
-    )
-    causal = precise_summation(
-        "snhij,snjhv->snihv", attention_scores, value_blocks
-    ) + precise_summation("snihk,snhkv->snihv", query_input, block_states)
-    causal = causal.reshape(seq_count, tok_count, head_count, val_width)
-    position_cum = (cumulative_decay + before[:, :, None]).reshape(
-        seq_count, tok_count, head_count, key_width
-    )
-    places = jnp.arange(tok_count)
-    select = (places[None, :] == end_local[:, None]).astype(jnp.float32)
-    end_cum = precise_summation("st,sthk->shk", select, position_cum)
-    keep_mask = (places[None, :] <= end_local[:, None]) & is_owner[:, None]
-    exponent = jnp.where(keep_mask[:, :, None, None], end_cum[:, None] - position_cum, 0.0)
-    weight_bundle = jnp.exp(exponent) * keep_mask.astype(jnp.float32)[:, :, None, None]
-    partial_state = precise_summation("sthk,sthv->shkv", key_matrix * weight_bundle, valued)
-    owner_weight = is_owner.astype(jnp.float32)[:, None, None, None]
-    partial_state = partial_state + owner_weight * jnp.exp(end_cum)[..., None] * incoming
-    return (causal, partial_state)
-
-
-def chain_forward(total_dev, state_dev, seq):
-    identity = (jnp.zeros_like(total_dev), jnp.zeros_like(state_dev))
-    return entering((total_dev, state_dev), seq, chain_combine, identity)[1]
-
-
-def chain_backward(total_dev, grad_in, seq):
-    identity = (jnp.zeros_like(total_dev), jnp.zeros_like(grad_in))
-    return carried_in((total_dev, grad_in), seq, chain_combine, identity)[1]
+    count = line_length(axes)
+    place = place_on(axes)
+    seqs = prefix_ref.shape[0]
+    toks = q_ref.shape[0] // seqs
+    chunks = toks // CHUNK
+    greet(axes, place, count)
+    lower = low(jnp.where(iota((CHUNK, CHUNK), 0) >= iota((CHUNK, CHUNK), 1), 1.0, 0.0))
+    causal = iota((CHUNK, CHUNK), 0) >= iota((CHUNK, CHUNK), 1)
+
+    def to_right(i):
+        return send(right_out.at[i], right_in.at[i], right_sent.at[i], right_got.at[i], axes, place + 1)
+
+    def to_left(i):
+        return send(left_out.at[i], left_in.at[i], left_sent.at[i], left_got.at[i], axes, place - 1)
+
+    def states_of(seq, carry):
+        rows = pl.ds(pl.multiple_of(seq * toks, toks), toks)
+        end_local = prefix_ref[seq] - 1 - place * toks
+        for head in range(HEADS):
+            i = seq * HEADS + head
+            keys = slice(head * HEAD_K, (head + 1) * HEAD_K)
+            vals = slice(head * HEAD_V, (head + 1) * HEAD_V)
+            before = jnp.zeros((1, HEAD_K), jnp.float32)
+            key = wide(k_ref[rows, keys])
+            value = v_ref[rows, vals]
+            decay = decay_ref[rows, keys]
+            pieces = []
+            local = jnp.zeros((HEAD_V, HEAD_K), jnp.float32)
+            for chunk in range(chunks):
+                at = slice(chunk * CHUNK, (chunk + 1) * CHUNK)
+                piece = three_way(lower, decay[at])
+                total = piece[CHUNK - 1 :]
+                share = tn(value[at], low(key[at] * jnp.exp(total - piece)))
+                kv_ref[i, chunk] = share
+                local = jnp.exp(total) * local + share
+                pieces.append(piece + before)
+                before = before + total
+            cum = jnp.concatenate(pieces, axis=0)
+            cum_ref[rows, keys] = cum
+            weights, edge = prefix_weights(cum, end_local, toks)
+            part_ref[i] = tn(value, low(key * weights))
+            edge_ref[i] = jnp.broadcast_to(edge, (8, HEAD_K))
+
+            @pl.when(place == 0)
+            def _():
+                right_out[i] = low(local)
+                if count > 1:
+                    to_right(i).start()
+
+        return carry
+
+    lax.fori_loop(0, seqs, states_of, 0)
+
+    def outputs_of(seq, carry):
+        rows = pl.ds(pl.multiple_of(seq * toks, toks), toks)
+        for head in range(HEADS):
+            i = seq * HEADS + head
+            keys = slice(head * HEAD_K, (head + 1) * HEAD_K)
+            vals = slice(head * HEAD_V, (head + 1) * HEAD_V)
+            cum = cum_ref[rows, keys]
+            query = wide(q_ref[rows, keys])
+            key = wide(k_ref[rows, keys])
+            value = v_ref[rows, vals]
+            scores = []
+            for chunk in range(chunks):
+                at = slice(chunk * CHUNK, (chunk + 1) * CHUNK)
+                piece, total, middle = chunk_parts(cum, chunk)
+                raw = nt(
+                    low(query[at] * jnp.exp(piece - middle)), low(key[at] * jnp.exp(middle - piece))
+                )
+                scores.append(low(jnp.where(causal, raw, 0.0)))
+
+            @pl.when(place == 0)
+            def _():
+                right_in[i] = jnp.zeros((HEAD_V, HEAD_K), jnp.bfloat16)
+
+            @pl.when(place > 0)
+            def _():
+                send(right_out.at[i], right_in.at[i], right_sent.at[i], right_got.at[i], axes, place - 1).wait_recv()
+
+            state = wide(right_in[i])
+            part = part_ref[i] + edge_ref[i][:1] * state
+            part_ref[i] = part
+            for chunk in range(chunks):
+                at = slice(chunk * CHUNK, (chunk + 1) * CHUNK)
+                piece, total, middle = chunk_parts(cum, chunk)
+                narrow = low(state)
+                state_ref[i, chunk] = narrow
+                output = nn(scores[chunk], value[at]) + nt(
+                    low(query[at] * jnp.exp(piece)), narrow
+                )
+                mixed_ref[pl.ds(seq * toks + chunk * CHUNK, CHUNK), vals] = output
+                state = jnp.exp(total) * state + kv_ref[i, chunk]
+            state_ref[i, chunks] = low(state)
+
+            @pl.when(jnp.logical_and(place > 0, place < count - 1))
+            def _():
+                right_out[i] = low(state)
+                to_right(i).start()
+
+            if count > 1:
+
+                @pl.when(place == count - 1)
+                def _():
+                    left_out[i] = low(part)
+                    to_left(i).start()
+
+        return carry
+
+    lax.fori_loop(0, seqs, outputs_of, 0)
+
+    def prefix_of(seq, carry):
+        rows = pl.ds(pl.multiple_of(seq * toks, toks), toks)
+        end_local = prefix_ref[seq] - 1 - place * toks
+        inside = iota((toks, HEAD_V), 0) <= end_local
+        for head in range(HEADS):
+            i = seq * HEADS + head
+            keys = slice(head * HEAD_K, (head + 1) * HEAD_K)
+            vals = slice(head * HEAD_V, (head + 1) * HEAD_V)
+
+            @pl.when(place < count - 1)
+            def _():
+                send(left_out.at[i], left_in.at[i], left_sent.at[i], left_got.at[i], axes, place + 1).wait_recv()
+
+            @pl.when(place == count - 1)
+            def _():
+                left_in[i] = jnp.zeros((HEAD_V, HEAD_K), jnp.bfloat16)
+
+            whole = low(part_ref[i] + wide(left_in[i]))
+
+            @pl.when(jnp.logical_and(place > 0, place < count - 1))
+            def _():
+                left_out[i] = whole
+                to_left(i).start()
+
+            prefix_state_ref[i] = whole
+            mixed_ref[rows, vals] = jnp.where(
+                inside, nt(q_ref[rows, keys], whole), mixed_ref[rows, vals]
+            )
+        return carry
+
+    lax.fori_loop(0, seqs, prefix_of, 0)
+
+    def finish(i, carry):
+        @pl.when(place < count - 1)
+        def _():
+            to_right(i).wait_send()
+
+        @pl.when(place > 0)
+        def _():
+            to_left(i).wait_send()
+
+        return carry
+
+    lax.fori_loop(0, seqs * HEADS, finish, 0)
+
+
+def backward_kernel(
+    axes,
+    prefix_ref,
+    q_ref,
+    k_ref,
+    v_ref,
+    cum_ref,
+    state_ref,
+    prefix_state_ref,
+    grad_ref,
+    dq_ref,
+    dk_ref,
+    dv_ref,
+    ddecay_ref,
+    local_ref,
+    acc_ref,
+    dk_part,
+    dv_part,
+    dcum_part,
+    right_out,
+    right_in,
+    left_out,
+    left_in,
+    right_sent,
+    right_got,
+    left_sent,
+    left_got,
+):
+    count = line_length(axes)
+    place = place_on(axes)
+    seqs = prefix_ref.shape[0]
+    toks = q_ref.shape[0] // seqs
+    chunks = toks // CHUNK
+    greet(axes, place, count)
+    causal = iota((CHUNK, CHUNK), 0) >= iota((CHUNK, CHUNK), 1)
+    upper = low(jnp.where(iota((toks, toks), 0) <= iota((toks, toks), 1), 1.0, 0.0))
+
+    def to_right(i):
+        return send(right_out.at[i], right_in.at[i], right_sent.at[i], right_got.at[i], axes, place + 1)
+
+    def to_left(i):
+        return send(left_out.at[i], left_in.at[i], left_sent.at[i], left_got.at[i], axes, place - 1)
+
+    def shares_of(seq, carry):
+        rows = pl.ds(pl.multiple_of(seq * toks, toks), toks)
+        end_local = prefix_ref[seq] - 1 - place * toks
+        inside = iota((toks, HEAD_V), 0) <= end_local
+        for head in range(HEADS):
+            i = seq * HEADS + head
+            keys = slice(head * HEAD_K, (head + 1) * HEAD_K)
+            vals = slice(head * HEAD_V, (head + 1) * HEAD_V)
+            cum = cum_ref[rows, keys]
+            query = q_ref[rows, keys]
+            grad = grad_ref[rows, vals]
+            share = tn(low(jnp.where(inside, grad, 0.0)), query)
+            acc_ref[i] = share
+
+            @pl.when(place == 0)
+            def _():
+                right_out[i] = low(share)
+                if count > 1:
+                    to_right(i).start()
+
+            later = low(jnp.where(inside, 0.0, grad))
+            for chunk in range(chunks):
+                at = slice(chunk * CHUNK, (chunk + 1) * CHUNK)
+                piece, total, middle = chunk_parts(cum, chunk)
+                local_ref[i, chunk] = tn(later[at], low(wide(query[at]) * jnp.exp(piece)))
+        return carry
+
+    lax.fori_loop(0, seqs, shares_of, 0)
+
+    def local_of(seq, carry):
+        rows = pl.ds(pl.multiple_of(seq * toks, toks), toks)
+        end_local = prefix_ref[seq] - 1 - place * toks
+        inside = iota((toks, HEAD_V), 0) <= end_local
+        inside_keys = iota((toks, HEAD_K), 0) <= end_local
+        at_end = iota((toks, HEAD_K), 0) == end_local
+        for head in range(HEADS):
+            i = seq * HEADS + head
+            keys = slice(head * HEAD_K, (head + 1) * HEAD_K)
+            vals = slice(head * HEAD_V, (head + 1) * HEAD_V)
+            cum = cum_ref[rows, keys]
+            query = wide(q_ref[rows, keys])
+            key = wide(k_ref[rows, keys])
+            value = v_ref[rows, vals]
+            grad = grad_ref[rows, vals]
+            later = low(jnp.where(inside, 0.0, grad))
+            weights, edge = prefix_weights(cum, end_local, toks)
+            prefix_state = prefix_state_ref[i]
+
+            @pl.when(place == 0)
+            def _():
+                right_in[i] = jnp.zeros((HEAD_V, HEAD_K), jnp.bfloat16)
+
+            @pl.when(place > 0)
+            def _():
+                send(right_out.at[i], right_in.at[i], right_sent.at[i], right_got.at[i], axes, place - 1).wait_recv()
+
+            acc = acc_ref[i] + wide(right_in[i])
+            narrow_acc = low(acc)
+
+            @pl.when(jnp.logical_and(place > 0, place < count - 1))
+            def _():
+                right_out[i] = narrow_acc
+                to_right(i).start()
+
+            local = jnp.zeros((HEAD_V, HEAD_K), jnp.float32)
+            starts = []
+            for chunk in reversed(range(chunks)):
+                piece, total, middle = chunk_parts(cum, chunk)
+                starts.append(local)
+                local = jnp.exp(total) * local + local_ref[i, chunk]
+            starts = starts[::-1]
+            local = local + edge * acc
+            acc_ref[i] = local
+            if count > 1:
+
+                @pl.when(place == count - 1)
+                def _():
+                    left_out[i] = low(local)
+                    to_left(i).start()
+
+            weighted = low(key * weights)
+            dk_all = weights * nn(value, narrow_acc)
+            dv_all = nt(weighted, narrow_acc)
+            dq_all = nn(low(jnp.where(inside, grad, 0.0)), prefix_state)
+            dqs, dks, dvs, dcs = [], [], [], []
+            for chunk in range(chunks):
+                at = slice(chunk * CHUNK, (chunk + 1) * CHUNK)
+                piece, total, middle = chunk_parts(cum, chunk)
+                rise = jnp.exp(piece - middle)
+                fall = jnp.exp(middle - piece)
+                q_in = low(query[at] * rise)
+                k_in = low(key[at] * fall)
+                scores = low(jnp.where(causal, nt(q_in, k_in), 0.0))
+                d_scores = low(jnp.where(causal, nt(later[at], value[at]), 0.0))
+                dq_in = nn(d_scores, k_in)
+                dk_in = tn(d_scores, q_in)
+                dq_state = jnp.exp(piece) * nn(later[at], state_ref[i, chunk])
+                to_end = jnp.exp(total - piece)
+                after = low(starts[chunk])
+                dk_state = to_end * nn(value[at], after) + dk_all[at]
+                dv = tn(scores, later[at]) + dv_all[at]
+                if chunk < chunks - 1:
+                    dv = dv + nt(low(key[at] * to_end), after)
+                dqs.append(rise * dq_in + dq_state + dq_all[at])
+                dks.append(fall * dk_in + dk_state)
+                dvs.append(dv)
+                dcs.append(
+                    wide(q_in) * dq_in
+                    - wide(k_in) * dk_in
+                    + query[at] * dq_state
+                    - key[at] * dk_state
+                )
+            dq_ref[rows, keys] = low(jnp.concatenate(dqs, axis=0))
+            dk_part[rows, keys] = jnp.concatenate(dks, axis=0)
+            dv_part[rows, vals] = jnp.concatenate(dvs, axis=0)
+            turn = jnp.sum(wide(narrow_acc) * wide(prefix_state), axis=0, keepdims=True)
+            dcum_part[rows, keys] = jnp.concatenate(dcs, axis=0) + jnp.where(at_end, turn, 0.0)
+        return carry
+
+    lax.fori_loop(0, seqs, local_of, 0)
+
+    def rest_of(seq, carry):
+        rows = pl.ds(pl.multiple_of(seq * toks, toks), toks)
+        for head in range(HEADS):
+            i = seq * HEADS + head
+            keys = slice(head * HEAD_K, (head + 1) * HEAD_K)
+            vals = slice(head * HEAD_V, (head + 1) * HEAD_V)
+            cum = cum_ref[rows, keys]
+            key = wide(k_ref[rows, keys])
+            value = v_ref[rows, vals]
+
+            @pl.when(place < count - 1)
+            def _():
+                send(left_out.at[i], left_in.at[i], left_sent.at[i], left_got.at[i], axes, place + 1).wait_recv()
+
+            @pl.when(place == count - 1)
+            def _():
+                left_in[i] = jnp.zeros((HEAD_V, HEAD_K), jnp.bfloat16)
+
+            after = left_in[i]
+            last = cum[toks - 1 :]
+
+            @pl.when(jnp.logical_and(place > 0, place < count - 1))
+            def _():
+                left_out[i] = low(jnp.exp(last) * wide(after) + acc_ref[i])
+                to_left(i).start()
+
+            to_end = jnp.exp(last - cum)
+            dk_more = to_end * nn(value, after)
+            dk_ref[rows, keys] = low(dk_part[rows, keys] + dk_more)
+            dv_ref[rows, vals] = low(dv_part[rows, vals] + nt(low(key * to_end), after))
+            carry_row = jnp.sum(wide(after) * wide(state_ref[i, chunks]), axis=0, keepdims=True)
+            dcum = dcum_part[rows, keys] - key * dk_more
+            ddecay_ref[rows, keys] = three_way(upper, dcum) + carry_row
+        return carry
+
+    lax.fori_loop(0, seqs, rest_of, 0)
+
+    def finish(i, carry):
+        @pl.when(place < count - 1)
+        def _():
+            to_right(i).wait_send()
+
+        @pl.when(place > 0)
+        def _():
+            to_left(i).wait_send()
+
+        return carry
+
+    lax.fori_loop(0, seqs * HEADS, finish, 0)
+
+
+def line_scratch(pieces):
+    block = pltpu.VMEM((pieces, HEAD_V, HEAD_K), jnp.bfloat16)
+    return [block] * 4 + [pltpu.SemaphoreType.DMA((pieces,))] * 4
+
+
+def whole_specs(count):
+    return [pl.BlockSpec(memory_space=pltpu.VMEM)] * count
+
+
+def mix_forward(axes, prefix_len, queries, keys, values, decays):
+    tokens = queries.shape[0]
+    seqs = prefix_len.shape[0]
+    pieces = seqs * HEADS
+    chunks = tokens // seqs // CHUNK
+    state = (pieces, HEAD_V, HEAD_K)
+    return pl.pallas_call(
+        partial(forward_kernel, axes),
+        out_shape=(
+            jax.ShapeDtypeStruct((tokens, VALS), jnp.float32),
+            jax.ShapeDtypeStruct((tokens, KEYS), jnp.float32),
+            jax.ShapeDtypeStruct((pieces, chunks + 1, HEAD_V, HEAD_K), jnp.bfloat16),
+            jax.ShapeDtypeStruct(state, jnp.bfloat16),
+        ),
+        in_specs=[pl.BlockSpec(memory_space=pltpu.SMEM)] + whole_specs(4),
+        out_specs=tuple(whole_specs(4)),
+        scratch_shapes=[
+            pltpu.VMEM((pieces, chunks, HEAD_V, HEAD_K), jnp.float32),
+            pltpu.VMEM(state, jnp.float32),
+            pltpu.VMEM((pieces, 8, HEAD_K), jnp.float32),
+            *line_scratch(pieces),
+        ],
+        compiler_params=pltpu.CompilerParams(
+            collective_id=1, has_side_effects=True, vmem_limit_bytes=50 * 2**20
+        ),
+        name="mix_forward",
+    )(prefix_len, queries, keys, values, decays)
+
+
+def mix_backward(axes, prefix_len, queries, keys, values, cum, states, prefix_state, grad_mixed):
+    tokens = queries.shape[0]
+    seqs = prefix_len.shape[0]
+    pieces = seqs * HEADS
+    chunks = tokens // seqs // CHUNK
+    state = (pieces, HEAD_V, HEAD_K)
+    return pl.pallas_call(
+        partial(backward_kernel, axes),
+        out_shape=(
+            jax.ShapeDtypeStruct((tokens, KEYS), jnp.bfloat16),
+            jax.ShapeDtypeStruct((tokens, KEYS), jnp.bfloat16),
+            jax.ShapeDtypeStruct((tokens, VALS), jnp.bfloat16),
+            jax.ShapeDtypeStruct((tokens, KEYS), jnp.float32),
+        ),
+        in_specs=[pl.BlockSpec(memory_space=pltpu.SMEM)] + whole_specs(7),
+        out_specs=tuple(whole_specs(4)),
+        scratch_shapes=[
+            pltpu.VMEM((pieces, chunks, HEAD_V, HEAD_K), jnp.float32),
+            pltpu.VMEM(state, jnp.float32),
+            pltpu.VMEM((tokens, KEYS), jnp.float32),
+            pltpu.VMEM((tokens, VALS), jnp.float32),
+            pltpu.VMEM((tokens, KEYS), jnp.float32),
+            *line_scratch(pieces),
+        ],
+        compiler_params=pltpu.CompilerParams(
+            collective_id=2, has_side_effects=True, vmem_limit_bytes=56 * 2**20
+        ),
+        name="mix_backward",
+    )(prefix_len, queries, keys, values, cum, states, prefix_state, grad_mixed)
 
 
 EXTRA = 128
@@ -269,7 +711,7 @@
 def local(
     names,
     sizes,
-    seq,
+    seq_axes,
     tokens,
     prefix_len,
     norm1_gain,
@@ -333,32 +775,14 @@
     lowrank = project(normed, weight_down).astype(jnp.bfloat16)
     logits = project(lowrank, weight_up) + bias_full.astype(jnp.float32)
     decays = jax.nn.log_sigmoid(logits) / 16.0
-    query_heads = queries.astype(jnp.float32).reshape(seq_count, tok_count, HEADS, HEAD_K)
-    key_heads = key_matrix.astype(jnp.float32).reshape(seq_count, tok_count, HEADS, HEAD_K)
-    value_heads = value_matrix.astype(jnp.float32).reshape(seq_count, tok_count, HEADS, HEAD_V)
-    decay_heads = decays.reshape(seq_count, tok_count, HEADS, HEAD_K)
-    seg_start = lax.axis_index(seq) * tok_count
-    places = seg_start + jnp.arange(tok_count)
-    in_prefix = (places[None, :] < prefix_len[:, None]).astype(jnp.float32)[:, :, None, None]
-    end_local = prefix_len - 1 - seg_start
-    is_owner = (end_local >= 0) & (end_local < tok_count)
-    local_out, pull_states = jax.vjp(local_states, key_heads, value_heads, decay_heads)
-    total_dev, state_dev, starts, cumulative_decay, running_totals = local_out
-    incoming = chain_forward(total_dev, state_dev, seq)
-    outputs_of = partial(local_outputs, end_local=end_local, is_owner=is_owner)
-    (causal, partial_state), pull_outputs = jax.vjp(
-        outputs_of,
-        query_heads,
-        key_heads,
-        value_heads,
-        incoming,
-        starts,
-        cumulative_decay,
-        running_totals,
-    )
-    prefix_carry_state = lax.psum(partial_state.astype(jnp.bfloat16), seq).astype(jnp.float32)
-    prefix_output = precise_summation("sthk,shkv->sthv", query_heads, prefix_carry_state)
-    mixed_heads = in_prefix * prefix_output + (1.0 - in_prefix) * causal
+    rows = seq_count * tok_count
+    flat_q = queries.reshape(rows, KEYS)
+    flat_k = key_matrix.reshape(rows, KEYS)
+    flat_v = value_matrix.reshape(rows, VALS)
+    mixed, cum, states, prefix_state = mix_forward(
+        seq_axes, prefix_len, flat_q, flat_k, flat_v, decays.reshape(rows, KEYS)
+    )
+    mixed_heads = mixed.reshape(seq_count, tok_count, HEADS, HEAD_V)
     scale_group = rms_scale(mixed_heads)
     unit_group = mixed_heads * scale_group
     normed_group = unit_group * gain_group.astype(jnp.float32)
@@ -404,24 +828,20 @@
     grad_mixed = rms_back(
         grad_normed_group * gain_group.astype(jnp.float32), unit_group, scale_group
     )
-    grad_prefix = grad_mixed * in_prefix
-    grad_causal = grad_mixed - grad_prefix
-    grad_query_pre = precise_summation("sthv,shkv->sthk", grad_prefix, prefix_carry_state)
-    prefix_term = precise_summation("sthk,sthv->shkv", query_heads, grad_prefix)
-    grad_state = lax.psum(prefix_term.astype(jnp.bfloat16), seq).astype(jnp.float32)
-    grad_q_local, grad_k_local, grad_v_local, grad_in, grad_starts, grad_cum, grad_tot = (
-        pull_outputs((grad_causal, grad_state))
-    )
-    grad_end = chain_backward(total_dev, grad_in, seq)
-    grad_total = jnp.sum(incoming * grad_end, axis=-1) * jnp.exp(total_dev)
-    grad_k_chain, grad_v_chain, grad_decay = pull_states(
-        (grad_total, grad_end, grad_starts, grad_cum, grad_tot)
-    )
-    grad_q = (
-        (grad_query_pre + grad_q_local).reshape(seq_count, tok_count, KEYS).astype(jnp.bfloat16)
-    )
-    grad_k = (grad_k_local + grad_k_chain).reshape(seq_count, tok_count, KEYS).astype(jnp.bfloat16)
-    grad_v = (grad_v_local + grad_v_chain).reshape(seq_count, tok_count, VALS).astype(jnp.bfloat16)
+    grad_q, grad_k, grad_v, grad_decay = mix_backward(
+        seq_axes,
+        prefix_len,
+        flat_q,
+        flat_k,
+        flat_v,
+        cum,
+        states,
+        prefix_state,
+        grad_mixed.reshape(rows, VALS),
+    )
+    grad_q = grad_q.reshape(seq_count, tok_count, KEYS)
+    grad_k = grad_k.reshape(seq_count, tok_count, KEYS)
+    grad_v = grad_v.reshape(seq_count, tok_count, VALS)
     grad_logits = (
         grad_decay.reshape(seq_count, tok_count, KEYS) * jax.nn.sigmoid(-logits) / 16.0
     ).astype(jnp.bfloat16)
@@ -459,7 +879,6 @@
         sizes,
     ).astype(jnp.float32)
     small = mine[:, 4096:]
-    rows = mine.shape[0]
     return (
         layer_out,
         tokens_grad,
@@ -488,7 +907,7 @@
     dp, seq = names[:cut], names[cut:]
     split = Mesh(mesh.devices.reshape(sizes), names)
     return jax.shard_map(
-        partial(local, names, sizes, seq),
+        partial(local, names, sizes, tuple(zip(seq, sizes[cut:]))),
         mesh=split,
         in_specs=(
             P(dp, seq, None),

time: 1280 us -> 921 us (0.72)
  waiting for transfers between devices: 609 us -> 348 us
  Pallas kernels: 0 us -> 201 us
  matrix products: 318 us -> 167 us
  local copies, waits for them, and re-layouts: 175 us -> 107 us
  other arithmetic: 117 us -> 72.2 us
  blocking collectives: 32.1 us -> 0 us
    pallas_call x0 -> x2, Pallas kernels: none -> 201 us  [the longest x1 135 us: mix_forward(): pl.pallas_call(partial(forward_kernel, axes), out_shape=(jax.ShapeDtypeSt...]
    all_gather x2 -> x0, waiting for transfers between devices: 134 us -> none  [the longest x1 117 us: entering(): gathered = jax.tree.map(lambda a: lax.all_gather(a, axis), part)]
    dot_general x21 -> x0, matrix products: 133 us -> none  [precise_summation(): jnp.einsum(pattern, *operands, precision=lax.Precision.HIGHEST, preferred...]
    all_gather x1, waiting for transfers between devices: 93.5 us -> 0.01 us  [local(): lax.all_gather(jnp.concatenate([ffn_gate, ffn_up, ffn_down.T], axis=1), n...]
    reshape x11 -> x1, local copies, waits for them, and re-layouts: 39 us -> 5.61 us  [local(): mixed_heads = mixed.reshape(seq_count, tok_count, HEADS, HEAD_V)]
    all_gather x2 -> x0, blocking collectives: 32.1 us -> none  [the longest x1 16.9 us: carried_in(): lax.all_gather(a.astype(kind), axis)]
    psum x2 -> x0, waiting for transfers between devices: 28.6 us -> none  [the longest x1 28.6 us: local(): lax.psum(prefix_term.astype(jnp.bfloat16), seq).astype(jnp.float32)]
    add x8 -> x0, other arithmetic: 21.9 us -> none  [the longest x3 10.8 us: chain_combine(): jnp.exp(later[0])[..., None] * earlier[1] + later[1]]
  transfers between devices with their start and end apart: 10 -> 6, of which waited for: 8 -> 4; matrix products, arithmetic and copies ran while one was open for 18% -> 15% of each run, Pallas kernels for 0% -> 15%
where the time goes in v2:
time: 921 us; the launch traced here: 911 us
  waiting for transfers between devices  348 us (38%)
  Pallas kernels  201 us (22%)
  matrix products  167 us (18%)
  local copies, waits for them, and re-layouts  107 us (12%)
  other arithmetic  72.2 us (8%)
  between operations  14.8 us (2%)
    reduce_scatter x2, waiting for transfers between devices, reduce_to_owner(): return lax.psum_scatter(total, rest, scatter_dimension=0, tiled=True)  263 us
    pallas_call x1, Pallas kernels, mix_forward(): pl.pallas_call(partial(forward_kernel, axes), out_shape=(jax.ShapeDtypeSt...  135 us
    all_gather x1, waiting for transfers between devices, local(): lax.all_gather(pack_mixer(norm1_gain, norm2_gain, query_weight, key_weigh...  77.2 us
    pallas_call x1, Pallas kernels, mix_backward(): pl.pallas_call(partial(backward_kernel, axes), out_shape=(jax.ShapeDtypeS...  66.3 us
    dot_general x10, matrix products, project(): jnp.einsum('std,de->ste', inputs, weight, preferred_element_type=jnp.floa...  63 us
    dot_general x10, matrix products, back_project(): jnp.einsum('ste,de->std', gradient, weight, preferred_element_type=jnp.fl...  57.9 us
    dot_general x10, matrix products, weight_grad(): jnp.einsum('std,ste->de', inputs, gradient, preferred_element_type=jnp.fl...  46.4 us
    unnamed x114, local copies, waits for them, and re-layouts  24.7 us
  transfers between devices with their start and end apart: 6, of which 4 were waited for; matrix products, arithmetic and copies ran while one was open for 15% of the time, Pallas kernels for 15%

profile of v2, /device:TPU:0, one launch (start us, length us, event | category | flops | bytes accessed | tf_op | source)
XLA Modules:
  0.0 911.0 jit_solution(18246620338153428270)
XLA Ops:
  36.5 77.2 %all-gather.3.cloned.1.call-done = bf16[1024,4224]{1,0:T(8,128)(2,1)} async-done(((bf16[32,4224]{1,0:T(8,128)(2,1)}), bf16[1024,4224]{1,0:T(8,128)(2,1)}) %all-gather.3.cloned.1.call-update) | async-done | bytes 8650768 | tf_op jit(solution)/shard_map/all_gather | solution.py:734
  129.1 5.7 convolution_convert_fusion
  134.8 135.2 %mix_forward.1 = (f32[1024,1024]{1,0:T(8,128)}, f32[1024,512]{1,0:T(8,128)}, bf16[16,3,256,128]{3,2,1,0:T(8,128)(2,1)}, bf16[16,256,128]{2,1,0:T(8,128)(2,1)S(1)}) custom-call(s32[4]{0:T(128)S(1)} %copy-done.3, bf16[1024,512]{1,0:T(8,128)(2,1)S(1)} %bitcast.207, bf16[1024,512]{1,0:T(8,128)(2,1)S(1)} %bitcast.209, bf16[1024,1024]{1,0:T(8,128)(2,1)} %bitcast.218, ...), custom_call_target="tpu_custom_call" | custom-call | tf_op jit(solution)/shard_map/mix_forward/pallas_call | solution.py:572
  270.9 5.6 reshape.394
  282.5 5.8 mul.229
  288.3 5.3 copy.142
  293.8 7.1 multiply_convert_fusion.3
  309.5 12.4 %fusion.9 = f32[4,256,2816]{2,1,0:T(8,128)} fusion(bf16[4,256,1024]{2,1,0:T(8,128)(2,1)} %multiply_convert_fusion.2, bf16[1024,8448]{1,0:T(8,128)(2,1)} %all-gather.5.cloned.1.call-done), kind=kOutput, calls=%fused_computation.26 | convolution fusion | flops 5905580032 | bytes 19398656 | tf_op jit(solution)/shard_map/std,de->ste/dot_general | solution.py:25
  321.9 11.4 %fusion.11 = f32[4,256,2816]{2,1,0:T(8,128)} fusion(bf16[4,256,1024]{2,1,0:T(8,128)(2,1)S(1)} %copy-done.14, bf16[1024,8448]{1,0:T(8,128)(2,1)} %all-gather.5.cloned.1.call-done), kind=kOutput, calls=%fused_computation.28 | convolution fusion | flops 5905580032 | bytes 19398656 | tf_op jit(solution)/shard_map/std,de->ste/dot_general | solution.py:25
  333.4 22.3 %fusion.2 = (bf16[4,256,2816]{2,1,0:T(8,128)(2,1)}, bf16[4,256,2816]{2,1,0:T(8,128)(2,1)}, bf16[4,256,2816]{2,1,0:T(8,128)(2,1)}) fusion(f32[4,256,2816]{2,1,0:T(8,128)} %fusion.9, f32[4,256,2816]{2,1,0:T(8,128)} %fusion.11, bf16[4,256,1024]{2,1,0:T(8,128)(2,1)} %param.45, bf16[1024,8448]{1,0:T(8,128)(2,1)} %all-gather.5.cloned.1.call-done), kind=kOutput, calls=%fused_computation.8 | convolution fusion | flops 5948833792 | bytes 48234496 | tf_op jit(solution)/shard_map/ste,de->std/dot_general | solution.py:29
  355.7 10.2 %fusion.8 = f32[4,256,1024]{2,1,0:T(8,128)S(1)} fusion(bf16[4,256,2816]{2,1,0:T(8,128)(2,1)} %get-tuple-element.167, bf16[1024,8448]{1,0:T(8,128)(2,1)} %all-gather.5.cloned.1.call-done), kind=kOutput, calls=%fused_computation.25 | convolution fusion | flops 5905580032 | bytes 15728640 | tf_op jit(solution)/shard_map/ste,de->std/dot_general | solution.py:29
  365.9 9.1 %multiply_reduce_fusion.1 = (bf16[1024]{0:T(1024)(128)(2,1)S(1)}, f32[4,256]{1,0:T(4,128)S(1)}, f32[4,256,1024]{2,1,0:T(8,128)S(1)}) fusion(f32[4,256,1024]{2,1,0:T(8,128)S(1)} %copy-done.7, f32[4,256]{1,0:T(4,128)S(1)} %add_rsqrt_fusion.1, f32[1024]{0:T(1024)S(1)} %get-tuple-element.152, f32[4,256,1024]{2,1,0:T(8,128)S(1)} %fusion.8, ...), kind=kOutput, calls=%fused_computation.47 | convolution fusion | flops 5912918016 | bytes 24131584 | tf_op jit(solution)/shard_map/ste,de->std/dot_general | solution.py:29
  382.4 7.5 multiply_reduce_fusion
  389.9 5.7 mul.260
  395.5 5.7 multiply_reduce_fusion.2
  407.7 7.5 fusion.22.grad_ref
  415.3 66.3 %mix_backward.1 = (bf16[1024,512]{1,0:T(8,128)(2,1)}, bf16[1024,512]{1,0:T(8,128)(2,1)}, bf16[1024,1024]{1,0:T(8,128)(2,1)}, f32[1024,512]{1,0:T(8,128)}) custom-call(s32[4]{0:T(128)} %prefix_ref.3, bf16[1024,512]{1,0:T(8,128)(2,1)} %bitcast.208, bf16[1024,512]{1,0:T(8,128)(2,1)} %bitcast.210, bf16[1024,1024]{1,0:T(8,128)(2,1)} %bitcast.219, ...), custom_call_target="tpu_custom_call" | custom-call | tf_op jit(solution)/shard_map/mix_backward/pallas_call | solution.py:601
  484.7 11.3 %bitcast_convert_fusion.1 = bf16[1024,2816]{1,0:T(8,128)(2,1)} fusion(bf16[4,256,1024]{2,1,0:T(8,128)(2,1)S(1)} %copy-done.15, bf16[4,256,2816]{2,1,0:T(8,128)(2,1)} %get-tuple-element.166), kind=kOutput, calls=%fused_computation.2 | convolution fusion | flops 5908463616 | bytes 13631488 | tf_op jit(solution)/shard_map/std,ste->de/dot_general | solution.py:33
  516.9 6.3 copy.101
  537.8 13.9 %concatenate.60 = bf16[4,2,128,4224]{3,2,1,0:T(8,128)(2,1)} concatenate(bf16[4,2,128,512]{3,2,1,0:T(8,128)(2,1)} %bitcast_convert_fusion.7, bf16[4,2,128,512]{3,2,1,0:T(8,128)(2,1)} %bitcast_convert_fusion.6, bf16[4,2,128,1024]{3,2,1,0:T(8,128)(2,1)} %bitcast_convert_fusion.5, bf16[4,2,128,1024]{3,2,1,0:T(8,128)(2,1)} %bitcast.226, bf16[4,2,128,1024]{3,2,1,0:T(8,128)(2,1)} %bitcast.225, ...), dimensions={3} | concatenate | bytes 17301504 | tf_op jit(solution)/shard_map/concatenate | solution.py:867
  551.8 4.9 dynamic-slice_bitcast_fusion.1
  556.7 9.4 %bitcast_convert_fusion = bf16[2816,1024]{0,1:T(8,128)(2,1)S(1)} fusion(bf16[4,256,2816]{2,1,0:T(8,128)(2,1)} %get-tuple-element.168, bf16[4,256,1024]{2,1,0:T(8,128)(2,1)S(1)} %copy-done.20), kind=kOutput, calls=%fused_computation.1 | convolution fusion | flops 5908463616 | bytes 13631488 | tf_op jit(solution)/shard_map/std,ste->de/dot_general | solution.py:33
  566.1 6.9 bitcast_convert_fusion.2
  573.1 7.0 pad_maximum_fusion
  580.1 7.4 dynamic-slice_bitcast_fusion
  587.9 6.0 bitcast_add_fusion.1
  593.9 7.5 collective-permute-done.1
  601.4 9.2 %bitcast_add_fusion = bf16[4,128,8448]{2,1,0:T(8,128)(2,1)} fusion(bf16[4,128,8448]{2,1,0:T(8,128)(2,1)} %collective-permute-done.1, bf16[4,2,128,8448]{3,2,1,0:T(8,128)(2,1)} %pad_maximum_fusion, s32[]{:T(128)S(6)} %select_n.16), kind=kLoop, calls=%fused_computation.12 | loop fusion | flops 4325376 | bytes 25952260 | tf_op jit(solution)/shard_map/add | solution.py:706
  611.3 5.7 fusion.18
  617.7 10.9 %add_convert_fusion = bf16[4,256,1024]{2,1,0:T(8,128)(2,1)} fusion(f32[4,256,1024]{2,1,0:T(8,128)S(1)} %copy-done.8, bf16[4,256,2816]{2,1,0:T(8,128)(2,1)} %get-tuple-element.168, bf16[1024,8448]{1,0:T(8,128)(2,1)} %all-gather.5.cloned.1.call-done), kind=kOutput, calls=%fused_computation.53 | convolution fusion | flops 5907677184 | bytes 17825792 | tf_op jit(solution)/shard_map/std,de->ste/dot_general | solution.py:25
  628.6 100.8 %reduce-scatter.3.cloned.1.call-done = bf16[32,4224]{1,0:T(8,128)(2,1)} async-done(((bf16[512,4224]{1,0:T(8,128)(2,1)}), bf16[32,4224]{1,0:T(8,128)(2,1)}) %reduce-scatter.3.cloned.1.call-update) | async-done | bytes 270352 | tf_op jit(solution)/shard_map/reduce_scatter | solution.py:708
  738.5 162.0 %reduce-scatter.5.cloned.1.call-done = bf16[32,8448]{1,0:T(8,128)(2,1)} async-done(((bf16[512,8448]{1,0:T(8,128)(2,1)}), bf16[32,8448]{1,0:T(8,128)(2,1)}) %reduce-scatter.5.cloned.1.call-update) | async-done | bytes 540688 | tf_op jit(solution)/shard_map/reduce_scatter | solution.py:708
  (225 shorter events, 127.1 us)
Async XLA Ops:
  7.2 111.2 %copy-start.5 = (bf16[4,256,1024]{2,1,0:T(8,128)(2,1)S(1)}, bf16[4,256,1024]{2,1,0:T(8,128)(2,1)}, u32[]{:S(2)}) copy-start(bf16[4,256,1024]{2,1,0:T(8,128)(2,1)} %param.29) | copy-start | bytes 6291460
  7.2 106.5 %all-gather.3.cloned.1.call-start = ((), (), s32[]{:S(2)}) async-start(), calls=%async_computation.2 | async-start | bytes 8921088 | tf_op jit(solution)/shard_map/all_gather | solution.py:734
  32.3 277.2 %all-gather.5.cloned.1.call-start = ((), (), s32[]{:S(2)}) async-start(), calls=%async_computation.3 | async-start | bytes 17842176 | tf_op jit(solution)/shard_map/all_gather | solution.py:752
  34.3 695.1 %reduce-scatter.3.cloned.1.call-start = ((), (), s32[]{:S(2)}) async-start(), calls=%async_computation.4 | async-start | bytes 4595712 | tf_op jit(solution)/shard_map/reduce_scatter | solution.py:708
  36.5 472.7 %copy-start.28 = (f32[4,256]{1,0:T(4,128)}, f32[4,256]{1,0:T(4,128)S(1)}, u32[]{:S(2)}) copy-start(f32[4,256]{1,0:T(4,128)S(1)} %add_rsqrt_fusion.2) | copy-start | bytes 12292
  115.6 7.9 copy-start.33
  116.9 6.6 copy-start.23
  118.4 390.8 %copy-start.26 = (f32[1024]{0:T(1024)}, f32[1024]{0:T(1024)S(1)}, u32[]{:S(2)}) copy-start(f32[1024]{0:T(1024)S(1)} %get-tuple-element.153) | copy-start | bytes 12292
  120.1 6.0 copy-start.30
  126.1 8.6 copy-start
  129.0 5.7 copy-start.1
  129.1 5.7 copy-start.3
  309.5 12.4 %copy-start.14 = (bf16[4,256,1024]{2,1,0:T(8,128)(2,1)S(1)}, bf16[4,256,1024]{2,1,0:T(8,128)(2,1)}, u32[]{:S(2)}) copy-start(bf16[4,256,1024]{2,1,0:T(8,128)(2,1)} %multiply_convert_fusion.2) | copy-start | bytes 6291460
  355.7 10.2 %copy-start.7 = (f32[4,256,1024]{2,1,0:T(8,128)S(1)}, f32[4,256,1024]{2,1,0:T(8,128)}, u32[]{:S(2)}) copy-start(f32[4,256,1024]{2,1,0:T(8,128)} %copy-done.6) | copy-start | bytes 12582916
  355.7 10.2 %copy-start.42 = (bf16[4,256,2816]{2,1,0:T(8,128)(2,1)S(1)}, bf16[4,256,2816]{2,1,0:T(8,128)(2,1)}, u32[]{:S(2)}) copy-start(bf16[4,256,2816]{2,1,0:T(8,128)(2,1)} %get-tuple-element.166) | copy-start | bytes 17301508
  365.9 9.2 %copy-start.19 = (bf16[4,256,1024]{2,1,0:T(8,128)(2,1)S(1)}, bf16[4,256,1024]{2,1,0:T(8,128)(2,1)}, u32[]{:S(2)}) copy-start(bf16[4,256,1024]{2,1,0:T(8,128)(2,1)} %param.45) | copy-start | bytes 6291460
  376.7 5.7 copy-start.40
  415.3 66.3 %copy-start.17 = (f32[4,256,512]{2,1,0:T(8,128)S(1)}, f32[4,256,512]{2,1,0:T(8,128)}, u32[]{:S(2)}) copy-start(f32[4,256,512]{2,1,0:T(8,128)} %get-tuple-element.183) | copy-start | bytes 6291460
  415.3 66.4 %copy-start.34 = (f32[512]{0:T(512)S(1)}, f32[512]{0:T(512)}, u32[]{:S(2)}) copy-start(f32[512]{0:T(512)} %copy-done.33) | copy-start | bytes 6148
  481.6 19.0 %slice-start.2 = ((s8[8650752]{0:T(1024)(128)(4,1)}), s8[4194304]{0:T(1024)(128)(4,1)S(1)}, s32[]{:S(2)}) async-start(s8[8650752]{0:T(1024)(128)(4,1)} %bitcast.228), calls=%async_computation.8 | async-start | bytes 8388608
  484.7 11.3 %copy-start.41 = (bf16[4,256,1024]{2,1,0:T(8,128)(2,1)S(1)}, bf16[4,256,1024]{2,1,0:T(8,128)(2,1)}, u32[]{:S(2)}) copy-start(bf16[4,256,1024]{2,1,0:T(8,128)(2,1)} %get-tuple-element.169) | copy-start | bytes 6291460
  484.7 15.9 %slice-start.3 = ((s8[8650752]{0:T(1024)(128)(4,1)}), s8[4194304]{0:T(1024)(128)(4,1)S(1)}, s32[]{:S(2)}) async-start(s8[8650752]{0:T(1024)(128)(4,1)} %bitcast.228), calls=%async_computation.9 | async-start | bytes 8388608
  484.7 15.9 %slice-start.4 = ((s8[8650752]{0:T(1024)(128)(4,1)}), s8[262144]{0:T(1024)(128)(4,1)S(1)}, s32[]{:S(2)}) async-start(s8[8650752]{0:T(1024)(128)(4,1)} %bitcast.228), calls=%async_computation.10 | async-start | bytes 524288
  551.8 14.3 %slice-start.5 = ((s8[5767168]{0:T(1024)(128)(4,1)}), s8[4194304]{0:T(1024)(128)(4,1)S(1)}, s32[]{:S(2)}) async-start(s8[5767168]{0:T(1024)(128)(4,1)} %bitcast.250), calls=%async_computation.11 | async-start | bytes 8388608
  551.8 21.3 %slice-start = ((s8[5767168]{0:T(1024)(128)(4,1)}), s8[1572864]{0:T(1024)(128)(4,1)S(1)}, s32[]{:S(2)}) async-start(s8[5767168]{0:T(1024)(128)(4,1)} %bitcast.220), calls=%async_computation.6 | async-start | bytes 3145728
  556.7 31.2 %collective-permute-start = (bf16[4,128,4224]{2,1,0:T(8,128)(2,1)}, bf16[4,128,4224]{2,1,0:T(8,128)(2,1)}, u32[]{:S(2)}, u32[]{:S(2)}) collective-permute-start(bf16[4,128,4224]{2,1,0:T(8,128)(2,1)} %dynamic-slice_bitcast_fusion.1), channel_id=1, source_target_pairs={{0,4},{4,0},{1,5},{5,1},{2,6},{6,2},{3,7},{7,3},{8,12},{12,8},{9,1... | collective-permute-start | bytes 12976136 | tf_op jit(solution)/shard_map/ppermute | solution.py:705
  556.7 9.4 %copy-start.16 = (bf16[4,256,1024]{2,1,0:T(8,128)(2,1)S(1)}, bf16[4,256,1024]{2,1,0:T(8,128)(2,1)}, u32[]{:S(2)}) copy-start(bf16[4,256,1024]{2,1,0:T(8,128)(2,1)} %multiply_convert_fusion.2) | copy-start | bytes 6291460
  556.7 9.4 %slice-start.6 = ((s8[5767168]{0:T(1024)(128)(4,1)}), s8[1572864]{0:T(1024)(128)(4,1)S(1)}, s32[]{:S(2)}) async-start(s8[5767168]{0:T(1024)(128)(4,1)} %bitcast.250), calls=%async_computation.12 | async-start | bytes 3145728
  556.7 16.4 %slice-start.1 = ((s8[5767168]{0:T(1024)(128)(4,1)}), s8[4194304]{0:T(1024)(128)(4,1)S(1)}, s32[]{:S(2)}) async-start(s8[5767168]{0:T(1024)(128)(4,1)} %bitcast.220), calls=%async_computation.7 | async-start | bytes 8388608
  587.5 13.9 %collective-permute-start.1 = (bf16[4,128,8448]{2,1,0:T(8,128)(2,1)}, bf16[4,128,8448]{2,1,0:T(8,128)(2,1)}, u32[]{:S(2)}, u32[]{:S(2)}) collective-permute-start(bf16[4,128,8448]{2,1,0:T(8,128)(2,1)} %dynamic-slice_bitcast_fusion), channel_id=1, source_target_pairs={{0,4},{4,0},{1,5},{5,1},{2,6},{6,2},{3,7},{7,3},{8,12},{12,8},{9,1... | collective-permute-start | bytes 25952264 | tf_op jit(solution)/shard_map/ppermute | solution.py:705
  593.9 306.6 %reduce-scatter.5.cloned.1.call-start = ((), (), s32[]{:S(2)}) async-start(), calls=%async_computation.5 | async-start | bytes 9191424 | tf_op jit(solution)/shard_map/reduce_scatter | solution.py:708
  611.3 6.4 copy-start.8
  (24 other events, 68.7 us)
Sparse Core Ops, SparseCore 0:
  32.4 81.2 all-gather.2
  116.5 148.4 all-gather.4
  594.0 135.3 reduce-scatter.2
  735.9 164.5 reduce-scatter.4

commit v3 on v2

--- a/solution.py
+++ b/solution.py
@@ -349,9 +349,7 @@
     state_ref,
     prefix_state_ref,
     grad_ref,
-    dq_ref,
-    dk_ref,
-    dv_ref,
+    dqkv_ref,
     ddecay_ref,
     local_ref,
     acc_ref,
@@ -494,7 +492,7 @@
                     + query[at] * dq_state
                     - key[at] * dk_state
                 )
-            dq_ref[rows, keys] = low(jnp.concatenate(dqs, axis=0))
+            dqkv_ref[rows, keys] = low(jnp.concatenate(dqs, axis=0))
             dk_part[rows, keys] = jnp.concatenate(dks, axis=0)
             dv_part[rows, vals] = jnp.concatenate(dvs, axis=0)
             turn = jnp.sum(wide(narrow_acc) * wide(prefix_state), axis=0, keepdims=True)
@@ -531,8 +529,12 @@
 
             to_end = jnp.exp(last - cum)
             dk_more = to_end * nn(value, after)
-            dk_ref[rows, keys] = low(dk_part[rows, keys] + dk_more)
-            dv_ref[rows, vals] = low(dv_part[rows, vals] + nt(low(key * to_end), after))
+            dqkv_ref[rows, slice(KEYS + keys.start, KEYS + keys.stop)] = low(
+                dk_part[rows, keys] + dk_more
+            )
+            dqkv_ref[rows, slice(2 * KEYS + vals.start, 2 * KEYS + vals.stop)] = low(
+                dv_part[rows, vals] + nt(low(key * to_end), after)
+            )
             carry_row = jnp.sum(wide(after) * wide(state_ref[i, chunks]), axis=0, keepdims=True)
             dcum = dcum_part[rows, keys] - key * dk_more
             ddecay_ref[rows, keys] = three_way(upper, dcum) + carry_row
@@ -588,6 +590,9 @@
         compiler_params=pltpu.CompilerParams(
             collective_id=1, has_side_effects=True, vmem_limit_bytes=50 * 2**20
         ),
+        cost_estimate=pl.CostEstimate(
+            flops=60_000_000_000, bytes_accessed=220_000_000, transcendentals=0
+        ),
         name="mix_forward",
     )(prefix_len, queries, keys, values, decays)
 
@@ -601,13 +606,11 @@
     return pl.pallas_call(
         partial(backward_kernel, axes),
         out_shape=(
-            jax.ShapeDtypeStruct((tokens, KEYS), jnp.bfloat16),
-            jax.ShapeDtypeStruct((tokens, KEYS), jnp.bfloat16),
-            jax.ShapeDtypeStruct((tokens, VALS), jnp.bfloat16),
+            jax.ShapeDtypeStruct((tokens, 2 * KEYS + VALS), jnp.bfloat16),
             jax.ShapeDtypeStruct((tokens, KEYS), jnp.float32),
         ),
         in_specs=[pl.BlockSpec(memory_space=pltpu.SMEM)] + whole_specs(7),
-        out_specs=tuple(whole_specs(4)),
+        out_specs=tuple(whole_specs(2)),
         scratch_shapes=[
             pltpu.VMEM((pieces, chunks, HEAD_V, HEAD_K), jnp.float32),
             pltpu.VMEM(state, jnp.float32),
@@ -618,6 +621,9 @@
         ],
         compiler_params=pltpu.CompilerParams(
             collective_id=2, has_side_effects=True, vmem_limit_bytes=56 * 2**20
+        ),
+        cost_estimate=pl.CostEstimate(
+            flops=60_000_000_000, bytes_accessed=220_000_000, transcendentals=0
         ),
         name="mix_backward",
     )(prefix_len, queries, keys, values, cum, states, prefix_state, grad_mixed)
@@ -690,22 +696,210 @@
     return jnp.concatenate(pieces, axis=1)
 
 
-def reduce_to_owner(total, names, sizes):
-    rows = total.shape[0]
-    width = total.shape[1]
-    devices = int(np.prod(sizes))
-    if "core" in names:
-        at = names.index("core")
-        before = int(np.prod(sizes[:at], initial=1))
-        after = rows // before // sizes[at]
-        shaped = total.reshape(before, sizes[at], after, width)
-        core = lax.axis_index("core")
-        kept = lax.dynamic_index_in_dim(shaped, core, 1, False)
-        given = lax.dynamic_index_in_dim(shaped, 1 - core, 1, False)
-        taken = lax.ppermute(given, "core", [(0, 1), (1, 0)])
-        total = (kept + taken).reshape(rows // sizes[at], width)
-    rest = tuple(n for n in names if n != "core")
-    return lax.psum_scatter(total, rest, scatter_dimension=0, tiled=True)
+def core_halves(rows, names, sizes):
+    width = rows.shape[1]
+    at = names.index("core")
+    before = int(np.prod(sizes[:at], initial=1))
+    after = width // before // sizes[at]
+    core = lax.axis_index("core")
+
+    def half(which):
+        return jnp.concatenate(
+            [
+                lax.dynamic_slice_in_dim(rows, (2 * i + which) * after, after, 1)
+                for i in range(before)
+            ],
+            axis=1,
+        )
+
+    return half(core), half(1 - core)
+
+
+def swap_cores(values):
+    return lax.ppermute(values, "core", [(0, 1), (1, 0)])
+
+
+def pair_sum(halves, gradient):
+    mine, other = halves
+    taken = swap_cores(flat_grad(other, gradient).astype(jnp.bfloat16))
+    return (flat_grad(mine, gradient) + taken.astype(jnp.float32)).astype(jnp.bfloat16)
+
+
+def flat_grad(inputs, gradient):
+    return jnp.einsum("td,te->de", inputs, gradient, preferred_element_type=jnp.float32)
+
+
+def by_chip(values, names, sizes):
+    chips = tuple(size for name, size in zip(names, sizes) if name != "core")
+    return values.reshape(*chips, -1, values.shape[-1])
+
+
+def pass_along(values, left, name):
+    at = left.index(name)
+    size = values.shape[at]
+    own = lax.axis_index(name)
+    arrived = []
+    for shift in range(1, size):
+        given = lax.dynamic_index_in_dim(values, lax.rem(own + shift, size), at, False)
+        arrived.append(
+            lax.ppermute(given, name, [(i, (i + shift) % size) for i in range(size)])
+        )
+    return arrived
+
+
+def take_in(values, arrived, left, name):
+    at = left.index(name)
+    total = lax.dynamic_index_in_dim(values, lax.axis_index(name), at, False).astype(jnp.float32)
+    for term in arrived:
+        total = total + term.astype(jnp.float32)
+    return total, [other for other in left if other != name]
+
+
+def reduce_kernel(plan, *refs):
+    inputs, jobs, sizes, slots = plan
+    count = len(jobs)
+    in_refs = refs[:inputs]
+    outputs = max(job[4] for job in jobs) + 1
+    out_refs = refs[inputs : inputs + outputs]
+    scratch = refs[inputs + outputs :]
+    send_sem, recv_sem = scratch[-2:]
+    scratch = list(scratch[:-2])
+
+    reached = sorted({name for job in jobs for name in job[3]})
+    barrier = pltpu.get_barrier_semaphore()
+    peers = 0
+    for name in reached:
+        for shift in range(1, sizes[name]):
+            peer = lax.rem(lax.axis_index(name) + shift, sizes[name])
+            pl.semaphore_signal(barrier, inc=1, device_id={name: peer}, device_id_type=MESH)
+            peers += 1
+    pl.semaphore_wait(barrier, peers)
+
+    class Job:
+        pass
+
+    work = []
+    slot = 0
+    for which, columns, axes, order, out, out_columns in jobs:
+        job = Job()
+        job.left = list(axes)
+        job.order = order
+        job.out = out_refs[out]
+        job.out_columns = slice(*out_columns)
+        job.source = in_refs[which]
+        job.columns = slice(*columns)
+        job.got = [scratch.pop(0) for _ in order]
+        job.kept = [scratch.pop(0) for _ in order[:-1]]
+        job.slots = []
+        for name in order:
+            job.slots.append(slot)
+            slot += sizes[name] - 1
+        work.append(job)
+
+    def part(job, index):
+        at = job.left.index(job.order[job.step])
+        lead = [slice(None)] * len(job.left)
+        lead[at] = index
+        return job.source.at[(*lead, slice(None), job.columns)]
+
+    def copies(job):
+        name = job.order[job.step]
+        own = lax.axis_index(name)
+        for shift in range(1, sizes[name]):
+            peer = lax.rem(own + shift, sizes[name])
+            at = job.slots[job.step] + shift - 1
+            yield pltpu.make_async_remote_copy(
+                src_ref=part(job, peer),
+                dst_ref=job.got[job.step].at[shift - 1],
+                send_sem=send_sem.at[at],
+                recv_sem=recv_sem.at[at],
+                device_id={name: peer},
+                device_id_type=MESH,
+            )
+
+    def start(job):
+        for copy in copies(job):
+            copy.start()
+
+    def add(job):
+        name = job.order[job.step]
+        at = job.left.index(name)
+        own = lax.axis_index(name)
+        rest = [n for n in job.left if n != name]
+        last = job.step == len(job.order) - 1
+        total = int(np.prod([sizes[n] for n in rest], initial=1))
+        got = job.got[job.step]
+        for copy in copies(job):
+            copy.wait()
+        source, columns, step = job.source, job.columns, job.step
+
+        def one(i, carry):
+            index = []
+            for n in reversed(rest):
+                index.insert(0, lax.rem(i, sizes[n]))
+                i = lax.div(i, sizes[n])
+            lead = list(index)
+            lead.insert(at, own)
+            value = source[(*lead, slice(None), columns)].astype(jnp.float32)
+            for shift in range(1, sizes[name]):
+                value = value + got[(shift - 1, *index)].astype(jnp.float32)
+            if last:
+                job.out[:, job.out_columns] = value
+            else:
+                job.kept[step][tuple(index)] = value.astype(jnp.bfloat16)
+            return carry
+
+        if total == 1:
+            one(jnp.int32(0), 0)
+        else:
+            lax.fori_loop(0, total, one, 0)
+        job.left = rest
+        if not last:
+            job.source = job.kept[step]
+            job.columns = slice(None)
+            job.step += 1
+            start(job)
+
+    for job in work:
+        job.step = 0
+        start(job)
+    for step in range(max(len(job.order) for job in work)):
+        for job in work:
+            if len(job.order) > step:
+                add(job)
+
+
+def reduce_rest(arrays, jobs, sizes, rows, widths, collective):
+    scratch = []
+    slots = 0
+    for which, (begin, end), axes, order, out, out_columns in jobs:
+        left = list(axes)
+        kept = []
+        got = []
+        for name in order:
+            left.remove(name)
+            shape = tuple(sizes[n] for n in left)
+            got.append(pltpu.VMEM((sizes[name] - 1, *shape, rows, end - begin), jnp.bfloat16))
+            kept.append(pltpu.VMEM((*shape, rows, end - begin), jnp.bfloat16))
+            slots += sizes[name] - 1
+        scratch += got + kept[:-1]
+    scratch += [pltpu.SemaphoreType.DMA((slots,))] * 2
+    return pl.pallas_call(
+        partial(reduce_kernel, (len(arrays), jobs, sizes, slots)),
+        out_shape=tuple(jax.ShapeDtypeStruct((rows, width), jnp.float32) for width in widths),
+        in_specs=whole_specs(len(arrays)),
+        out_specs=tuple(whole_specs(len(widths))),
+        scratch_shapes=scratch,
+        compiler_params=pltpu.CompilerParams(
+            collective_id=collective, has_side_effects=True, vmem_limit_bytes=40 * 2**20
+        ),
+        name="reduce_rest",
+    )(*arrays)
+
+
+def chip_orders(names):
+    first, second, last = [name for name in names if name != "core"]
+    return (first, second, last), (second, last, first), (last, first, second)
 
 
 def local(
@@ -803,23 +997,24 @@
     layer_out = (resid_mid + ffn_out).astype(jnp.bfloat16)
     grad_out = out_grad.astype(jnp.float32)
     grad_hidden = back_project(out_grad, weight_lower)
-    lower_grad = weight_grad(out_grad, hidden)
     grad_gate = (grad_hidden * up_part * silu_slope(gate_part)).astype(jnp.bfloat16)
     grad_up = (grad_hidden * gate_act).astype(jnp.bfloat16)
-    gate_w_grad = weight_grad(normed_two, grad_gate)
-    up_w_grad = weight_grad(normed_two, grad_up)
     grad_normed_two = back_project(grad_gate, weight_gate) + back_project(grad_up, weight_upper)
     gain_two_grad = jnp.sum(grad_normed_two * unit_two, axis=(0, 1))
     grad_mid = grad_out + rms_back(
         grad_normed_two * gain_two.astype(jnp.float32), unit_two, scale_two
     )
-    ffn_mine = reduce_to_owner(
-        jnp.concatenate([gate_w_grad, up_w_grad, lower_grad], axis=1).astype(jnp.bfloat16),
-        names,
-        sizes,
-    ).astype(jnp.float32)
     grad_branch = grad_mid.astype(jnp.bfloat16)
-    out_w_grad = weight_grad(gated_rows, grad_branch)
+    normed_halves = core_halves(normed.reshape(rows, -1), names, sizes)
+    two_halves = core_halves(normed_two.reshape(rows, -1), names, sizes)
+    gate_sum = pair_sum(two_halves, grad_gate.reshape(rows, FF))
+    up_sum = pair_sum(two_halves, grad_up.reshape(rows, FF))
+    down_sum = pair_sum(
+        core_halves(out_grad.reshape(rows, -1), names, sizes), hidden.reshape(rows, FF)
+    )
+    out_sum = pair_sum(
+        core_halves(gated_rows.reshape(rows, -1), names, sizes), grad_branch.reshape(rows, -1)
+    )
     grad_gated = back_project(grad_branch, weight_o).reshape(seq_count, tok_count, HEADS, HEAD_V)
     grad_normed_group = grad_gated * swish_gate
     grad_swish = (grad_gated * normed_group).reshape(seq_count, tok_count, VALS)
@@ -828,7 +1023,19 @@
     grad_mixed = rms_back(
         grad_normed_group * gain_group.astype(jnp.float32), unit_group, scale_group
     )
-    grad_q, grad_k, grad_v, grad_decay = mix_backward(
+    gate_out_sum = pair_sum(normed_halves, grad_gate_out.reshape(rows, VALS))
+    groups = (
+        jnp.concatenate([gate_sum, out_sum, down_sum[:, 2048:2432]], axis=1),
+        jnp.concatenate([up_sum, gate_out_sum, down_sum[:, 2432:]], axis=1),
+        down_sum[:, :2048],
+    )
+    groups, grad_mixed = lax.optimization_barrier((groups, grad_mixed))
+    chips = [name for name in names if name != "core"]
+    orders = chip_orders(names)
+    lefts = [chips] * 3
+    groups = [by_chip(group, names, sizes) for group in groups]
+    arrived = [pass_along(g, left, order[0]) for g, left, order in zip(groups, lefts, orders)]
+    grad_qkv, grad_decay = mix_backward(
         seq_axes,
         prefix_len,
         flat_q,
@@ -839,9 +1046,23 @@
         prefix_state,
         grad_mixed.reshape(rows, VALS),
     )
-    grad_q = grad_q.reshape(seq_count, tok_count, KEYS)
-    grad_k = grad_k.reshape(seq_count, tok_count, KEYS)
-    grad_v = grad_v.reshape(seq_count, tok_count, VALS)
+    arrived, grad_qkv, grad_decay = lax.optimization_barrier((arrived, grad_qkv, grad_decay))
+
+    def next_axis(groups, arrived, lefts, step):
+        taken = [
+            take_in(g, more, left, order[step])
+            for g, more, left, order in zip(groups, arrived, lefts, orders)
+        ]
+        lefts = [left for _, left in taken]
+        if step == 2:
+            return [total for total, _ in taken], None, lefts
+        groups = [total.astype(jnp.bfloat16) for total, _ in taken]
+        arrived = [
+            pass_along(g, left, order[step + 1]) for g, left, order in zip(groups, lefts, orders)
+        ]
+        return groups, arrived, lefts
+
+    groups, arrived, lefts = next_axis(groups, arrived, lefts, 0)
     grad_logits = (
         grad_decay.reshape(seq_count, tok_count, KEYS) * jax.nn.sigmoid(-logits) / 16.0
     ).astype(jnp.bfloat16)
@@ -850,9 +1071,7 @@
     grad_lowrank = back_project(grad_logits, weight_up).astype(jnp.bfloat16)
     down_rank_grad = weight_grad(normed, grad_lowrank)
     grad_normed = (
-        back_project(grad_q, weight_q)
-        + back_project(grad_k, weight_k)
-        + back_project(grad_v, weight_v)
+        back_project(grad_qkv.reshape(seq_count, tok_count, -1), mixer_full[:, :2048])
         + back_project(grad_gate_out, weight_g)
         + back_project(grad_lowrank, weight_down)
     )
@@ -863,22 +1082,34 @@
     small_grads = pack_small_grads(
         down_rank_grad, gain_one_grad, gain_two_grad, bias_grad, group_grad, up_rank_grad, devices
     )
-    mine = reduce_to_owner(
-        jnp.concatenate(
-            [
-                weight_grad(normed, grad_q),
-                weight_grad(normed, grad_k),
-                weight_grad(normed, grad_v),
-                weight_grad(normed, grad_gate_out),
-                out_w_grad,
-                small_grads,
-            ],
-            axis=1,
-        ).astype(jnp.bfloat16),
-        names,
-        sizes,
-    ).astype(jnp.float32)
-    small = mine[:, 4096:]
+    late = flat_grad(normed.reshape(rows, -1), grad_qkv).astype(jnp.bfloat16)
+    small_grads = small_grads.astype(jnp.bfloat16)
+    arrived, late, small_grads, tokens_grad = lax.optimization_barrier(
+        (arrived, late, small_grads, tokens_grad)
+    )
+    groups = [
+        take_in(g, more, left, order[1])[0].astype(jnp.bfloat16)
+        for g, more, left, order in zip(groups, arrived, lefts, orders)
+    ]
+    own_rows = feature_count // devices
+    late = late.reshape(*sizes, own_rows, -1)
+    small_grads = small_grads.reshape(*sizes, own_rows, -1)
+    size_of = dict(zip(names, sizes))
+    jobs = [
+        (which, columns, names, ("core", *order), which, columns)
+        for which, columns, order in (
+            (3, (0, 896), orders[0]),
+            (3, (896, 1792), orders[1]),
+            (3, (1792, 2048), orders[2]),
+            (4, (0, EXTRA), orders[2]),
+        )
+    ] + [
+        (i, (0, groups[i].shape[-1]), (order[2],), (order[2],), i, (0, groups[i].shape[-1]))
+        for i, order in enumerate(orders)
+    ]
+    first_group, second_group, third_group, mine, small = reduce_rest(
+        (*groups, late, small_grads), jobs, size_of, own_rows, (4224, 4224, 2048, 2048, EXTRA), 3
+    )
     return (
         layer_out,
         tokens_grad,
@@ -886,16 +1117,18 @@
         mine[:, :512],
         mine[:, 512:1024],
         mine[:, 1024:2048],
-        mine[:, 2048:3072],
+        second_group[:, FF : FF + VALS],
         small[:, :16],
         small[:, 24:32].reshape(KEYS // devices, 16).T,
         small[: KEYS // devices, 18],
         small[: HEAD_V // devices, 19],
-        mine[:, 3072:4096],
+        first_group[:, FF : FF + VALS],
         small[:, 17],
-        ffn_mine[:, :FF],
-        ffn_mine[:, FF : 2 * FF],
-        ffn_mine[:, 2 * FF :].T,
+        first_group[:, :FF],
+        second_group[:, :FF],
+        jnp.concatenate(
+            [third_group, first_group[:, FF + VALS :], second_group[:, FF + VALS :]], axis=1
+        ).T,
     )
 
 

time: 921 us -> 737 us (0.80)
  waiting for transfers between devices: 348 us -> 92.3 us
  Pallas kernels: 201 us -> 288 us
  other arithmetic: 72.2 us -> 51.7 us
  local copies, waits for them, and re-layouts: 107 us -> 86.5 us
  matrix products: 167 us -> 181 us
  starting transfers between devices: 0.52 us -> 12.4 us
    reduce_scatter x2 -> x0, waiting for transfers between devices: 263 us -> none  [reduce_to_owner(): return lax.psum_scatter(total, rest, scatter_dimension=0, tiled=True)]
    pallas_call x0 -> x1, Pallas kernels: none -> 58.6 us  [reduce_rest(): pl.pallas_call(partial(reduce_kernel, (len(arrays), jobs, sizes, slots)),...]
    dot_general x0 -> x11, matrix products: none -> 49.3 us  [flat_grad(): jnp.einsum('td,te->de', inputs, gradient, preferred_element_type=jnp.floa...]
    dot_general x10 -> x2, matrix products: 46.4 us -> 0.62 us  [weight_grad(): jnp.einsum('std,ste->de', inputs, gradient, preferred_element_type=jnp.fl...]
    pallas_call x1, Pallas kernels: 66.3 us -> 95.6 us  [mix_backward(): pl.pallas_call(partial(backward_kernel, axes), out_shape=(jax.ShapeDtypeS...]
    add x3 -> x0, other arithmetic: 16.4 us -> none  [the longest x2 15.2 us: reduce_to_owner(): total = (kept + taken).reshape(rows // sizes[at], width)]
    concatenate x6 -> x1, local copies, waits for them, and re-layouts: 16.4 us -> 3.42 us  [pack_small_grads(): return jnp.concatenate(pieces, axis=1)]
    convert_element_type x2 -> x8, other arithmetic: 2.11 us -> 14.2 us  [the longest x3 6.41 us: next_axis(): groups = [total.astype(jnp.bfloat16) for total, _ in taken]]
  transfers between devices with their start and end apart: 6 -> 17, of which waited for: 4 -> 2; matrix products, arithmetic and copies ran while one was open for 15% -> 20% of each run, Pallas kernels for 15% -> 32%
where the time goes in v3:
time: 737 us; the launch traced here: 728 us
  Pallas kernels  288 us (39%)
  matrix products  181 us (25%)
  waiting for transfers between devices  92.3 us (13%)
  local copies, waits for them, and re-layouts  86.5 us (12%)
  other arithmetic  51.7 us (7%)
  between operations  15.8 us (2%)
  starting transfers between devices  12.4 us (2%)
    pallas_call x1, Pallas kernels, mix_forward(): pl.pallas_call(partial(forward_kernel, axes), out_shape=(jax.ShapeDtypeSt...  134 us
    pallas_call x1, Pallas kernels, mix_backward(): pl.pallas_call(partial(backward_kernel, axes), out_shape=(jax.ShapeDtypeS...  95.6 us
    all_gather x1, waiting for transfers between devices, local(): lax.all_gather(pack_mixer(norm1_gain, norm2_gain, query_weight, key_weigh...  76.5 us
    dot_general x8, matrix products, back_project(): jnp.einsum('ste,de->std', gradient, weight, preferred_element_type=jnp.fl...  66.1 us
    dot_general x10, matrix products, project(): jnp.einsum('std,de->ste', inputs, weight, preferred_element_type=jnp.floa...  64.9 us
    pallas_call x1, Pallas kernels, reduce_rest(): pl.pallas_call(partial(reduce_kernel, (len(arrays), jobs, sizes, slots)),...  58.6 us
    dot_general x11, matrix products, flat_grad(): jnp.einsum('td,te->de', inputs, gradient, preferred_element_type=jnp.floa...  49.3 us
    unnamed x203, local copies, waits for them, and re-layouts  23.3 us
  transfers between devices with their start and end apart: 17, of which 2 were waited for; matrix products, arithmetic and copies ran while one was open for 20% of the time, Pallas kernels for 32%

profile of v3, /device:TPU:0, one launch (start us, length us, event | category | flops | bytes accessed | tf_op | source)
XLA Modules:
  0.0 727.6 jit_solution(2436598973778684950)
XLA Ops:
  37.2 76.5 %all-gather.3.cloned.1.call-done = bf16[1024,4224]{1,0:T(8,128)(2,1)} async-done(((bf16[32,4224]{1,0:T(8,128)(2,1)}), bf16[1024,4224]{1,0:T(8,128)(2,1)}) %all-gather.3.cloned.1.call-update) | async-done | bytes 8650768 | tf_op jit(solution)/shard_map/all_gather | solution.py:928
  122.5 3.4 fusion.27
  131.3 5.7 fusion.30
  137.0 133.7 %mix_forward.1 = (f32[1024,1024]{1,0:T(8,128)}, f32[1024,512]{1,0:T(8,128)}, bf16[16,3,256,128]{3,2,1,0:T(8,128)(2,1)}, bf16[16,256,128]{2,1,0:T(8,128)(2,1)S(1)}) custom-call(s32[4]{0:T(128)S(1)} %copy-done.1, bf16[1024,512]{1,0:T(8,128)(2,1)S(1)} %bitcast.212, bf16[1024,512]{1,0:T(8,128)(2,1)S(1)} %bitcast.210, bf16[1024,1024]{1,0:T(8,128)(2,1)} %bitcast.256, ...), custom_call_target="tpu_custom_call" | custom-call | flops 60000002048 | bytes 220000000 | tf_op jit(solution)/shard_map/mix_forward/pallas_call | solution.py:574
  271.7 5.6 reshape.404
  283.4 6.2 mul.259
  290.0 10.3 %multiply_convert_fusion.3 = (bf16[4,256,1024]{2,1,0:T(8,128)(2,1)S(1)}, f32[4,256,1024]{2,1,0:T(8,128)}, f32[4,256,1024]{2,1,0:T(8,128)}) fusion(f32[1024]{0:T(1024)S(1)} %bitcast.234, f32[4,256,1024]{2,1,0:T(8,128)} %bitcast.225, f32[4,256,1024]{2,1,0:T(8,128)} %mul.259, bf16[4,256,1024]{2,1,0:T(8,128)(2,1)S(1)} %fusion.16, ...), kind=kOutput, calls=%fused_computation.57 | convolution fusion | flops 2155872256 | bytes 23072768 | tf_op jit(solution)/shard_map/std,de->ste/dot_general | solution.py:25
  300.3 4.1 multiply_reduce_fusion.4
  310.9 11.6 %fusion.11 = f32[4,256,2816]{2,1,0:T(8,128)} fusion(bf16[4,256,1024]{2,1,0:T(8,128)(2,1)S(1)} %copy-done.27, bf16[1024,8448]{1,0:T(8,128)(2,1)} %all-gather.5.cloned.1.call-done), kind=kOutput, calls=%fused_computation.28 | convolution fusion | flops 5905580032 | bytes 19398656 | tf_op jit(solution)/shard_map/std,de->ste/dot_general | solution.py:25
  322.4 11.6 %fusion.9 = f32[4,256,2816]{2,1,0:T(8,128)} fusion(bf16[4,256,1024]{2,1,0:T(8,128)(2,1)S(1)} %copy-done.28, bf16[1024,8448]{1,0:T(8,128)(2,1)} %all-gather.5.cloned.1.call-done), kind=kOutput, calls=%fused_computation.26 | convolution fusion | flops 5905580032 | bytes 19398656 | tf_op jit(solution)/shard_map/std,de->ste/dot_general | solution.py:25
  334.1 20.4 %fusion.2 = (bf16[4,256,2816]{2,1,0:T(8,128)(2,1)}, bf16[4,256,2816]{2,1,0:T(8,128)(2,1)}, bf16[4,256,2816]{2,1,0:T(8,128)(2,1)}) fusion(f32[4,256,2816]{2,1,0:T(8,128)} %fusion.9, f32[4,256,2816]{2,1,0:T(8,128)} %fusion.11, bf16[4,256,1024]{2,1,0:T(8,128)(2,1)S(1)} %copy-done.14, bf16[1024,8448]{1,0:T(8,128)(2,1)} %all-gather.5.cloned.1.call-done), kind=kOutput, calls=%fused_computation.4 | convolution fusion | flops 5948833792 | bytes 48234496 | tf_op jit(solution)/shard_map/ste,de->std/dot_general | solution.py:29
  354.4 10.0 %fusion.8 = f32[4,256,1024]{2,1,0:T(8,128)S(1)} fusion(bf16[4,256,2816]{2,1,0:T(8,128)(2,1)} %get-tuple-element.211, bf16[1024,8448]{1,0:T(8,128)(2,1)} %all-gather.5.cloned.1.call-done), kind=kOutput, calls=%fused_computation.25 | convolution fusion | flops 5905580032 | bytes 15728640 | tf_op jit(solution)/shard_map/ste,de->std/dot_general | solution.py:29
  364.5 9.0 %multiply_reduce_fusion.1 = (bf16[1024]{0:T(1024)(128)(2,1)S(1)}, f32[4,256]{1,0:T(4,128)S(1)}, f32[4,256,1024]{2,1,0:T(8,128)S(1)}) fusion(f32[4,256,1024]{2,1,0:T(8,128)S(1)} %copy-done.8, f32[4,256]{1,0:T(4,128)S(1)} %add_rsqrt_fusion.1, f32[1024]{0:T(1024)S(1)} %get-tuple-element.196, f32[4,256,1024]{2,1,0:T(8,128)S(1)} %fusion.8, ...), kind=kOutput, calls=%fused_computation.47 | convolution fusion | flops 5912918016 | bytes 24131584 | tf_op jit(solution)/shard_map/ste,de->std/dot_general | solution.py:29
  379.2 7.5 %multiply_reduce_fusion = (f32[1024]{0:T(1024)S(1)}, f32[4,256,1024]{2,1,0:T(8,128)}, bf16[4,256,1024]{2,1,0:T(8,128)(2,1)}) fusion(f32[4,256,1024]{2,1,0:T(8,128)S(1)} %copy-done.83, f32[4,256,1024]{2,1,0:T(8,128)S(1)} %copy-done.84, f32[1024]{0:T(1024)S(1)} %bitcast.235, bf16[4,256,1024]{2,1,0:T(8,128)(2,1)S(1)} %fusion.95, ...), kind=kOutput, calls=%fused_computation.46 | convolution fusion | flops 2163211264 | bytes 18882560 | tf_op jit(solution)/shard_map/ste,de->std/dot_general | solution.py:29
  386.7 5.7 mul.297
  392.5 5.8 multiply_reduce_fusion.2
  398.5 5.0 convolution_convert_fusion
  406.4 4.8 convolution_convert_fusion.1
  414.0 11.1 %add_convert_fusion.3 = bf16[4,256,1024]{2,1,0:T(8,128)(2,1)} fusion(f32[4,256,1024]{2,1,0:T(8,128)S(1)} %copy-done.9, bf16[4,256,2816]{2,1,0:T(8,128)(2,1)} %get-tuple-element.212, bf16[1024,8448]{1,0:T(8,128)(2,1)} %all-gather.5.cloned.1.call-done), kind=kOutput, calls=%fused_computation.54 | convolution fusion | flops 5907677184 | bytes 17825792 | tf_op jit(solution)/shard_map/std,de->ste/dot_general | solution.py:25
  425.1 4.3 subtract_multiply_fusion
  429.4 5.3 convolution_convert_fusion.2
  436.5 6.7 fusion.31
  448.7 6.8 add_convert_fusion.1
  456.8 6.1 add_convert_fusion
  463.3 5.2 add_convert_fusion.2
  482.7 3.7 collective-permute-start.9
  486.4 95.6 %mix_backward.1 = (bf16[1024,2048]{1,0:T(8,128)(2,1)}, f32[1024,512]{1,0:T(8,128)}) custom-call(s32[4]{0:T(128)} %prefix_ref.3, bf16[1024,512]{1,0:T(8,128)(2,1)} %bitcast.213, bf16[1024,512]{1,0:T(8,128)(2,1)} %bitcast.211, bf16[1024,1024]{1,0:T(8,128)(2,1)} %bitcast.257, f32[1024,512]{1,0:T(8,128)} %get-tuple-element.122.cum_ref, ...), custom_call_target="tpu_custom_call" | custom-call | flops 60000002048 | bytes 220000000 | tf_op jit(solution)/shard_map/mix_backward/pallas_call | solution.py:606
  586.2 6.3 convolution_convert_fusion.3
  594.4 10.3 %fusion.18 = (f32[4,256]{1,0:T(4,128)S(1)}, bf16[1024]{0:T(1024)(128)(2,1)S(1)}, f32[4,256,1024]{2,1,0:T(8,128)}) fusion(bf16[4,256,1024]{2,1,0:T(8,128)(2,1)S(1)} %copy-done.18, f32[1024]{0:T(1024)S(1)} %copy-done.74, f32[4,256]{1,0:T(4,128)S(1)} %copy-done.76, f32[4,256,1024]{2,1,0:T(8,128)S(1)} %fusion.96, f32[4,256,1024]{2,1,0:T(8,128)} %fusion.31, ...), kind=kOutput, calls=%fused_computation.39 | convolution fusion | flops 4304402432 | bytes 23083008 | tf_op jit(solution)/shard_map/ste,de->std/dot_general | solution.py:29
  620.5 3.7 fusion.21
  633.3 15.7 %collective-permute-done.12 = bf16[2,32,4224]{2,1,0:T(8,128)(2,1)} collective-permute-done((bf16[2,32,4224]{2,1,0:T(8,128)(2,1)}, bf16[2,32,4224]{2,1,0:T(8,128)(2,1)}, u32[]{:S(2)}, u32[]{:S(2)}) %collective-permute-start.12) | collective-permute-done | bytes 540704 | tf_op jit(solution)/shard_map/ppermute | solution.py:745
  653.3 58.6 %reduce_rest.1 = (f32[32,4224]{1,0:T(8,128)S(1)}, f32[32,4224]{1,0:T(8,128)S(1)}, f32[32,2048]{1,0:T(8,128)S(1)}, f32[32,2048]{1,0:T(8,128)S(1)}, f32[32,128]{1,0:T(8,128)S(1)}) custom-call(bf16[4,32,4224]{2,1,0:T(8,128)(2,1)S(1)} %fusion.25.refs_0_, bf16[2,32,4224]{2,1,0:T(8,128)(2,1)S(1)} %fusion.38.refs_1_, bf16[2,32,2048]{2,1,0:T(8,128)(2,1)S(1)} %fusion.94.refs_2_, ...), custom_call_target="tpu_custom_call" | custom-call | tf_op jit(solution)/shard_map/reduce_rest/pallas_call | solution.py:887
  (353 shorter events, 135.2 us)
Async XLA Ops:
  7.2 27.2 %copy-start.13 = (bf16[4,256,1024]{2,1,0:T(8,128)(2,1)S(1)}, bf16[4,256,1024]{2,1,0:T(8,128)(2,1)}, u32[]{:S(2)}) copy-start(bf16[4,256,1024]{2,1,0:T(8,128)(2,1)} %param.45) | copy-start | bytes 6291460
  7.2 106.5 %all-gather.3.cloned.1.call-start = ((), (), s32[]{:S(2)}) async-start(), calls=%async_computation | async-start | bytes 8921088 | tf_op jit(solution)/shard_map/all_gather | solution.py:928
  32.3 277.8 %all-gather.5.cloned.1.call-start = ((), (), s32[]{:S(2)}) async-start(), calls=%async_computation.1 | async-start | bytes 17842176 | tf_op jit(solution)/shard_map/all_gather | solution.py:946
  37.2 80.8 %copy-start.75 = (f32[4,256]{1,0:T(4,128)}, f32[4,256]{1,0:T(4,128)S(1)}, u32[]{:S(2)}) copy-start(f32[4,256]{1,0:T(4,128)S(1)} %add_rsqrt_fusion.2) | copy-start | bytes 12292
  118.0 255.5 %copy-start.67 = (f32[1024]{0:T(1024)}, f32[1024]{0:T(1024)S(1)}, u32[]{:S(2)}) copy-start(f32[1024]{0:T(1024)S(1)} %get-tuple-element.196) | copy-start | bytes 12292
  120.7 186.3 %copy-start.11 = (bf16[4,256,1024]{2,1,0:T(8,128)(2,1)}, bf16[4,256,1024]{2,1,0:T(8,128)(2,1)S(1)}, u32[]{:S(2)}) copy-start(bf16[4,256,1024]{2,1,0:T(8,128)(2,1)S(1)} %fusion.16) | copy-start | bytes 6291460
  304.4 69.1 %copy-start.69 = (f32[4,256]{1,0:T(4,128)}, f32[4,256]{1,0:T(4,128)S(1)}, u32[]{:S(2)}) copy-start(f32[4,256]{1,0:T(4,128)S(1)} %add_rsqrt_fusion.1) | copy-start | bytes 12292
  322.4 11.6 %copy-start.14 = (bf16[4,256,1024]{2,1,0:T(8,128)(2,1)S(1)}, bf16[4,256,1024]{2,1,0:T(8,128)(2,1)}, u32[]{:S(2)}) copy-start(bf16[4,256,1024]{2,1,0:T(8,128)(2,1)} %param.45) | copy-start | bytes 6291460
  386.7 11.6 %slice-start.4 = ((s8[5767168]{0:T(1024)(128)(4,1)}), s8[1572864]{0:T(1024)(128)(4,1)S(1)}, s32[]{:S(2)}) async-start(s8[5767168]{0:T(1024)(128)(4,1)} %bitcast.245), calls=%async_computation.6 | async-start | bytes 3145728
  392.5 13.8 %slice-start.8 = ((s8[5767168]{0:T(1024)(128)(4,1)}), s8[4194304]{0:T(1024)(128)(4,1)S(1)}, s32[]{:S(2)}) async-start(s8[5767168]{0:T(1024)(128)(4,1)} %bitcast.252), calls=%async_computation.10 | async-start | bytes 8388608
  403.5 52.5 %collective-permute-start.3 = (bf16[512,2816]{1,0:T(8,128)(2,1)}, bf16[512,2816]{1,0:T(8,128)(2,1)}, u32[]{:S(2)}, u32[]{:S(2)}) collective-permute-start(bf16[512,2816]{1,0:T(8,128)(2,1)} %convolution_convert_fusion), channel_id=1, source_target_pairs={{0,4},{4,0},{1,5},{5,1},{2,6},{6,2},{3,7},{7,3},{8,12},{12,8},{9,1... | collective-permute-start | bytes 8650760 | tf_op jit(solution)/shard_map/ppermute | solution.py:719
  405.8 37.4 %collective-permute-start.4 = (bf16[512,1024]{1,0:T(8,128)(2,1)}, bf16[512,1024]{1,0:T(8,128)(2,1)}, u32[]{:S(2)}, u32[]{:S(2)}) collective-permute-start(bf16[512,1024]{1,0:T(8,128)(2,1)} %convolution_convert_fusion.4), channel_id=1, source_target_pairs={{0,4},{4,0},{1,5},{5,1},{2,6},{6,2},{3,7},{7,3},{8,12},{12,8},{9,1... | collective-permute-start | bytes 3145736 | tf_op jit(solution)/shard_map/ppermute | solution.py:719
  411.2 37.5 %collective-permute-start.2 = (bf16[512,2816]{1,0:T(8,128)(2,1)}, bf16[512,2816]{1,0:T(8,128)(2,1)}, u32[]{:S(2)}, u32[]{:S(2)}) collective-permute-start(bf16[512,2816]{1,0:T(8,128)(2,1)} %convolution_convert_fusion.1), channel_id=1, source_target_pairs={{0,4},{4,0},{1,5},{5,1},{2,6},{6,2},{3,7},{7,3},{8,12},{12,8},{9,1... | collective-permute-start | bytes 8650760 | tf_op jit(solution)/shard_map/ppermute | solution.py:719
  411.3 18.2 %slice-start = ((s8[5767168]{0:T(1024)(128)(4,1)}), s8[1572864]{0:T(1024)(128)(4,1)S(1)}, s32[]{:S(2)}) async-start(s8[5767168]{0:T(1024)(128)(4,1)} %bitcast.239), calls=%async_computation.2 | async-start | bytes 3145728
  413.5 15.9 %slice-start.1 = ((s8[5767168]{0:T(1024)(128)(4,1)}), s8[4194304]{0:T(1024)(128)(4,1)S(1)}, s32[]{:S(2)}) async-start(s8[5767168]{0:T(1024)(128)(4,1)} %bitcast.239), calls=%async_computation.3 | async-start | bytes 8388608
  413.5 32.4 %collective-permute-start.1 = (bf16[512,1024]{1,0:T(8,128)(2,1)}, bf16[512,1024]{1,0:T(8,128)(2,1)}, u32[]{:S(2)}, u32[]{:S(2)}) collective-permute-start(bf16[512,1024]{1,0:T(8,128)(2,1)} %convolution_convert_fusion.5), channel_id=1, source_target_pairs={{0,4},{4,0},{1,5},{5,1},{2,6},{6,2},{3,7},{7,3},{8,12},{12,8},{9,1... | collective-permute-start | bytes 3145736 | tf_op jit(solution)/shard_map/ppermute | solution.py:719
  434.8 28.5 %collective-permute-start = (bf16[512,2816]{1,0:T(8,128)(2,1)}, bf16[512,2816]{1,0:T(8,128)(2,1)}, u32[]{:S(2)}, u32[]{:S(2)}) collective-permute-start(bf16[512,2816]{1,0:T(8,128)(2,1)} %convolution_convert_fusion.2), channel_id=1, source_target_pairs={{0,4},{4,0},{1,5},{5,1},{2,6},{6,2},{3,7},{7,3},{8,12},{12,8},{9,1... | collective-permute-start | bytes 8650760 | tf_op jit(solution)/shard_map/ppermute | solution.py:719
  455.9 25.6 %copy-start.29 = (bf16[512,2048]{1,0:T(8,128)(2,1)}, bf16[512,2048]{1,0:T(8,128)(2,1)S(1)}, u32[]{:S(2)}) copy-start(bf16[512,2048]{1,0:T(8,128)(2,1)S(1)} %slice.276) | copy-start | bytes 6291460
  476.9 105.3 %collective-permute-start.6 = (bf16[2,4,32,4224]{3,2,0,1:T(8,128)(2,1)}, bf16[2,4,32,4224]{3,2,0,1:T(8,128)(2,1)}, u32[]{:S(2)}, u32[]{:S(2)}) collective-permute-start(bf16[2,4,32,4224]{3,2,0,1:T(8,128)(2,1)} %bitcast.205), channel_id=1, source_target_pairs={{0,8},{8,0},{1,9},{9,1},{2,10},{10,2},{3,11},{11,3},{4,12},{12,4},... | collective-permute-start | bytes 6488072 | tf_op jit(solution)/shard_map/ppermute | solution.py:745
  480.0 102.2 %collective-permute-start.5 = (bf16[2,4,32,4224]{3,2,1,0:T(8,128)(2,1)}, bf16[2,4,32,4224]{3,2,1,0:T(8,128)(2,1)}, u32[]{:S(2)}, u32[]{:S(2)}) collective-permute-start(bf16[2,4,32,4224]{3,2,1,0:T(8,128)(2,1)} %dynamic-slice_bitcast_fusion), channel_id=1, source_target_pairs={{0,16},{16,0},{1,17},{17,1},{2,18},{18,2},{3,19},{19,3},{4,20},{20... | collective-permute-start | bytes 6488072 | tf_op jit(solution)/shard_map/ppermute | solution.py:745
  482.4 99.7 %collective-permute-start.7 = (bf16[2,2,32,2048]{3,2,1,0:T(8,128)(2,1)}, bf16[2,2,32,2048]{3,2,1,0:T(8,128)(2,1)}, u32[]{:S(2)}, u32[]{:S(2)}) collective-permute-start(bf16[2,2,32,2048]{3,2,1,0:T(8,128)(2,1)} %get-tuple-element.223), channel_id=1, source_target_pairs={{0,1},{1,2},{2,3},{3,0},{4,5},{5,6},{6,7},{7,4},{8,9},{9,10},{10,1... | collective-permute-start | bytes 1572872 | tf_op jit(solution)/shard_map/ppermute | solution.py:745
  482.6 99.5 %collective-permute-start.8 = (bf16[2,2,32,2048]{3,2,1,0:T(8,128)(2,1)S(1)}, bf16[2,2,32,2048]{3,2,1,0:T(8,128)(2,1)}, u32[]{:S(2)}, u32[]{:S(2)}) collective-permute-start(bf16[2,2,32,2048]{3,2,1,0:T(8,128)(2,1)S(1)} %get-tuple-element.222), channel_id=1, source_target_pairs={{0,2},{1,3},{2,0},{3,1},{4,6},{5,7},{6,4},{7,5},{8,10},{9,11},{10,... | collective-permute-start | bytes 1572872 | tf_op jit(solution)/shard_map/ppermute | solution.py:745
  482.7 99.4 %collective-permute-start.9 = (bf16[2,2,32,2048]{3,2,1,0:T(8,128)(2,1)S(1)}, bf16[2,2,32,2048]{3,2,1,0:T(8,128)(2,1)}, u32[]{:S(2)}, u32[]{:S(2)}) collective-permute-start(bf16[2,2,32,2048]{3,2,1,0:T(8,128)(2,1)S(1)} %get-tuple-element.221), channel_id=1, source_target_pairs={{0,3},{1,0},{2,1},{3,2},{4,7},{5,4},{6,5},{7,6},{8,11},{9,8},{10,9... | collective-permute-start | bytes 1572872 | tf_op jit(solution)/shard_map/ppermute | solution.py:745
  486.4 95.7 %copy-start.78 = (f32[512]{0:T(512)S(1)}, f32[512]{0:T(512)}, u32[]{:S(2)}) copy-start(f32[512]{0:T(512)} %copy-done.77) | copy-start | bytes 6148
  607.4 25.9 %collective-permute-start.14 = (bf16[2,32,2048]{2,1,0:T(8,128)(2,1)}, bf16[2,32,2048]{2,1,0:T(8,128)(2,1)}, u32[]{:S(2)}, u32[]{:S(2)}) collective-permute-start(bf16[2,32,2048]{2,1,0:T(8,128)(2,1)} %dynamic-slice_bitcast_fusion.8), channel_id=1, source_target_pairs={{0,16},{16,0},{1,17},{17,1},{2,18},{18,2},{3,19},{19,3},{4,20},{20... | collective-permute-start | bytes 786440 | tf_op jit(solution)/shard_map/ppermute | solution.py:745
  607.9 12.5 %copy-start.30 = (f32[4,256,1024]{2,1,0:T(8,128)S(1)}, f32[4,256,1024]{2,1,0:T(8,128)}, u32[]{:S(2)}) copy-start(f32[4,256,1024]{2,1,0:T(8,128)} %get-tuple-element.268) | copy-start | bytes 12582916
  611.4 21.8 %collective-permute-start.11 = (bf16[2,32,4224]{2,1,0:T(8,128)(2,1)}, bf16[2,32,4224]{2,1,0:T(8,128)(2,1)}, u32[]{:S(2)}, u32[]{:S(2)}) collective-permute-start(bf16[2,32,4224]{2,1,0:T(8,128)(2,1)} %get-tuple-element.220), channel_id=1, source_target_pairs={{0,1},{1,2},{2,3},{3,0},{4,5},{5,6},{6,7},{7,4},{8,9},{9,10},{10,1... | collective-permute-start | bytes 1622024 | tf_op jit(solution)/shard_map/ppermute | solution.py:745
  611.4 37.6 %collective-permute-start.12 = (bf16[2,32,4224]{2,1,0:T(8,128)(2,1)}, bf16[2,32,4224]{2,1,0:T(8,128)(2,1)}, u32[]{:S(2)}, u32[]{:S(2)}) collective-permute-start(bf16[2,32,4224]{2,1,0:T(8,128)(2,1)} %get-tuple-element.219), channel_id=1, source_target_pairs={{0,2},{1,3},{2,0},{3,1},{4,6},{5,7},{6,4},{7,5},{8,10},{9,11},{10,... | collective-permute-start | bytes 1622024 | tf_op jit(solution)/shard_map/ppermute | solution.py:745
  612.1 36.9 %collective-permute-start.13 = (bf16[2,32,4224]{2,1,0:T(8,128)(2,1)}, bf16[2,32,4224]{2,1,0:T(8,128)(2,1)}, u32[]{:S(2)}, u32[]{:S(2)}) collective-permute-start(bf16[2,32,4224]{2,1,0:T(8,128)(2,1)} %get-tuple-element.218), channel_id=1, source_target_pairs={{0,3},{1,0},{2,1},{3,2},{4,7},{5,4},{6,5},{7,6},{8,11},{9,8},{10,9... | collective-permute-start | bytes 1622024 | tf_op jit(solution)/shard_map/ppermute | solution.py:745
  619.9 29.1 %collective-permute-start.10 = (bf16[4,32,4224]{2,1,0:T(8,128)(2,1)}, bf16[4,32,4224]{2,1,0:T(8,128)(2,1)}, u32[]{:S(2)}, u32[]{:S(2)}) collective-permute-start(bf16[4,32,4224]{2,1,0:T(8,128)(2,1)} %dynamic-slice_bitcast_fusion.1), channel_id=1, source_target_pairs={{0,8},{8,0},{1,9},{9,1},{2,10},{10,2},{3,11},{11,3},{4,12},{12,4},... | collective-permute-start | bytes 3244040 | tf_op jit(solution)/shard_map/ppermute | solution.py:745
  626.8 23.3 %copy-start.24 = (bf16[2,4,32,4224]{3,2,1,0:T(8,128)(2,1)S(1)}, bf16[2,4,32,4224]{3,2,1,0:T(8,128)(2,1)}, u32[]{:S(2)}) copy-start(bf16[2,4,32,4224]{3,2,1,0:T(8,128)(2,1)} %copy-done.23) | copy-start | bytes 6488068
  633.2 20.1 %copy-start = (bf16[1024,2048]{1,0:T(8,128)(2,1)S(1)}, bf16[1024,2048]{1,0:T(8,128)(2,1)}, u32[]{:S(2)}) copy-start(bf16[1024,2048]{1,0:T(8,128)(2,1)} %convolution_convert_fusion.3) | copy-start | bytes 12582916
  (80 other events, 404.6 us)
Sparse Core Ops, SparseCore 0:
  32.4 81.2 all-gather.2
  116.5 150.0 all-gather.4

commit v4 on v3

--- a/solution.py
+++ b/solution.py
@@ -22,15 +22,11 @@
 
 
 def project(inputs, weight):
-    return jnp.einsum("std,de->ste", inputs, weight, preferred_element_type=jnp.float32)
+    return jnp.einsum("td,de->te", inputs, weight, preferred_element_type=jnp.float32)
 
 
 def back_project(gradient, weight):
-    return jnp.einsum("ste,de->std", gradient, weight, preferred_element_type=jnp.float32)
-
-
-def weight_grad(inputs, gradient):
-    return jnp.einsum("std,ste->de", inputs, gradient, preferred_element_type=jnp.float32)
+    return jnp.einsum("te,de->td", gradient, weight, preferred_element_type=jnp.float32)
 
 
 def rms_scale(values):
@@ -103,7 +99,7 @@
     return int(np.prod([size for _, size in axes]))
 
 
-def greet(axes, place, count):
+def greet(axes, place, count, extra=0):
     barrier = pltpu.get_barrier_semaphore()
 
     @pl.when(place > 0)
@@ -120,11 +116,11 @@
 
     @pl.when(jnp.logical_or(place == 0, place == count - 1))
     def _():
-        pl.semaphore_wait(barrier, 1)
+        pl.semaphore_wait(barrier, 1 + extra)
 
     @pl.when(jnp.logical_and(place > 0, place < count - 1))
     def _():
-        pl.semaphore_wait(barrier, 2)
+        pl.semaphore_wait(barrier, 2 + extra)
 
 
 def send(source, target, send_sem, recv_sem, axes, place):
@@ -138,6 +134,154 @@
     )
 
 
+class Gather:
+    def __init__(self, names, sizes, pieces, local_sem, send_sem, recv_sem, pair_send, pair_recv):
+        self.names = names
+        self.sizes = dict(zip(names, sizes))
+        self.pieces = pieces
+        self.sems = local_sem, send_sem, recv_sem, pair_send, pair_recv
+        self.steps = len(pieces[0][4])
+
+    def region(self, piece, known, at):
+        lead = []
+        for name in self.names:
+            if name in known:
+                lead.append(slice(None))
+            elif name in at:
+                lead.append(at[name])
+            else:
+                lead.append(lax.axis_index(name))
+        _, whole, _, columns, _ = piece
+        return whole.at[(*lead, slice(None), slice(*columns))]
+
+    def local(self, i):
+        shard, _, columns, _, _ = self.pieces[i]
+        return pltpu.make_async_copy(
+            shard.at[:, slice(*columns)], self.region(self.pieces[i], (), {}), self.sems[0].at[i]
+        )
+
+    def copies(self, i, step):
+        piece = self.pieces[i]
+        order = piece[4]
+        name = order[step]
+        own = lax.axis_index(name)
+        base = (i * self.steps + step) * 3
+        for shift in range(1, self.sizes[name]):
+            peer = lax.rem(own + shift, self.sizes[name])
+            here = self.region(piece, order[:step], {})
+            yield pltpu.make_async_remote_copy(
+                src_ref=here,
+                dst_ref=here,
+                send_sem=self.sems[1].at[base + shift - 1],
+                recv_sem=self.sems[2].at[base + shift - 1],
+                device_id={name: peer},
+                device_id_type=MESH,
+            )
+
+    def pair(self, i, step, shift):
+        piece = self.pieces[i]
+        order = piece[4]
+        if step < 0:
+            here = self.region(piece, (), {})
+            at = 0
+        else:
+            name = order[step]
+            source = lax.rem(lax.axis_index(name) + self.sizes[name] - shift, self.sizes[name])
+            here = self.region(piece, order[:step], {name: source})
+            at = 1 + step * 3 + shift - 1
+        at += i * (1 + 3 * self.steps)
+        return pltpu.make_async_remote_copy(
+            src_ref=here,
+            dst_ref=here,
+            send_sem=self.sems[3].at[at],
+            recv_sem=self.sems[4].at[at],
+            device_id={"core": 1 - lax.axis_index("core")},
+            device_id_type=MESH,
+        )
+
+    def begin(self):
+        for i in range(len(self.pieces)):
+            self.local(i).start()
+        for i in range(len(self.pieces)):
+            self.local(i).wait()
+            for copy in self.copies(i, 0):
+                copy.start()
+            self.pair(i, -1, 0).start()
+
+    def advance(self, step):
+        for i, piece in enumerate(self.pieces):
+            for copy in self.copies(i, step):
+                copy.wait_recv()
+            if step < self.steps - 1:
+                for copy in self.copies(i, step + 1):
+                    copy.start()
+            for shift in range(1, self.sizes[piece[4][step]]):
+                self.pair(i, step, shift).start()
+
+    def end(self):
+        for i, piece in enumerate(self.pieces):
+            for step in range(self.steps):
+                for copy in self.copies(i, step):
+                    copy.wait_send()
+                for shift in range(1, self.sizes[piece[4][step]]):
+                    self.pair(i, step, shift).wait()
+            self.pair(i, -1, 0).wait()
+
+    @staticmethod
+    def scratch(count):
+        return [
+            pltpu.SemaphoreType.DMA((count,)),
+            pltpu.SemaphoreType.DMA((count * 9,)),
+            pltpu.SemaphoreType.DMA((count * 9,)),
+            pltpu.SemaphoreType.DMA((count * 10,)),
+            pltpu.SemaphoreType.DMA((count * 10,)),
+        ]
+
+
+def signal_axes(names, sizes):
+    barrier = pltpu.get_barrier_semaphore()
+    peers = 0
+    for name, size in zip(names, sizes):
+        for shift in range(1, size):
+            peer = lax.rem(lax.axis_index(name) + shift, size)
+            pl.semaphore_signal(barrier, inc=1, device_id={name: peer}, device_id_type=MESH)
+            peers += 1
+    return peers
+
+
+def gather_kernel(plan, *refs):
+    names, sizes, inputs, outputs, pieces = plan
+    wholes = refs[inputs : inputs + outputs]
+    peers = signal_axes(names, sizes)
+    pl.semaphore_wait(pltpu.get_barrier_semaphore(), peers)
+    gather = Gather(
+        names,
+        sizes,
+        [(refs[i], wholes[o], cols, to, order) for i, o, cols, to, order in pieces],
+        *refs[inputs + outputs :],
+    )
+    gather.begin()
+    for step in range(gather.steps):
+        gather.advance(step)
+    gather.end()
+
+
+def gather_first(names, sizes, shards, widths, pieces):
+    rows = shards[0].shape[0]
+    anywhere = pl.BlockSpec(memory_space=pl.ANY)
+    return pl.pallas_call(
+        partial(gather_kernel, (names, sizes, len(shards), len(widths), pieces)),
+        out_shape=tuple(
+            jax.ShapeDtypeStruct((*sizes, rows, width), jnp.bfloat16) for width in widths
+        ),
+        in_specs=[anywhere] * len(shards),
+        out_specs=(anywhere,) * len(widths),
+        scratch_shapes=Gather.scratch(len(pieces)),
+        compiler_params=pltpu.CompilerParams(collective_id=4, has_side_effects=True),
+        name="gather_first",
+    )(*shards)
+
+
 def row_places(count):
     return iota((count, HEAD_K), 0)
 
@@ -159,33 +303,33 @@
     return piece, piece[CHUNK - 1 :], piece[CHUNK // 2 - 1 : CHUNK // 2]
 
 
-def forward_kernel(
-    axes,
-    prefix_ref,
-    q_ref,
-    k_ref,
-    v_ref,
-    decay_ref,
-    mixed_ref,
-    cum_ref,
-    state_ref,
-    prefix_state_ref,
-    kv_ref,
-    part_ref,
-    edge_ref,
-    right_out,
-    right_in,
-    left_out,
-    left_in,
-    right_sent,
-    right_got,
-    left_sent,
-    left_got,
-):
+def query_columns(head):
+    return slice(head * HEAD_K, (head + 1) * HEAD_K)
+
+
+def key_columns(head):
+    return slice(KEYS + head * HEAD_K, KEYS + (head + 1) * HEAD_K)
+
+
+def value_columns(head):
+    return slice(2 * KEYS + head * HEAD_V, 2 * KEYS + (head + 1) * HEAD_V)
+
+
+def gate_columns(head):
+    begin = 2 * KEYS + VALS + head * HEAD_V
+    return slice(begin, begin + HEAD_V)
+
+
+def forward_kernel(plan, *refs):
+    axes = plan
+    prefix_ref, proj_ref, decay_ref, gain_ref = refs[:4]
+    gated_ref, unit_ref, scale_ref, cum_ref, state_ref, prefix_state_ref = refs[4:10]
+    mixed_ref, kv_ref, part_ref, edge_ref, *line = refs[10:]
+    right_out, right_in, left_out, left_in, right_sent, right_got, left_sent, left_got = line
     count = line_length(axes)
     place = place_on(axes)
     seqs = prefix_ref.shape[0]
-    toks = q_ref.shape[0] // seqs
+    toks = proj_ref.shape[0] // seqs
     chunks = toks // CHUNK
     greet(axes, place, count)
     lower = low(jnp.where(iota((CHUNK, CHUNK), 0) >= iota((CHUNK, CHUNK), 1), 1.0, 0.0))
@@ -205,8 +349,8 @@
             keys = slice(head * HEAD_K, (head + 1) * HEAD_K)
             vals = slice(head * HEAD_V, (head + 1) * HEAD_V)
             before = jnp.zeros((1, HEAD_K), jnp.float32)
-            key = wide(k_ref[rows, keys])
-            value = v_ref[rows, vals]
+            key = wide(proj_ref[rows, key_columns(head)])
+            value = proj_ref[rows, value_columns(head)]
             decay = decay_ref[rows, keys]
             pieces = []
             local = jnp.zeros((HEAD_V, HEAD_K), jnp.float32)
@@ -242,9 +386,9 @@
             keys = slice(head * HEAD_K, (head + 1) * HEAD_K)
             vals = slice(head * HEAD_V, (head + 1) * HEAD_V)
             cum = cum_ref[rows, keys]
-            query = wide(q_ref[rows, keys])
-            key = wide(k_ref[rows, keys])
-            value = v_ref[rows, vals]
+            query = wide(proj_ref[rows, query_columns(head)])
+            key = wide(proj_ref[rows, key_columns(head)])
+            value = proj_ref[rows, value_columns(head)]
             scores = []
             for chunk in range(chunks):
                 at = slice(chunk * CHUNK, (chunk + 1) * CHUNK)
@@ -318,9 +462,15 @@
                 to_left(i).start()
 
             prefix_state_ref[i] = whole
-            mixed_ref[rows, vals] = jnp.where(
-                inside, nt(q_ref[rows, keys], whole), mixed_ref[rows, vals]
+            mixed = jnp.where(
+                inside, nt(proj_ref[rows, query_columns(head)], whole), mixed_ref[rows, vals]
             )
+            scale = lax.rsqrt(jnp.mean(mixed * mixed, axis=1, keepdims=True) + norm_eps)
+            unit = mixed * scale
+            gate = wide(proj_ref[rows, gate_columns(head)])
+            gated_ref[rows, vals] = low(unit * gain_ref[:1] * (gate / (1.0 + jnp.exp(-gate))))
+            unit_ref[rows, vals] = low(unit)
+            scale_ref[rows, slice(head, head + 1)] = scale
         return carry
 
     lax.fori_loop(0, seqs, prefix_of, 0)
@@ -342,15 +492,18 @@
 def backward_kernel(
     axes,
     prefix_ref,
-    q_ref,
-    k_ref,
-    v_ref,
+    proj_ref,
     cum_ref,
     state_ref,
     prefix_state_ref,
+    gated_grad_ref,
+    unit_ref,
+    scale_ref,
+    gain_ref,
+    dproj_ref,
+    ddecay_ref,
+    gain_grad_ref,
     grad_ref,
-    dqkv_ref,
-    ddecay_ref,
     local_ref,
     acc_ref,
     dk_part,
@@ -368,7 +521,7 @@
     count = line_length(axes)
     place = place_on(axes)
     seqs = prefix_ref.shape[0]
-    toks = q_ref.shape[0] // seqs
+    toks = proj_ref.shape[0] // seqs
     chunks = toks // CHUNK
     greet(axes, place, count)
     causal = iota((CHUNK, CHUNK), 0) >= iota((CHUNK, CHUNK), 1)
@@ -389,8 +542,23 @@
             keys = slice(head * HEAD_K, (head + 1) * HEAD_K)
             vals = slice(head * HEAD_V, (head + 1) * HEAD_V)
             cum = cum_ref[rows, keys]
-            query = q_ref[rows, keys]
-            grad = grad_ref[rows, vals]
+            query = proj_ref[rows, query_columns(head)]
+            gate = wide(proj_ref[rows, gate_columns(head)])
+            logistic = 1.0 / (1.0 + jnp.exp(-gate))
+            unit = wide(unit_ref[rows, vals])
+            gain = gain_ref[:1]
+            gated_grad = wide(gated_grad_ref[rows, vals])
+            through = gated_grad * unit
+            active = gate * logistic
+            dproj_ref[rows, gate_columns(head)] = low(
+                through * gain * (logistic + active * (1.0 - logistic))
+            )
+            gain_grad_ref[:1] += jnp.sum(through * active, axis=0, keepdims=True)
+            weighted = gated_grad * active * gain
+            grad = scale_ref[rows, slice(head, head + 1)] * (
+                weighted - unit * jnp.mean(weighted * unit, axis=1, keepdims=True)
+            )
+            grad_ref[rows, vals] = low(grad)
             share = tn(low(jnp.where(inside, grad, 0.0)), query)
             acc_ref[i] = share
 
@@ -407,6 +575,7 @@
                 local_ref[i, chunk] = tn(later[at], low(wide(query[at]) * jnp.exp(piece)))
         return carry
 
+    gain_grad_ref[...] = jnp.zeros_like(gain_grad_ref)
     lax.fori_loop(0, seqs, shares_of, 0)
 
     def local_of(seq, carry):
@@ -420,10 +589,10 @@
             keys = slice(head * HEAD_K, (head + 1) * HEAD_K)
             vals = slice(head * HEAD_V, (head + 1) * HEAD_V)
             cum = cum_ref[rows, keys]
-            query = wide(q_ref[rows, keys])
-            key = wide(k_ref[rows, keys])
-            value = v_ref[rows, vals]
-            grad = grad_ref[rows, vals]
+            query = wide(proj_ref[rows, query_columns(head)])
+            key = wide(proj_ref[rows, key_columns(head)])
+            value = proj_ref[rows, value_columns(head)]
+            grad = wide(grad_ref[rows, vals])
             later = low(jnp.where(inside, 0.0, grad))
             weights, edge = prefix_weights(cum, end_local, toks)
             prefix_state = prefix_state_ref[i]
@@ -492,7 +661,7 @@
                     + query[at] * dq_state
                     - key[at] * dk_state
                 )
-            dqkv_ref[rows, keys] = low(jnp.concatenate(dqs, axis=0))
+            dproj_ref[rows, query_columns(head)] = low(jnp.concatenate(dqs, axis=0))
             dk_part[rows, keys] = jnp.concatenate(dks, axis=0)
             dv_part[rows, vals] = jnp.concatenate(dvs, axis=0)
             turn = jnp.sum(wide(narrow_acc) * wide(prefix_state), axis=0, keepdims=True)
@@ -508,8 +677,8 @@
             keys = slice(head * HEAD_K, (head + 1) * HEAD_K)
             vals = slice(head * HEAD_V, (head + 1) * HEAD_V)
             cum = cum_ref[rows, keys]
-            key = wide(k_ref[rows, keys])
-            value = v_ref[rows, vals]
+            key = wide(proj_ref[rows, key_columns(head)])
+            value = proj_ref[rows, value_columns(head)]
 
             @pl.when(place < count - 1)
             def _():
@@ -529,10 +698,10 @@
 
             to_end = jnp.exp(last - cum)
             dk_more = to_end * nn(value, after)
-            dqkv_ref[rows, slice(KEYS + keys.start, KEYS + keys.stop)] = low(
+            dproj_ref[rows, key_columns(head)] = low(
                 dk_part[rows, keys] + dk_more
             )
-            dqkv_ref[rows, slice(2 * KEYS + vals.start, 2 * KEYS + vals.stop)] = low(
+            dproj_ref[rows, value_columns(head)] = low(
                 dv_part[rows, vals] + nt(low(key * to_end), after)
             )
             carry_row = jnp.sum(wide(after) * wide(state_ref[i, chunks]), axis=0, keepdims=True)
@@ -565,27 +734,30 @@
     return [pl.BlockSpec(memory_space=pltpu.VMEM)] * count
 
 
-def mix_forward(axes, prefix_len, queries, keys, values, decays):
-    tokens = queries.shape[0]
+def mix_forward(axes, prefix_len, projected, decays, group_gain):
+    tokens = projected.shape[0]
     seqs = prefix_len.shape[0]
-    pieces = seqs * HEADS
+    heads = seqs * HEADS
     chunks = tokens // seqs // CHUNK
-    state = (pieces, HEAD_V, HEAD_K)
+    state = (heads, HEAD_V, HEAD_K)
     return pl.pallas_call(
         partial(forward_kernel, axes),
         out_shape=(
-            jax.ShapeDtypeStruct((tokens, VALS), jnp.float32),
+            jax.ShapeDtypeStruct((tokens, VALS), jnp.bfloat16),
+            jax.ShapeDtypeStruct((tokens, VALS), jnp.bfloat16),
+            jax.ShapeDtypeStruct((tokens, 128), jnp.float32),
             jax.ShapeDtypeStruct((tokens, KEYS), jnp.float32),
-            jax.ShapeDtypeStruct((pieces, chunks + 1, HEAD_V, HEAD_K), jnp.bfloat16),
+            jax.ShapeDtypeStruct((heads, chunks + 1, HEAD_V, HEAD_K), jnp.bfloat16),
             jax.ShapeDtypeStruct(state, jnp.bfloat16),
         ),
-        in_specs=[pl.BlockSpec(memory_space=pltpu.SMEM)] + whole_specs(4),
-        out_specs=tuple(whole_specs(4)),
+        in_specs=[pl.BlockSpec(memory_space=pltpu.SMEM)] + whole_specs(3),
+        out_specs=tuple(whole_specs(6)),
         scratch_shapes=[
-            pltpu.VMEM((pieces, chunks, HEAD_V, HEAD_K), jnp.float32),
+            pltpu.VMEM((tokens, VALS), jnp.float32),
+            pltpu.VMEM((heads, chunks, HEAD_V, HEAD_K), jnp.float32),
             pltpu.VMEM(state, jnp.float32),
-            pltpu.VMEM((pieces, 8, HEAD_K), jnp.float32),
-            *line_scratch(pieces),
+            pltpu.VMEM((heads, 8, HEAD_K), jnp.float32),
+            *line_scratch(heads),
         ],
         compiler_params=pltpu.CompilerParams(
             collective_id=1, has_side_effects=True, vmem_limit_bytes=50 * 2**20
@@ -594,11 +766,13 @@
             flops=60_000_000_000, bytes_accessed=220_000_000, transcendentals=0
         ),
         name="mix_forward",
-    )(prefix_len, queries, keys, values, decays)
-
-
-def mix_backward(axes, prefix_len, queries, keys, values, cum, states, prefix_state, grad_mixed):
-    tokens = queries.shape[0]
+    )(prefix_len, projected, decays, group_gain)
+
+
+def mix_backward(
+    axes, prefix_len, projected, cum, states, prefix_state, gated_grad, unit, scale, group_gain
+):
+    tokens = projected.shape[0]
     seqs = prefix_len.shape[0]
     pieces = seqs * HEADS
     chunks = tokens // seqs // CHUNK
@@ -606,12 +780,14 @@
     return pl.pallas_call(
         partial(backward_kernel, axes),
         out_shape=(
-            jax.ShapeDtypeStruct((tokens, 2 * KEYS + VALS), jnp.bfloat16),
+            jax.ShapeDtypeStruct(projected.shape, jnp.bfloat16),
             jax.ShapeDtypeStruct((tokens, KEYS), jnp.float32),
+            jax.ShapeDtypeStruct((8, HEAD_V), jnp.float32),
         ),
-        in_specs=[pl.BlockSpec(memory_space=pltpu.SMEM)] + whole_specs(7),
-        out_specs=tuple(whole_specs(2)),
+        in_specs=[pl.BlockSpec(memory_space=pltpu.SMEM)] + whole_specs(8),
+        out_specs=tuple(whole_specs(3)),
         scratch_shapes=[
+            pltpu.VMEM((tokens, VALS), jnp.bfloat16),
             pltpu.VMEM((pieces, chunks, HEAD_V, HEAD_K), jnp.float32),
             pltpu.VMEM(state, jnp.float32),
             pltpu.VMEM((tokens, KEYS), jnp.float32),
@@ -626,7 +802,17 @@
             flops=60_000_000_000, bytes_accessed=220_000_000, transcendentals=0
         ),
         name="mix_backward",
-    )(prefix_len, queries, keys, values, cum, states, prefix_state, grad_mixed)
+    )(
+        prefix_len,
+        projected,
+        cum,
+        states,
+        prefix_state,
+        gated_grad,
+        unit,
+        scale,
+        group_gain,
+    )
 
 
 EXTRA = 128
@@ -651,16 +837,23 @@
     return tuple(names), tuple(sizes)
 
 
-def pack_mixer(norm1_gain, norm2_gain, query, key, value, gate, down, up, bias, group, out):
-    rows = query.shape[0]
-    small = jnp.zeros((rows, EXTRA), query.dtype)
-    small = small.at[:, :16].set(down)
-    small = small.at[:, 16].set(norm1_gain)
-    small = small.at[:, 17].set(norm2_gain)
-    small = small.at[: bias.shape[0], 18].set(bias)
-    small = small.at[: group.shape[0], 19].set(group)
-    small = small.at[:, 24:32].set(up.T.reshape(rows, 8))
-    return jnp.concatenate([query, key, value, gate, out, small], axis=1)
+def pack_small(norm1_gain, norm2_gain, down, up, bias, group):
+    rows = down.shape[0]
+
+    def column(vector):
+        return jnp.pad(vector, (0, rows - vector.shape[0]))[:, None]
+
+    pieces = [
+        down,
+        column(norm1_gain),
+        column(norm2_gain),
+        column(bias),
+        column(group),
+        jnp.zeros((rows, 4), down.dtype),
+        up.T.reshape(rows, 8),
+        jnp.zeros((rows, EXTRA - 32), down.dtype),
+    ]
+    return jnp.concatenate(pieces, axis=1)
 
 
 def unpack_small(small, devices):
@@ -902,6 +1095,16 @@
     return (first, second, last), (second, last, first), (last, first, second)
 
 
+def two_orders(names):
+    first, second, last = [name for name in names if name != "core"]
+    return (first, second, last), (second, last, first)
+
+
+def last_orders(names):
+    first, second, last = [name for name in names if name != "core"]
+    return (first, second, last), (second, first, last)
+
+
 def local(
     names,
     sizes,
@@ -925,67 +1128,50 @@
     out_grad,
 ):
     devices = int(np.prod(sizes))
-    mixer_full = lax.all_gather(
-        pack_mixer(
-            norm1_gain,
-            norm2_gain,
-            query_weight,
-            key_weight,
-            value_weight,
-            gate_weight,
-            decay_down,
-            decay_up,
-            decay_bias,
-            group_gain,
-            out_weight,
+    orders = chip_orders(names)
+    wide_order, long_order, late_order = (order[::-1] for order in orders)
+    small_shard = pack_small(norm1_gain, norm2_gain, decay_down, decay_up, decay_bias, group_gain)
+    first, small_full = gather_first(
+        names,
+        sizes,
+        (query_weight, key_weight, value_weight, gate_weight, small_shard),
+        (3072, EXTRA),
+        (
+            (3, 0, (0, 1024), (2048, 3072), wide_order),
+            (4, 1, (0, EXTRA), (0, EXTRA), wide_order),
+            (0, 0, (0, 128), (0, 128), wide_order),
+            (2, 0, (0, 1024), (1024, 2048), long_order),
+            (0, 0, (128, 384), (128, 384), long_order),
+            (1, 0, (0, 512), (512, 1024), late_order),
+            (0, 0, (384, 512), (384, 512), late_order),
         ),
-        names,
-        axis=0,
-        tiled=True,
-    )
-    ffn_full = lax.all_gather(
-        jnp.concatenate([ffn_gate, ffn_up, ffn_down.T], axis=1), names, axis=0, tiled=True
-    )
-    weight_q = mixer_full[:, :512]
-    weight_k = mixer_full[:, 512:1024]
-    weight_v = mixer_full[:, 1024:2048]
-    weight_g = mixer_full[:, 2048:3072]
-    weight_o = mixer_full[:, 3072:4096]
-    weight_down, gain_one, gain_two, bias_full, gain_group, weight_up = unpack_small(
-        mixer_full[:, 4096:], devices
-    )
+    )
+    ffn_shard = jnp.concatenate([ffn_gate, ffn_up, ffn_down.T, out_weight], axis=1)
+    ffn_full = lax.all_gather(ffn_shard, names, axis=0, tiled=True)
     weight_gate = ffn_full[:, :FF]
     weight_upper = ffn_full[:, FF : 2 * FF]
-    weight_lower = ffn_full[:, 2 * FF :].T
+    weight_lower = ffn_full[:, 2 * FF : 3 * FF].T
+    weight_o = ffn_full[:, 3 * FF :]
+    mixer_full = first.reshape(-1, 3072)
+    small_full = small_full.reshape(-1, EXTRA)
+    weight_down, gain_one, gain_two, bias_full, gain_group, weight_up = unpack_small(
+        small_full, devices
+    )
     seq_count, tok_count, feature_count = tokens.shape
-    resid_in = tokens.astype(jnp.float32)
+    rows = seq_count * tok_count
+    resid_in = tokens.reshape(rows, feature_count).astype(jnp.float32)
     scale_one = rms_scale(resid_in)
     unit_one = resid_in * scale_one
     normed = (unit_one * gain_one.astype(jnp.float32)).astype(jnp.bfloat16)
-    queries = project(normed, weight_q).astype(jnp.bfloat16)
-    key_matrix = project(normed, weight_k).astype(jnp.bfloat16)
-    value_matrix = project(normed, weight_v).astype(jnp.bfloat16)
-    gate_out = project(normed, weight_g)
+    projected = project(normed, mixer_full).astype(jnp.bfloat16)
     lowrank = project(normed, weight_down).astype(jnp.bfloat16)
     logits = project(lowrank, weight_up) + bias_full.astype(jnp.float32)
     decays = jax.nn.log_sigmoid(logits) / 16.0
-    rows = seq_count * tok_count
-    flat_q = queries.reshape(rows, KEYS)
-    flat_k = key_matrix.reshape(rows, KEYS)
-    flat_v = value_matrix.reshape(rows, VALS)
-    mixed, cum, states, prefix_state = mix_forward(
-        seq_axes, prefix_len, flat_q, flat_k, flat_v, decays.reshape(rows, KEYS)
-    )
-    mixed_heads = mixed.reshape(seq_count, tok_count, HEADS, HEAD_V)
-    scale_group = rms_scale(mixed_heads)
-    unit_group = mixed_heads * scale_group
-    normed_group = unit_group * gain_group.astype(jnp.float32)
-    swish_gate = jax.nn.silu(gate_out).reshape(seq_count, tok_count, HEADS, HEAD_V)
-    gated_rows = (
-        (normed_group * swish_gate).reshape(seq_count, tok_count, VALS).astype(jnp.bfloat16)
-    )
-    branch = project(gated_rows, weight_o)
-    resid_mid = resid_in + branch
+    wide_gain = jnp.broadcast_to(gain_group.astype(jnp.float32)[None], (8, HEAD_V))
+    gated_rows, unit_group, scale_group, cum, states, prefix_state = mix_forward(
+        seq_axes, prefix_len, projected, decays, wide_gain
+    )
+    resid_mid = resid_in + project(gated_rows, weight_o)
     scale_two = rms_scale(resid_mid)
     unit_two = resid_mid * scale_two
     normed_two = (unit_two * gain_two.astype(jnp.float32)).astype(jnp.bfloat16)
@@ -995,95 +1181,77 @@
     hidden = (gate_act * up_part).astype(jnp.bfloat16)
     ffn_out = project(hidden, weight_lower)
     layer_out = (resid_mid + ffn_out).astype(jnp.bfloat16)
+    out_grad = out_grad.reshape(rows, feature_count)
     grad_out = out_grad.astype(jnp.float32)
     grad_hidden = back_project(out_grad, weight_lower)
     grad_gate = (grad_hidden * up_part * silu_slope(gate_part)).astype(jnp.bfloat16)
     grad_up = (grad_hidden * gate_act).astype(jnp.bfloat16)
     grad_normed_two = back_project(grad_gate, weight_gate) + back_project(grad_up, weight_upper)
-    gain_two_grad = jnp.sum(grad_normed_two * unit_two, axis=(0, 1))
+    gain_two_grad = jnp.sum(grad_normed_two * unit_two, axis=0)
     grad_mid = grad_out + rms_back(
         grad_normed_two * gain_two.astype(jnp.float32), unit_two, scale_two
     )
     grad_branch = grad_mid.astype(jnp.bfloat16)
-    normed_halves = core_halves(normed.reshape(rows, -1), names, sizes)
-    two_halves = core_halves(normed_two.reshape(rows, -1), names, sizes)
-    gate_sum = pair_sum(two_halves, grad_gate.reshape(rows, FF))
-    up_sum = pair_sum(two_halves, grad_up.reshape(rows, FF))
-    down_sum = pair_sum(
-        core_halves(out_grad.reshape(rows, -1), names, sizes), hidden.reshape(rows, FF)
-    )
-    out_sum = pair_sum(
-        core_halves(gated_rows.reshape(rows, -1), names, sizes), grad_branch.reshape(rows, -1)
-    )
-    grad_gated = back_project(grad_branch, weight_o).reshape(seq_count, tok_count, HEADS, HEAD_V)
-    grad_normed_group = grad_gated * swish_gate
-    grad_swish = (grad_gated * normed_group).reshape(seq_count, tok_count, VALS)
-    grad_gate_out = (grad_swish * silu_slope(gate_out)).astype(jnp.bfloat16)
-    group_grad = jnp.sum(grad_normed_group * unit_group, axis=(0, 1, 2))
-    grad_mixed = rms_back(
-        grad_normed_group * gain_group.astype(jnp.float32), unit_group, scale_group
-    )
-    gate_out_sum = pair_sum(normed_halves, grad_gate_out.reshape(rows, VALS))
+    gated_grad = back_project(grad_branch, weight_o).astype(jnp.bfloat16)
+    two_halves = core_halves(normed_two, names, sizes)
+    gate_sum = pair_sum(two_halves, grad_gate)
+    up_sum = pair_sum(two_halves, grad_up)
+    down_sum = pair_sum(core_halves(out_grad, names, sizes), hidden)
+    out_sum = pair_sum(core_halves(gated_rows, names, sizes), grad_branch)
     groups = (
-        jnp.concatenate([gate_sum, out_sum, down_sum[:, 2048:2432]], axis=1),
-        jnp.concatenate([up_sum, gate_out_sum, down_sum[:, 2432:]], axis=1),
-        down_sum[:, :2048],
-    )
-    groups, grad_mixed = lax.optimization_barrier((groups, grad_mixed))
+        jnp.concatenate([gate_sum, out_sum, down_sum[:, :896]], axis=1),
+        jnp.concatenate([up_sum, down_sum[:, 896:]], axis=1),
+    )
+    groups, gated_grad = lax.optimization_barrier((groups, gated_grad))
     chips = [name for name in names if name != "core"]
-    orders = chip_orders(names)
-    lefts = [chips] * 3
+    orders = two_orders(names)
+    lefts = [chips] * 2
     groups = [by_chip(group, names, sizes) for group in groups]
     arrived = [pass_along(g, left, order[0]) for g, left, order in zip(groups, lefts, orders)]
-    grad_qkv, grad_decay = mix_backward(
+    grad_projected, grad_decay, group_grad = mix_backward(
         seq_axes,
         prefix_len,
-        flat_q,
-        flat_k,
-        flat_v,
+        projected,
         cum,
         states,
         prefix_state,
-        grad_mixed.reshape(rows, VALS),
-    )
-    arrived, grad_qkv, grad_decay = lax.optimization_barrier((arrived, grad_qkv, grad_decay))
-
-    def next_axis(groups, arrived, lefts, step):
-        taken = [
-            take_in(g, more, left, order[step])
-            for g, more, left, order in zip(groups, arrived, lefts, orders)
-        ]
-        lefts = [left for _, left in taken]
-        if step == 2:
-            return [total for total, _ in taken], None, lefts
-        groups = [total.astype(jnp.bfloat16) for total, _ in taken]
-        arrived = [
-            pass_along(g, left, order[step + 1]) for g, left, order in zip(groups, lefts, orders)
-        ]
-        return groups, arrived, lefts
-
-    groups, arrived, lefts = next_axis(groups, arrived, lefts, 0)
-    grad_logits = (
-        grad_decay.reshape(seq_count, tok_count, KEYS) * jax.nn.sigmoid(-logits) / 16.0
-    ).astype(jnp.bfloat16)
-    bias_grad = jnp.sum(grad_logits.astype(jnp.float32), axis=(0, 1))
-    up_rank_grad = weight_grad(lowrank, grad_logits)
+        gated_grad,
+        unit_group,
+        scale_group,
+        wide_gain,
+    )
+    arrived, grad_projected, grad_decay = lax.optimization_barrier(
+        (arrived, grad_projected, grad_decay)
+    )
+    taken = [
+        take_in(g, more, left, order[0])
+        for g, more, left, order in zip(groups, arrived, lefts, orders)
+    ]
+    groups = [total.astype(jnp.bfloat16) for total, _ in taken]
+    lefts = [left for _, left in taken]
+    arrived = [pass_along(g, left, order[1]) for g, left, order in zip(groups, lefts, orders)]
+    late = flat_grad(normed, grad_projected).astype(jnp.bfloat16)
+    grad_logits = (grad_decay * jax.nn.sigmoid(-logits) / 16.0).astype(jnp.bfloat16)
+    bias_grad = jnp.sum(grad_logits.astype(jnp.float32), axis=0)
+    up_rank_grad = flat_grad(lowrank, grad_logits)
     grad_lowrank = back_project(grad_logits, weight_up).astype(jnp.bfloat16)
-    down_rank_grad = weight_grad(normed, grad_lowrank)
-    grad_normed = (
-        back_project(grad_qkv.reshape(seq_count, tok_count, -1), mixer_full[:, :2048])
-        + back_project(grad_gate_out, weight_g)
-        + back_project(grad_lowrank, weight_down)
-    )
-    gain_one_grad = jnp.sum(grad_normed * unit_one, axis=(0, 1))
+    down_rank_grad = flat_grad(normed, grad_lowrank)
+    grad_normed = back_project(grad_projected, mixer_full) + back_project(
+        grad_lowrank, weight_down
+    )
+    gain_one_grad = jnp.sum(grad_normed * unit_one, axis=0)
     tokens_grad = grad_mid + rms_back(
         grad_normed * gain_one.astype(jnp.float32), unit_one, scale_one
     )
     small_grads = pack_small_grads(
-        down_rank_grad, gain_one_grad, gain_two_grad, bias_grad, group_grad, up_rank_grad, devices
-    )
-    late = flat_grad(normed.reshape(rows, -1), grad_qkv).astype(jnp.bfloat16)
-    small_grads = small_grads.astype(jnp.bfloat16)
+        down_rank_grad,
+        gain_one_grad,
+        gain_two_grad,
+        bias_grad,
+        group_grad[0],
+        up_rank_grad,
+        devices,
+    ).astype(jnp.bfloat16)
     arrived, late, small_grads, tokens_grad = lax.optimization_barrier(
         (arrived, late, small_grads, tokens_grad)
     )
@@ -1095,29 +1263,30 @@
     late = late.reshape(*sizes, own_rows, -1)
     small_grads = small_grads.reshape(*sizes, own_rows, -1)
     size_of = dict(zip(names, sizes))
+    ends = last_orders(names)
     jobs = [
         (which, columns, names, ("core", *order), which, columns)
         for which, columns, order in (
-            (3, (0, 896), orders[0]),
-            (3, (896, 1792), orders[1]),
-            (3, (1792, 2048), orders[2]),
-            (4, (0, EXTRA), orders[2]),
+            (2, (0, 1536), ends[0]),
+            (2, (1536, 3072), ends[1]),
+            (3, (0, EXTRA), ends[0]),
         )
     ] + [
         (i, (0, groups[i].shape[-1]), (order[2],), (order[2],), i, (0, groups[i].shape[-1]))
         for i, order in enumerate(orders)
     ]
-    first_group, second_group, third_group, mine, small = reduce_rest(
-        (*groups, late, small_grads), jobs, size_of, own_rows, (4224, 4224, 2048, 2048, EXTRA), 3
-    )
+    first_group, second_group, mine, small = reduce_rest(
+        (*groups, late, small_grads), jobs, size_of, own_rows, (4736, 4736, 3072, EXTRA), 3
+    )
+    shape = tokens.shape
     return (
-        layer_out,
-        tokens_grad,
+        layer_out.reshape(shape),
+        tokens_grad.reshape(shape),
         small[:, 16],
         mine[:, :512],
         mine[:, 512:1024],
         mine[:, 1024:2048],
-        second_group[:, FF : FF + VALS],
+        mine[:, 2048:],
         small[:, :16],
         small[:, 24:32].reshape(KEYS // devices, 16).T,
         small[: KEYS // devices, 18],
@@ -1126,9 +1295,7 @@
         small[:, 17],
         first_group[:, :FF],
         second_group[:, :FF],
-        jnp.concatenate(
-            [third_group, first_group[:, FF + VALS :], second_group[:, FF + VALS :]], axis=1
-        ).T,
+        jnp.concatenate([first_group[:, FF + VALS :], second_group[:, FF:]], axis=1).T,
     )
 
 

time: 737 us -> 572 us (0.78)
  waiting for transfers between devices: 92.3 us -> 3.48 us
  local copies, waits for them, and re-layouts: 86.5 us -> 48.9 us
  matrix products: 181 us -> 147 us
  Pallas kernels: 288 us -> 317 us
  other arithmetic: 51.7 us -> 24.4 us
    all_gather x2 -> x1, waiting for transfers between devices: 76.5 us -> 0.01 us  [local(): ffn_full = lax.all_gather(ffn_shard, names, axis=0, tiled=True)]
    pallas_call x0 -> x1, Pallas kernels: none -> 75.2 us  [gather_first(): pl.pallas_call(partial(gather_kernel, (names, sizes, len(shards), len(wid...]
    pallas_call x1, Pallas kernels: 134 us -> 101 us  [mix_forward(): pl.pallas_call(partial(forward_kernel, axes), out_shape=(jax.ShapeDtypeSt...]
    dot_general x20 -> x14, matrix products: 132 us -> 102 us  [the longest x7 58.7 us: project(): jnp.einsum('td,de->te', inputs, weight, preferred_element_type=jnp.float32)]
    pallas_call x1, Pallas kernels: 95.6 us -> 73.6 us  [mix_backward(): pl.pallas_call(partial(backward_kernel, axes), out_shape=(jax.ShapeDtypeS...]
    mul x3 -> x0, local copies, waits for them, and re-layouts: 14.6 us -> none  [the longest x2 8.83 us: local(): unit_group = mixed_heads * scale_group]
    ppermute x10 -> x6, waiting for transfers between devices: 15.8 us -> 3.45 us  [pass_along(): lax.ppermute(given, name, [(i, (i + shift) % size) for i in range(size)])]
    another operation x13 -> x0, other arithmetic: 11.3 us -> none
  transfers between devices with their start and end apart: 17 -> 11, of which waited for: 2 -> 1; matrix products, arithmetic and copies ran while one was open for 20% -> 23% of each run, Pallas kernels for 32% -> 44%
where the time goes in v4:
time: 572 us; the launch traced here: 565 us
  Pallas kernels  317 us (55%)
  matrix products  147 us (26%)
  local copies, waits for them, and re-layouts  48.9 us (9%)
  other arithmetic  24.4 us (4%)
  between operations  15.7 us (3%)
  starting transfers between devices  8.93 us (2%)
    pallas_call x1, Pallas kernels, mix_forward(): pl.pallas_call(partial(forward_kernel, axes), out_shape=(jax.ShapeDtypeSt...  101 us
    pallas_call x1, Pallas kernels, gather_first(): pl.pallas_call(partial(gather_kernel, (names, sizes, len(shards), len(wid...  75.2 us
    pallas_call x1, Pallas kernels, mix_backward(): pl.pallas_call(partial(backward_kernel, axes), out_shape=(jax.ShapeDtypeS...  73.6 us
    pallas_call x1, Pallas kernels, reduce_rest(): pl.pallas_call(partial(reduce_kernel, (len(arrays), jobs, sizes, slots)),...  66.4 us
    dot_general x7, matrix products, project(): jnp.einsum('td,de->te', inputs, weight, preferred_element_type=jnp.float32)  58.7 us
    dot_general x11, matrix products, flat_grad(): jnp.einsum('td,te->de', inputs, gradient, preferred_element_type=jnp.floa...  44.2 us
    dot_general x7, matrix products, back_project(): jnp.einsum('te,de->td', gradient, weight, preferred_element_type=jnp.floa...  43.7 us
    unnamed x145, local copies, waits for them, and re-layouts  12.2 us
  transfers between devices with their start and end apart: 11, of which 1 were waited for; matrix products, arithmetic and copies ran while one was open for 23% of the time, Pallas kernels for 44%

profile of v4, /device:TPU:0, one launch (start us, length us, event | category | flops | bytes accessed | tf_op | source)
XLA Modules:
  0.0 564.7 jit_solution(1850598500196706465)
XLA Ops:
  7.2 2.1 pad_maximum_fusion.4
  14.8 75.2 %gather_first.1 = (bf16[2,2,2,4,32,3072]{5,4,3,2,1,0:T(8,128)(2,1)}, bf16[2,2,2,4,32,128]{5,4,3,2,1,0:T(8,128)(2,1)}) custom-call(bf16[32,512]{1,0:T(8,128)(2,1)} %refs_0_.2, bf16[32,512]{1,0:T(8,128)(2,1)} %refs_1_.1, bf16[32,1024]{1,0:T(8,128)(2,1)} %refs_2_.1, bf16[32,1024]{1,0:T(8,128)(2,1)} %refs_3_.1, bf16[32,128]{1,0:T(8,128)(2,1)} %concatenate.37.refs_4_), custom_call_target="tpu_custom_call" | custom-call | tf_op jit(solution)/shard_map/gather_first/pallas_call | solution.py:272
  96.1 2.9 constant_dynamic-slice_fusion.9
  100.8 3.4 fusion.33
  104.2 8.8 %convolution_convert_fusion.1.refs_1_.proj_ref = bf16[1024,3072]{1,0:T(8,128)(2,1)} fusion(bf16[1024,1024]{1,0:T(8,128)(2,1)S(1)} %bitcast.138, bf16[1024,3072]{1,0:T(8,128)(2,1)S(1)} %bitcast.152), kind=kOutput, calls=%fused_computation.13 | convolution fusion | flops 6445596672 | bytes 14680064 | tf_op jit(solution)/shard_map/td,de->te/dot_general | solution.py:25
  113.0 101.3 %mix_forward.1 = (bf16[1024,1024]{1,0:T(8,128)(2,1)S(1)}, bf16[1024,1024]{1,0:T(8,128)(2,1)}, f32[1024,128]{1,0:T(8,128)S(1)}, f32[1024,512]{1,0:T(8,128)}, bf16...) custom-call(s32[4]{0:T(128)S(1)} %copy-done.1, ...), custom_call_target="tpu_custom_call" | custom-call | flops 60000002048 | bytes 220000000 | tf_op jit(solution)/shard_map/mix_forward/pallas_call | solution.py:743
  217.7 4.8 multiply_reduce_fusion.2
  222.6 2.1 copy-done.9
  228.6 8.9 %fusion.4 = f32[2816,1024]{0,1:T(8,128)} fusion(bf16[1024,1024]{1,0:T(8,128)(2,1)S(1)} %bitcast.136, bf16[1024,9472]{1,0:T(8,128)(2,1)S(1)} %copy-done.56), kind=kOutput, calls=%fused_computation.14 | convolution fusion | flops 5905580032 | bytes 19398656 | tf_op jit(solution)/shard_map/te,de->td/dot_general | solution.py:29
  237.5 8.8 %fusion.14 = f32[1024,2816]{1,0:T(8,128)} fusion(bf16[1024,1024]{1,0:T(8,128)(2,1)S(1)} %multiply_convert_fusion.1, bf16[1024,9472]{1,0:T(8,128)(2,1)S(1)} %copy-done.56), kind=kOutput, calls=%fused_computation.24 | convolution fusion | flops 5905580032 | bytes 19398656 | tf_op jit(solution)/shard_map/td,de->te/dot_general | solution.py:25
  246.3 21.3 %fusion.1 = (bf16[1024,2816]{1,0:T(8,128)(2,1)}, bf16[1024,2816]{1,0:T(8,128)(2,1)}, bf16[1024,2816]{1,0:T(8,128)(2,1)}) fusion(f32[2816,1024]{0,1:T(8,128)} %fusion.4, f32[1024,2816]{1,0:T(8,128)} %fusion.14, bf16[1024,1024]{1,0:T(8,128)(2,1)S(1)} %multiply_convert_fusion.1, bf16[1024,9472]{1,0:T(8,128)(2,1)} %all-gather.2.cloned.1.call-done), kind=kOutput, calls=%fused_computation.3 | convolution fusion | flops 5948833792 | bytes 48234496 | tf_op jit(solution)/shard_map/td,de->te/dot_general | solution.py:25
  267.7 6.4 %convolution_convert_fusion.3 = bf16[512,2816]{1,0:T(8,128)(2,1)S(1)} fusion(bf16[1024,2816]{1,0:T(8,128)(2,1)} %get-tuple-element.116, bf16[1024,128]{1,0:T(8,128)(2,1)S(1)} %copy-done.40, bf16[1024,128]{1,0:T(8,128)(2,1)S(1)} %copy-done.37, bf16[1024,128]{1,0:T(8,128)(2,1)S(1)} %copy-done.38, bf16[1024,128]{1,0:T(8,128)(2,1)S(1)} %copy-done.39), kind=kOutput, calls=%fused_computation.33 | convolution fusion | flops 2958426112 | bytes 9699328 | tf_op jit(solution)/shard_map/td,te->de/dot_general | solution.py:922
  274.3 4.8 convolution_convert_fusion.4
  279.1 3.8 convolution_convert_fusion.2
  283.0 8.3 %fusion.8 = f32[1024,1024]{1,0:T(8,128)S(1)} fusion(bf16[1024,2816]{1,0:T(8,128)(2,1)S(1)} %bitcast.158, bf16[1024,9472]{1,0:T(8,128)(2,1)} %all-gather.2.cloned.1.call-done), kind=kOutput, calls=%fused_computation.18 | convolution fusion | flops 5905580032 | bytes 15728640 | tf_op jit(solution)/shard_map/te,de->td/dot_general | solution.py:29
  291.3 10.9 %multiply_reduce_fusion = (bf16[1024]{0:T(1024)(128)(2,1)S(1)}, f32[1024]{0:T(1024)S(1)}, f32[1024,1024]{1,0:T(8,128)S(1)}) fusion(f32[1024,1024]{1,0:T(8,128)S(1)} %copy-done.10, f32[1024]{0:T(1024)S(1)} %add_rsqrt_fusion, f32[1024]{0:T(1024)S(1)} %bitcast.141, f32[1024,1024]{1,0:T(8,128)S(1)} %fusion.8, bf16[1024,2816]{1,0:T(8,128)(2,1)} %get-tuple-element.114, ...), kind=kOutput, calls=%fused_computation.52 | convolution fusion | flops 5912918016 | bytes 24131584 | tf_op jit(solution)/shard_map/te,de->td/dot_general | solution.py:29
  306.3 10.9 %add_convert_fusion.3 = bf16[1024,1024]{1,0:T(8,128)(2,1)} fusion(f32[1024,1024]{1,0:T(8,128)S(1)} %copy-done.10, bf16[1024,2816]{1,0:T(8,128)(2,1)} %get-tuple-element.116, bf16[1024,9472]{1,0:T(8,128)(2,1)} %all-gather.2.cloned.1.call-done), kind=kOutput, calls=%fused_computation.55 | convolution fusion | flops 5907677184 | bytes 17825792 | tf_op jit(solution)/shard_map/td,de->te/dot_general | solution.py:25
  318.1 5.5 convolution_convert_fusion.5.gated_grad_ref
  325.1 6.5 %add_convert_fusion.1 = bf16[512,2816]{1,0:T(8,128)(2,1)S(1)} fusion(bf16[512,2816]{1,0:T(8,128)(2,1)S(1)} %collective-permute-done.2, bf16[1024,2816]{1,0:T(8,128)(2,1)} %get-tuple-element.116, bf16[1024,128]{1,0:T(8,128)(2,1)S(1)} %copy-done.26, bf16[1024,128]{1,0:T(8,128)(2,1)S(1)} %copy-done.27, bf16[1024,128]{1,0:T(8,128)(2,1)S(1)} %copy-done.28, ...), kind=kOutput, calls=%fused_computation.10 | convolution fusion | flops 2961309696 | bytes 12582912 | tf_op jit(solution)/shard_map/td,te->de/dot_general | solution.py:922
  333.6 3.9 add_convert_fusion
  337.8 6.6 %add_convert_fusion.2 = bf16[512,2816]{1,0:T(8,128)(2,1)S(1)} fusion(bf16[512,2816]{1,0:T(8,128)(2,1)S(1)} %collective-permute-done, bf16[1024,2816]{1,0:T(8,128)(2,1)} %get-tuple-element.114, bf16[1024,128]{1,0:T(8,128)(2,1)S(1)} %copy-done.30, bf16[1024,128]{1,0:T(8,128)(2,1)S(1)} %copy-done.31, bf16[1024,128]{1,0:T(8,128)(2,1)S(1)} %copy-done.32, ...), kind=kOutput, calls=%fused_computation.11 | convolution fusion | flops 2961309696 | bytes 12582912 | tf_op jit(solution)/shard_map/td,te->de/dot_general | solution.py:922
  351.8 73.6 %mix_backward.1 = (bf16[1024,3072]{1,0:T(8,128)(2,1)}, f32[1024,512]{1,0:T(8,128)}, f32[8,256]{1,0:T(8,128)}) custom-call(s32[4]{0:T(128)} %prefix_ref.1, bf16[1024,3072]{1,0:T(8,128)(2,1)} %convolution_convert_fusion.1.refs_1_.proj_ref, f32[1024,512]{1,0:T(8,128)} %get-tuple-element.50.cum_ref, bf16[16,3,256,128]{3,2,1,0:T(8,128)(2,1)} %get-tuple-element.51.state_ref, ...), custom_call_target="tpu_custom_call" | custom-call | flops 60000002048 | bytes 220000000 | tf_op jit(solution)/shard_map/mix_backward/pallas_call | solution.py:780
  426.8 3.0 fusion.17
  431.8 3.0 fusion.16
  437.9 3.8 collective-permute-start.9
  441.7 8.9 %convolution_convert_fusion = bf16[1024,3072]{1,0:T(8,128)(2,1)} fusion(bf16[1024,1024]{1,0:T(8,128)(2,1)S(1)} %copy-done.8, bf16[1024,3072]{1,0:T(8,128)(2,1)S(1)} %copy-done.58), kind=kOutput, calls=%fused_computation.12 | convolution fusion | flops 6445596672 | bytes 14680064 | tf_op jit(solution)/shard_map/td,te->de/dot_general | solution.py:922
  452.7 9.0 %fusion.24 = (f32[1024]{0:T(1024)S(1)}, bf16[1024]{0:T(1024)(128)(2,1)S(1)}, f32[1024,1024]{1,0:T(8,128)}) fusion(bf16[4,256,1024]{2,1,0:T(8,128)(2,1)S(1)} %copy-done.5, f32[1024]{0:T(1024)S(1)} %copy-done.51, f32[1024]{0:T(1024)S(1)} %bitcast.144, f32[1024,1024]{1,0:T(8,128)S(1)} %fusion.78, bf16[1024,3072]{1,0:T(8,128)(2,1)S(1)} %copy-done.58, ...), kind=kOutput, calls=%fused_computation.45 | convolution fusion | flops 6450837504 | bytes 23083008 | tf_op jit(solution)/shard_map/te,de->td/dot_general | solution.py:29
  466.6 3.9 concatenate.47
  470.5 5.6 fusion.27
  476.1 3.4 collective-permute-done.8
  481.1 1.9 fusion.43.refs_1_
  483.0 66.4 %reduce_rest.1 = (f32[32,4736]{1,0:T(8,128)S(1)}, f32[32,4736]{1,0:T(8,128)S(1)}, f32[32,3072]{1,0:T(8,128)S(1)}, f32[32,128]{1,0:T(8,128)S(1)}) custom-call(bf16[4,32,4736]{2,1,0:T(8,128)(2,1)S(1)} %fusion.31.refs_0_, bf16[2,32,4736]{2,1,0:T(8,128)(2,1)S(1)} %fusion.43.refs_1_, bf16[2,2,2,4,32,3072]{5,4,3,2,1,0:T(8,128)(2,1)S(1)} %bitcast.122, ...), custom_call_target="tpu_custom_call" | custom-call | tf_op jit(solution)/shard_map/reduce_rest/pallas_call | solution.py:1080
  (247 shorter events, 59.1 us)
Async XLA Ops:
  7.2 85.2 %copy-start.4 = (bf16[4,256,1024]{2,1,0:T(8,128)(2,1)S(1)}, bf16[4,256,1024]{2,1,0:T(8,128)(2,1)}, u32[]{:S(2)}) copy-start(bf16[4,256,1024]{2,1,0:T(8,128)(2,1)} %param.17) | copy-start | bytes 6291460
  7.2 210.5 %all-gather.2.cloned.1.call-start = ((), (), s32[]{:S(2)}) async-start(), calls=%async_computation | async-start | bytes 20004864 | tf_op jit(solution)/shard_map/all_gather | solution.py:1150
  113.0 101.4 %copy-start = (f32[8,256]{1,0:T(8,128)}, f32[8,256]{1,0:T(8,128)S(1)}, u32[]{:S(2)}) copy-start(f32[8,256]{1,0:T(8,128)S(1)} %broadcast_in_dim.53.refs_3_.gain_ref) | copy-start | bytes 24580
  217.7 10.1 %copy-start.56 = (bf16[1024,9472]{1,0:T(8,128)(2,1)S(1)}, bf16[1024,9472]{1,0:T(8,128)(2,1)}, u32[]{:S(2)}) copy-start(bf16[1024,9472]{1,0:T(8,128)(2,1)} %all-gather.2.cloned.1.call-done) | copy-start | bytes 58195972
  246.3 21.4 %copy-start.37 = (bf16[1024,128]{1,0:T(8,128)(2,1)S(1)}, bf16[1024,128]{1,0:T(8,128)(2,1)}, u32[]{:S(2)}) copy-start(bf16[1024,128]{1,0:T(8,128)(2,1)} %get-tuple-element.139) | copy-start | bytes 786436
  246.3 21.4 %copy-start.38 = (bf16[1024,128]{1,0:T(8,128)(2,1)S(1)}, bf16[1024,128]{1,0:T(8,128)(2,1)}, u32[]{:S(2)}) copy-start(bf16[1024,128]{1,0:T(8,128)(2,1)} %get-tuple-element.140) | copy-start | bytes 786436
  246.3 21.4 %copy-start.39 = (bf16[1024,128]{1,0:T(8,128)(2,1)S(1)}, bf16[1024,128]{1,0:T(8,128)(2,1)}, u32[]{:S(2)}) copy-start(bf16[1024,128]{1,0:T(8,128)(2,1)} %get-tuple-element.141) | copy-start | bytes 786436
  246.3 21.4 %copy-start.40 = (bf16[1024,128]{1,0:T(8,128)(2,1)S(1)}, bf16[1024,128]{1,0:T(8,128)(2,1)}, u32[]{:S(2)}) copy-start(bf16[1024,128]{1,0:T(8,128)(2,1)} %get-tuple-element.145) | copy-start | bytes 786436
  267.7 11.4 %slice-start.7 = ((s8[5767168]{0:T(1024)(128)(4,1)}), s8[4194304]{0:T(1024)(128)(4,1)S(1)}, s32[]{:S(2)}) async-start(s8[5767168]{0:T(1024)(128)(4,1)} %bitcast.157), calls=%async_computation.8 | async-start | bytes 8388608
  274.1 50.8 %collective-permute-start.2 = (bf16[512,2816]{1,0:T(8,128)(2,1)S(1)}, bf16[512,2816]{1,0:T(8,128)(2,1)S(1)}, u32[]{:S(2)}, u32[]{:S(2)}) collective-permute-start(bf16[512,2816]{1,0:T(8,128)(2,1)S(1)} %convolution_convert_fusion.3), channel_id=1, source_target_pairs={{0,4},{4,0},{1,5},{5,1},{2,6},{6,2},{3,7},{7,3},{8,12},{12,8},{9,1... | collective-permute-start | bytes 8650760 | tf_op jit(solution)/shard_map/ppermute | solution.py:912
  291.3 10.9 %copy-start.18 = (bf16[4,256,1024]{2,1,0:T(8,128)(2,1)S(1)}, bf16[4,256,1024]{2,1,0:T(8,128)(2,1)}, u32[]{:S(2)}) copy-start(bf16[4,256,1024]{2,1,0:T(8,128)(2,1)} %param.33) | copy-start | bytes 6291460
  304.0 19.6 %copy-start.11 = (f32[1024,1024]{1,0:T(8,128)}, f32[1024,1024]{1,0:T(8,128)S(1)}, u32[]{:S(2)}) copy-start(f32[1024,1024]{1,0:T(8,128)S(1)} %multiply_add_fusion) | copy-start | bytes 12582916
  305.3 18.3 %collective-permute-start.1 = (bf16[512,1024]{1,0:T(8,128)(2,1)S(1)}, bf16[512,1024]{1,0:T(8,128)(2,1)S(1)}, u32[]{:S(2)}, u32[]{:S(2)}) collective-permute-start(bf16[512,1024]{1,0:T(8,128)(2,1)S(1)} %convolution_convert_fusion.6), channel_id=1, source_target_pairs={{0,4},{4,0},{1,5},{5,1},{2,6},{6,2},{3,7},{7,3},{8,12},{12,8},{9,1... | collective-permute-start | bytes 3145736 | tf_op jit(solution)/shard_map/ppermute | solution.py:912
  305.8 32.0 %collective-permute-start = (bf16[512,2816]{1,0:T(8,128)(2,1)}, bf16[512,2816]{1,0:T(8,128)(2,1)S(1)}, u32[]{:S(2)}, u32[]{:S(2)}) collective-permute-start(bf16[512,2816]{1,0:T(8,128)(2,1)} %convolution_convert_fusion.4), channel_id=1, source_target_pairs={{0,4},{4,0},{1,5},{5,1},{2,6},{6,2},{3,7},{7,3},{8,12},{12,8},{9,1... | collective-permute-start | bytes 8650760 | tf_op jit(solution)/shard_map/ppermute | solution.py:912
  305.9 25.9 %collective-permute-start.3 = (bf16[512,2816]{1,0:T(8,128)(2,1)S(1)}, bf16[512,2816]{1,0:T(8,128)(2,1)S(1)}, u32[]{:S(2)}, u32[]{:S(2)}) collective-permute-start(bf16[512,2816]{1,0:T(8,128)(2,1)S(1)} %convolution_convert_fusion.2), channel_id=1, source_target_pairs={{0,4},{4,0},{1,5},{5,1},{2,6},{6,2},{3,7},{7,3},{8,12},{12,8},{9,1... | collective-permute-start | bytes 8650760 | tf_op jit(solution)/shard_map/ppermute | solution.py:912
  346.6 80.2 %collective-permute-start.4 = (bf16[2,4,32,4736]{3,2,1,0:T(8,128)(2,1)}, bf16[2,4,32,4736]{3,2,1,0:T(8,128)(2,1)}, u32[]{:S(2)}, u32[]{:S(2)}) collective-permute-start(bf16[2,4,32,4736]{3,2,1,0:T(8,128)(2,1)} %dynamic-slice_bitcast_fusion), channel_id=1, source_target_pairs={{0,16},{16,0},{1,17},{17,1},{2,18},{18,2},{3,19},{19,3},{4,20},{20... | collective-permute-start | bytes 7274504 | tf_op jit(solution)/shard_map/ppermute | solution.py:938
  350.4 76.5 %collective-permute-start.5 = (bf16[2,4,32,4736]{3,2,0,1:T(8,128)(2,1)}, bf16[2,4,32,4736]{3,2,0,1:T(8,128)(2,1)}, u32[]{:S(2)}, u32[]{:S(2)}) collective-permute-start(bf16[2,4,32,4736]{3,2,0,1:T(8,128)(2,1)} %bitcast.118), channel_id=1, source_target_pairs={{0,8},{8,0},{1,9},{9,1},{2,10},{10,2},{3,11},{11,3},{4,12},{12,4},... | collective-permute-start | bytes 7274504 | tf_op jit(solution)/shard_map/ppermute | solution.py:938
  429.8 11.8 %copy-start.58 = (bf16[1024,3072]{1,0:T(8,128)(2,1)S(1)}, bf16[1024,3072]{1,0:T(8,128)(2,1)}, u32[]{:S(2)}) copy-start(bf16[1024,3072]{1,0:T(8,128)(2,1)} %get-tuple-element.60) | copy-start | bytes 18874372
  431.0 48.5 %collective-permute-start.6 = (bf16[4,32,4736]{2,1,0:T(8,128)(2,1)}, bf16[4,32,4736]{2,1,0:T(8,128)(2,1)}, u32[]{:S(2)}, u32[]{:S(2)}) collective-permute-start(bf16[4,32,4736]{2,1,0:T(8,128)(2,1)} %dynamic-slice_bitcast_fusion.1), channel_id=1, source_target_pairs={{0,8},{8,0},{1,9},{9,1},{2,10},{10,2},{3,11},{11,3},{4,12},{12,4},... | collective-permute-start | bytes 3637256 | tf_op jit(solution)/shard_map/ppermute | solution.py:938
  431.8 9.9 %copy-start.8 = (bf16[1024,1024]{1,0:T(8,128)(2,1)S(1)}, bf16[1024,1024]{1,0:T(8,128)(2,1)}, u32[]{:S(2)}) copy-start(bf16[1024,1024]{1,0:T(8,128)(2,1)} %copy-done.7) | copy-start | bytes 6291460
  431.8 20.8 %slice-start.5 = ((s8[6291456]{0:T(1024)(128)(4,1)}), s8[4194304]{0:T(1024)(128)(4,1)S(1)}, s32[]{:S(2)}) async-start(s8[6291456]{0:T(1024)(128)(4,1)} %bitcast.153), calls=%async_computation.6 | async-start | bytes 8388608
  437.5 38.5 %collective-permute-start.7 = (bf16[2,32,4736]{2,1,0:T(8,128)(2,1)}, bf16[2,32,4736]{2,1,0:T(8,128)(2,1)}, u32[]{:S(2)}, u32[]{:S(2)}) collective-permute-start(bf16[2,32,4736]{2,1,0:T(8,128)(2,1)} %get-tuple-element.121), channel_id=1, source_target_pairs={{0,1},{1,2},{2,3},{3,0},{4,5},{5,6},{6,7},{7,4},{8,9},{9,10},{10,1... | collective-permute-start | bytes 1818632 | tf_op jit(solution)/shard_map/ppermute | solution.py:938
  437.8 41.7 %collective-permute-start.8 = (bf16[2,32,4736]{2,1,0:T(8,128)(2,1)}, bf16[2,32,4736]{2,1,0:T(8,128)(2,1)}, u32[]{:S(2)}, u32[]{:S(2)}) collective-permute-start(bf16[2,32,4736]{2,1,0:T(8,128)(2,1)} %get-tuple-element.120), channel_id=1, source_target_pairs={{0,2},{1,3},{2,0},{3,1},{4,6},{5,7},{6,4},{7,5},{8,10},{9,11},{10,... | collective-permute-start | bytes 1818632 | tf_op jit(solution)/shard_map/ppermute | solution.py:938
  437.8 12.7 %copy-start.20 = (f32[1024,512]{1,0:T(8,128)S(1)}, f32[1024,512]{1,0:T(8,128)}, u32[]{:S(2)}) copy-start(f32[1024,512]{1,0:T(8,128)} %get-tuple-element.153) | copy-start | bytes 6291460
  437.9 12.7 %copy-start.21 = (f32[1024,512]{1,0:T(8,128)S(1)}, f32[1024,512]{1,0:T(8,128)}, u32[]{:S(2)}) copy-start(f32[1024,512]{1,0:T(8,128)} %get-tuple-element.61) | copy-start | bytes 6291460
  437.9 12.7 %copy-start.55 = (f32[512]{0:T(512)S(1)}, f32[512]{0:T(512)}, u32[]{:S(2)}) copy-start(f32[512]{0:T(512)} %copy-done.54) | copy-start | bytes 6148
  437.9 14.8 %slice-start.6 = ((s8[6291456]{0:T(1024)(128)(4,1)}), s8[2097152]{0:T(1024)(128)(4,1)S(1)}, s32[]{:S(2)}) async-start(s8[6291456]{0:T(1024)(128)(4,1)} %bitcast.153), calls=%async_computation.7 | async-start | bytes 4194304
  437.9 41.6 %collective-permute-start.9 = (bf16[2,32,4736]{2,1,0:T(8,128)(2,1)}, bf16[2,32,4736]{2,1,0:T(8,128)(2,1)}, u32[]{:S(2)}, u32[]{:S(2)}) collective-permute-start(bf16[2,32,4736]{2,1,0:T(8,128)(2,1)} %get-tuple-element.119), channel_id=1, source_target_pairs={{0,3},{1,0},{2,1},{3,2},{4,7},{5,4},{6,5},{7,6},{8,11},{9,8},{10,9... | collective-permute-start | bytes 1818632 | tf_op jit(solution)/shard_map/ppermute | solution.py:938
  452.7 9.0 %copy-start.49 = (bf16[1024,16]{0,1:T(8,128)(2,1)S(1)}, bf16[1024,16]{0,1:T(8,128)(2,1)}, u32[]{:S(2)}) copy-start(bf16[1024,16]{0,1:T(8,128)(2,1)} %copy-done.48) | copy-start | bytes 98308
  470.5 12.5 %slice-start = ((s8[6291456]{0:T(1024)(128)(4,1)}), s8[4194304]{0:T(1024)(128)(4,1)S(1)}, s32[]{:S(2)}) async-start(s8[6291456]{0:T(1024)(128)(4,1)} %bitcast.120), calls=%async_computation.1 | async-start | bytes 8388608
  470.5 9.0 %copy-start.14 = (bf16[2,4,32,4736]{3,2,1,0:T(8,128)(2,1)S(1)}, bf16[2,4,32,4736]{3,2,1,0:T(8,128)(2,1)}, u32[]{:S(2)}) copy-start(bf16[2,4,32,4736]{3,2,1,0:T(8,128)(2,1)} %copy-done.13) | copy-start | bytes 7274500
  470.5 12.5 %slice-start.1 = ((s8[6291456]{0:T(1024)(128)(4,1)}), s8[2097152]{0:T(1024)(128)(4,1)S(1)}, s32[]{:S(2)}) async-start(s8[6291456]{0:T(1024)(128)(4,1)} %bitcast.120), calls=%async_computation.2 | async-start | bytes 4194304
  (49 other events, 198.4 us)
Sparse Core Ops, SparseCore 0:
  11.4 169.1 all-gather.1

commit v5 on v4

--- a/solution.py
+++ b/solution.py
@@ -37,11 +37,6 @@
     return scale_rows * (
         grad_unit - unit_rows * jnp.mean(grad_unit * unit_rows, axis=-1, keepdims=True)
     )
-
-
-def silu_slope(values):
-    logistic = jax.nn.sigmoid(values)
-    return logistic * (1.0 + values * (1.0 - logistic))
 
 
 CHUNK = 128
@@ -815,6 +810,161 @@
     )
 
 
+FFN_BLOCK = 256
+FFN_ROWS = 512
+
+
+def ffn_kernel(
+    rows_ref,
+    grad_ref,
+    mine_ref,
+    other_ref,
+    grad_mine_ref,
+    grad_other_ref,
+    weight_ref,
+    out_ref,
+    drows_ref,
+    gate_sum_ref,
+    up_sum_ref,
+    down_sum_ref,
+    pair_slots,
+    down_slots,
+    hidden_ref,
+    dpair_ref,
+    turned,
+    given,
+    taken,
+    load_sem,
+    sent_sem,
+    got_sem,
+):
+    blocks = FF // FFN_BLOCK
+    tokens = rows_ref.shape[0]
+    other_core = {"core": 1 - lax.axis_index("core")}
+    barrier = pltpu.get_barrier_semaphore()
+    pl.semaphore_signal(barrier, inc=1, device_id=other_core, device_id_type=MESH)
+    pl.semaphore_wait(barrier, 1)
+    first, second = slice(0, FFN_BLOCK), slice(FFN_BLOCK, 2 * FFN_BLOCK)
+
+    def load(block, part):
+        begin = pl.multiple_of(part * FF + block * FFN_BLOCK, FFN_BLOCK)
+        slot = lax.rem(block, 2)
+        target = down_slots.at[slot] if part == 2 else pair_slots.at[slot, :, (first, second)[part]]
+        return pltpu.make_async_copy(
+            weight_ref.at[:, pl.ds(begin, FFN_BLOCK)], target, load_sem.at[slot, part]
+        )
+
+    def give(block):
+        return pltpu.make_async_remote_copy(
+            src_ref=given.at[lax.rem(block, 2)],
+            dst_ref=taken.at[block],
+            send_sem=sent_sem.at[block],
+            recv_sem=got_sem.at[block],
+            device_id=other_core,
+            device_id_type=MESH,
+        )
+
+    def take(block):
+        give(block).wait_recv()
+        columns = pl.ds(pl.multiple_of(block * FFN_BLOCK, FFN_BLOCK), FFN_BLOCK)
+        for part, sum_ref in enumerate((gate_sum_ref, up_sum_ref, down_sum_ref)):
+            at = slice(part * FFN_BLOCK, (part + 1) * FFN_BLOCK)
+            sum_ref[:, columns] = low(wide(sum_ref[:, columns]) + wide(taken[block, :, at]))
+
+    for part in range(3):
+        load(0, part).start()
+
+    def turn(i, carry):
+        begin = pl.multiple_of(i * FFN_BLOCK, FFN_BLOCK)
+        at = pl.ds(begin, FFN_BLOCK)
+        for which, ref in enumerate((mine_ref, other_ref, grad_mine_ref, grad_other_ref)):
+            turned[which, :, at] = jnp.transpose(ref[at, :])
+        out_ref[at, :] = jnp.zeros((FFN_BLOCK, out_ref.shape[1]), jnp.float32)
+        drows_ref[at, :] = jnp.zeros((FFN_BLOCK, out_ref.shape[1]), jnp.float32)
+        return carry
+
+    lax.fori_loop(0, tokens // FFN_BLOCK, turn, 0)
+
+    def one(block, carry):
+        slot = lax.rem(block, 2)
+
+        @pl.when(block < blocks - 1)
+        def _():
+            for part in range(3):
+                load(block + 1, part).start()
+
+        @pl.when(block > 1)
+        def _():
+            give(block - 2).wait_send()
+
+        for part in range(3):
+            load(block, part).wait()
+        columns = pl.ds(pl.multiple_of(block * FFN_BLOCK, FFN_BLOCK), FFN_BLOCK)
+        for tile in range(tokens // FFN_ROWS):
+            at = slice(tile * FFN_ROWS, (tile + 1) * FFN_ROWS)
+            both = nn(rows_ref[at], pair_slots[slot])
+            dhidden = nn(grad_ref[at], down_slots[slot])
+            gate = both[:, first]
+            up = both[:, second]
+            logistic = 0.5 * jnp.tanh(0.5 * gate) + 0.5
+            active = gate * logistic
+            hidden_ref[at] = low(active * up)
+            dpair_ref[at, first] = low(dhidden * up * (logistic + active * (1.0 - logistic)))
+            dpair_ref[at, second] = low(dhidden * active)
+        for tile in range(tokens // FFN_ROWS):
+            at = slice(tile * FFN_ROWS, (tile + 1) * FFN_ROWS)
+            out_ref[at] += nt(hidden_ref[at], down_slots[slot])
+            drows_ref[at] += nt(dpair_ref[at], pair_slots[slot])
+        given[slot, :, : 2 * FFN_BLOCK] = low(nn(turned[1], dpair_ref[...]))
+        given[slot, :, 2 * FFN_BLOCK :] = low(nn(turned[3], hidden_ref[...]))
+        give(block).start()
+        pair = nn(turned[0], dpair_ref[...])
+        gate_sum_ref[:, columns] = low(pair[:, first])
+        up_sum_ref[:, columns] = low(pair[:, second])
+        down_sum_ref[:, columns] = low(nn(turned[2], hidden_ref[...]))
+
+        @pl.when(block > 0)
+        def _():
+            take(block - 1)
+
+        return carry
+
+    lax.fori_loop(0, blocks, one, 0)
+    take(blocks - 1)
+    give(blocks - 2).wait_send()
+    give(blocks - 1).wait_send()
+
+
+def ffn_both(rows, grad, row_halves, grad_halves, weights):
+    tokens, width = rows.shape
+    half = width // 2
+    blocks = FF // FFN_BLOCK
+    share = jax.ShapeDtypeStruct((half, FF), jnp.bfloat16)
+    total = jax.ShapeDtypeStruct((tokens, width), jnp.float32)
+    return pl.pallas_call(
+        ffn_kernel,
+        out_shape=(total, total, share, share, share),
+        in_specs=whole_specs(6) + [pl.BlockSpec(memory_space=pl.ANY)],
+        out_specs=tuple(whole_specs(5)),
+        scratch_shapes=[
+            pltpu.VMEM((2, width, 2 * FFN_BLOCK), jnp.bfloat16),
+            pltpu.VMEM((2, width, FFN_BLOCK), jnp.bfloat16),
+            pltpu.VMEM((tokens, FFN_BLOCK), jnp.bfloat16),
+            pltpu.VMEM((tokens, 2 * FFN_BLOCK), jnp.bfloat16),
+            pltpu.VMEM((4, half, tokens), jnp.bfloat16),
+            pltpu.VMEM((2, half, 3 * FFN_BLOCK), jnp.bfloat16),
+            pltpu.VMEM((blocks, half, 3 * FFN_BLOCK), jnp.bfloat16),
+            pltpu.SemaphoreType.DMA((2, 3)),
+            pltpu.SemaphoreType.DMA((blocks,)),
+            pltpu.SemaphoreType.DMA((blocks,)),
+        ],
+        compiler_params=pltpu.CompilerParams(
+            collective_id=5, has_side_effects=True, vmem_limit_bytes=58 * 2**20
+        ),
+        name="ffn_both",
+    )(rows, grad, *row_halves, *grad_halves, weights)
+
+
 EXTRA = 128
 
 
@@ -1148,9 +1298,6 @@
     )
     ffn_shard = jnp.concatenate([ffn_gate, ffn_up, ffn_down.T, out_weight], axis=1)
     ffn_full = lax.all_gather(ffn_shard, names, axis=0, tiled=True)
-    weight_gate = ffn_full[:, :FF]
-    weight_upper = ffn_full[:, FF : 2 * FF]
-    weight_lower = ffn_full[:, 2 * FF : 3 * FF].T
     weight_o = ffn_full[:, 3 * FF :]
     mixer_full = first.reshape(-1, 3072)
     small_full = small_full.reshape(-1, EXTRA)
@@ -1175,28 +1322,22 @@
     scale_two = rms_scale(resid_mid)
     unit_two = resid_mid * scale_two
     normed_two = (unit_two * gain_two.astype(jnp.float32)).astype(jnp.bfloat16)
-    gate_part = project(normed_two, weight_gate)
-    up_part = project(normed_two, weight_upper)
-    gate_act = jax.nn.silu(gate_part)
-    hidden = (gate_act * up_part).astype(jnp.bfloat16)
-    ffn_out = project(hidden, weight_lower)
-    layer_out = (resid_mid + ffn_out).astype(jnp.bfloat16)
     out_grad = out_grad.reshape(rows, feature_count)
     grad_out = out_grad.astype(jnp.float32)
-    grad_hidden = back_project(out_grad, weight_lower)
-    grad_gate = (grad_hidden * up_part * silu_slope(gate_part)).astype(jnp.bfloat16)
-    grad_up = (grad_hidden * gate_act).astype(jnp.bfloat16)
-    grad_normed_two = back_project(grad_gate, weight_gate) + back_project(grad_up, weight_upper)
+    ffn_out, grad_normed_two, gate_sum, up_sum, down_sum = ffn_both(
+        normed_two,
+        out_grad,
+        core_halves(normed_two, names, sizes),
+        core_halves(out_grad, names, sizes),
+        ffn_full,
+    )
+    layer_out = (resid_mid + ffn_out).astype(jnp.bfloat16)
     gain_two_grad = jnp.sum(grad_normed_two * unit_two, axis=0)
     grad_mid = grad_out + rms_back(
         grad_normed_two * gain_two.astype(jnp.float32), unit_two, scale_two
     )
     grad_branch = grad_mid.astype(jnp.bfloat16)
     gated_grad = back_project(grad_branch, weight_o).astype(jnp.bfloat16)
-    two_halves = core_halves(normed_two, names, sizes)
-    gate_sum = pair_sum(two_halves, grad_gate)
-    up_sum = pair_sum(two_halves, grad_up)
-    down_sum = pair_sum(core_halves(out_grad, names, sizes), hidden)
     out_sum = pair_sum(core_halves(gated_rows, names, sizes), grad_branch)
     groups = (
         jnp.concatenate([gate_sum, out_sum, down_sum[:, :896]], axis=1),

time: 572 us -> 556 us (0.972)
  matrix products: 147 us -> 47.4 us
  Pallas kernels: 317 us -> 400 us
  other arithmetic: 24.4 us -> 34.2 us
    pallas_call x0 -> x1, Pallas kernels: none -> 78 us  [ffn_both(): pl.pallas_call(ffn_kernel, out_shape=(total, total, share, share, share),...]
    dot_general x7 -> x4, matrix products: 58.7 us -> 17.7 us  [project(): jnp.einsum('td,de->te', inputs, weight, preferred_element_type=jnp.float32)]
    dot_general x11 -> x5, matrix products: 44.2 us -> 12.3 us  [flat_grad(): jnp.einsum('td,te->de', inputs, gradient, preferred_element_type=jnp.floa...]
    dot_general x7 -> x4, matrix products: 43.7 us -> 17.4 us  [back_project(): jnp.einsum('te,de->td', gradient, weight, preferred_element_type=jnp.floa...]
    unnamed x145 -> x101, local copies, waits for them, and re-layouts: 12.2 us -> 9.05 us
  transfers between devices with their start and end apart: 11 -> 8, of which waited for: 1 -> 1; matrix products, arithmetic and copies ran while one was open for 23% -> 14% of each run, Pallas kernels for 44% -> 47%
where the time goes in v5:
time: 556 us; the launch traced here: 549 us
  Pallas kernels  400 us (72%)
  matrix products  47.4 us (9%)
  local copies, waits for them, and re-layouts  44.3 us (8%)
  other arithmetic  34.2 us (6%)
  between operations  15.3 us (3%)
  starting transfers between devices  7.7 us (1%)
    pallas_call x1, Pallas kernels, mix_forward(): pl.pallas_call(partial(forward_kernel, axes), out_shape=(jax.ShapeDtypeSt...  106 us
    pallas_call x1, Pallas kernels, ffn_both(): pl.pallas_call(ffn_kernel, out_shape=(total, total, share, share, share),...  78 us
    pallas_call x1, Pallas kernels, gather_first(): pl.pallas_call(partial(gather_kernel, (names, sizes, len(shards), len(wid...  75.2 us
    pallas_call x1, Pallas kernels, mix_backward(): pl.pallas_call(partial(backward_kernel, axes), out_shape=(jax.ShapeDtypeS...  74.4 us
    pallas_call x1, Pallas kernels, reduce_rest(): pl.pallas_call(partial(reduce_kernel, (len(arrays), jobs, sizes, slots)),...  66.1 us
    dot_general x4, matrix products, project(): jnp.einsum('td,de->te', inputs, weight, preferred_element_type=jnp.float32)  17.7 us
    dot_general x4, matrix products, back_project(): jnp.einsum('te,de->td', gradient, weight, preferred_element_type=jnp.floa...  17.4 us
    dot_general x5, matrix products, flat_grad(): jnp.einsum('td,te->de', inputs, gradient, preferred_element_type=jnp.floa...  12.3 us
  transfers between devices with their start and end apart: 8, of which 1 were waited for; matrix products, arithmetic and copies ran while one was open for 14% of the time, Pallas kernels for 47%

profile of v5, /device:TPU:0, one launch (start us, length us, event | category | flops | bytes accessed | tf_op | source)
XLA Modules:
  0.0 548.9 jit_solution(8682825699058518778)
XLA Ops:
  7.2 2.1 pad_maximum_fusion.6
  14.8 75.2 %gather_first.1 = (bf16[2,2,2,4,32,3072]{5,4,3,2,1,0:T(8,128)(2,1)}, bf16[2,2,2,4,32,128]{5,4,3,2,1,0:T(8,128)(2,1)}) custom-call(bf16[32,512]{1,0:T(8,128)(2,1)} %refs_0_.2, bf16[32,512]{1,0:T(8,128)(2,1)} %refs_1_.1, bf16[32,1024]{1,0:T(8,128)(2,1)} %refs_2_.1, bf16[32,1024]{1,0:T(8,128)(2,1)} %refs_3_.1, bf16[32,128]{1,0:T(8,128)(2,1)} %concatenate.37.refs_4_), custom_call_target="tpu_custom_call" | custom-call | tf_op jit(solution)/shard_map/gather_first/pallas_call | solution.py:267
  96.1 3.4 fusion.17
  99.5 9.0 %convolution_convert_fusion.1.refs_1_.proj_ref = bf16[1024,3072]{1,0:T(8,128)(2,1)} fusion(bf16[1024,1024]{1,0:T(8,128)(2,1)S(1)} %bitcast.117, bf16[1024,3072]{1,0:T(8,128)(2,1)S(1)} %bitcast.132), kind=kOutput, calls=%fused_computation.2 | convolution fusion | flops 6445596672 | bytes 14680064 | tf_op jit(solution)/shard_map/td,de->te/dot_general | solution.py:25
  108.5 105.9 %mix_forward.1 = (bf16[1024,1024]{1,0:T(8,128)(2,1)S(1)}, bf16[1024,1024]{1,0:T(8,128)(2,1)}, f32[1024,128]{1,0:T(8,128)S(1)}, f32[1024,512]{1,0:T(8,128)}, bf16...) custom-call(s32[4]{0:T(128)S(1)} %copy-done.1, ...), custom_call_target="tpu_custom_call" | custom-call | flops 60000002048 | bytes 220000000 | tf_op jit(solution)/shard_map/mix_forward/pallas_call | solution.py:738
  214.5 2.0 constant_dynamic-slice_fusion.9
  218.6 4.7 multiply_reduce_fusion.2
  223.8 1.6 copy-done.4
  225.9 1.6 pad_maximum_fusion.2
  227.5 78.0 %ffn_both.1 = (f32[1024,1024]{1,0:T(8,128)}, f32[1024,1024]{1,0:T(8,128)}, bf16[512,2816]{1,0:T(8,128)(2,1)}, bf16[512,2816]{1,0:T(8,128)(2,1)}, bf16[512,2816]{1,0:T(8,128)(2,1)}) custom-call(bf16[1024,1024]{1,0:T(8,128)(2,1)} %copy-done.11, bf16[1024,1024]{1,0:T(8,128)(2,1)} %bitcast.107, bf16[1024,512]{1,0:T(8,128)(2,1)} %get-tuple-element.174.mine_ref, ...), custom_call_target="tpu_custom_call" | custom-call | tf_op jit(solution)/shard_map/ffn_both/pallas_call | solution.py:944
  305.5 1.4 slice.83
  306.9 1.8 slice.84
  308.8 3.5 multiply_reduce_fusion
  312.8 4.3 multiply_add_fusion
  317.2 1.3 convolution_convert_fusion.3
  319.4 5.4 convolution_convert_fusion.2.gated_grad_ref
  328.5 1.8 dynamic-slice_bitcast_fusion
  330.3 1.7 collective-permute-start.1
  332.4 1.6 copy.71
  334.0 1.4 collective-permute-start.2
  335.4 74.4 %mix_backward.1 = (bf16[1024,3072]{1,0:T(8,128)(2,1)}, f32[1024,512]{1,0:T(8,128)}, f32[8,256]{1,0:T(8,128)}) custom-call(s32[4]{0:T(128)} %prefix_ref.1, bf16[1024,3072]{1,0:T(8,128)(2,1)} %convolution_convert_fusion.1.refs_1_.proj_ref, f32[1024,512]{1,0:T(8,128)} %get-tuple-element.60.cum_ref, bf16[16,3,256,128]{3,2,1,0:T(8,128)(2,1)} %get-tuple-element.61.state_ref, ...), custom_call_target="tpu_custom_call" | custom-call | flops 60000002048 | bytes 220000000 | tf_op jit(solution)/shard_map/mix_backward/pallas_call | solution.py:775
  411.3 3.0 fusion.1
  416.1 3.0 fusion
  419.2 1.4 copy-done.16
  421.9 3.9 collective-permute-start.6
  425.8 9.1 %convolution_convert_fusion = bf16[1024,3072]{1,0:T(8,128)(2,1)} fusion(bf16[1024,1024]{1,0:T(8,128)(2,1)S(1)} %copy-done.10, bf16[1024,3072]{1,0:T(8,128)(2,1)S(1)} %copy-done.40), kind=kOutput, calls=%fused_computation.1 | convolution fusion | flops 6445596672 | bytes 14680064 | tf_op jit(solution)/shard_map/td,te->de/dot_general | solution.py:1072
  437.8 10.8 %fusion.8 = (f32[1024]{0:T(1024)S(1)}, bf16[1024]{0:T(1024)(128)(2,1)S(1)}, f32[1024,1024]{1,0:T(8,128)}) fusion(bf16[4,256,1024]{2,1,0:T(8,128)(2,1)S(1)} %copy-done.7, f32[1024]{0:T(1024)S(1)} %copy-done.35, f32[1024]{0:T(1024)S(1)} %bitcast.124, f32[1024,1024]{1,0:T(8,128)S(1)} %fusion.40, bf16[1024,3072]{1,0:T(8,128)(2,1)} %get-tuple-element.70, ...), kind=kOutput, calls=%fused_computation.19 | convolution fusion | flops 6450837504 | bytes 23083008 | tf_op jit(solution)/shard_map/te,de->td/dot_general | solution.py:29
  453.5 4.0 concatenate.47
  457.5 6.1 %fusion.11 = f32[1024,1024]{1,0:T(8,128)} fusion(f32[1024,1024]{1,0:T(8,128)} %copy-done.15, bf16[4,256,1024]{2,1,0:T(8,128)(2,1)} %param.17, f32[1024,1024]{1,0:T(8,128)} %get-tuple-element.165, f32[1024]{0:T(1024)S(1)} %broadcast_multiply_fusion, f32[1024]{0:T(1024)S(1)} %copy-done.35, f32[1024]{0:T(1024)S(1)} %bitcast.125), kind=kLoop, calls=%fused_computation.22 | loop fusion | flops 7340032 | bytes 14692352 | tf_op jit(solution)/shard_map/add | solution.py:1384
  464.0 1.6 fusion.15.refs_0_
  465.6 1.9 fusion.22.refs_1_
  467.5 66.1 %reduce_rest.1 = (f32[32,4736]{1,0:T(8,128)S(1)}, f32[32,4736]{1,0:T(8,128)S(1)}, f32[32,3072]{1,0:T(8,128)S(1)}, f32[32,128]{1,0:T(8,128)S(1)}) custom-call(bf16[4,32,4736]{2,1,0:T(8,128)(2,1)S(1)} %fusion.15.refs_0_, bf16[2,32,4736]{2,1,0:T(8,128)(2,1)S(1)} %fusion.22.refs_1_, bf16[2,2,2,4,32,3072]{5,4,3,2,1,0:T(8,128)(2,1)S(1)} %bitcast.101, ...), custom_call_target="tpu_custom_call" | custom-call | tf_op jit(solution)/shard_map/reduce_rest/pallas_call | solution.py:1230
  (186 shorter events, 40.5 us)
Async XLA Ops:
  7.2 85.2 %copy-start.6 = (bf16[4,256,1024]{2,1,0:T(8,128)(2,1)S(1)}, bf16[4,256,1024]{2,1,0:T(8,128)(2,1)}, u32[]{:S(2)}) copy-start(bf16[4,256,1024]{2,1,0:T(8,128)(2,1)} %param.17) | copy-start | bytes 6291460
  7.2 211.4 %all-gather.2.cloned.1.call-start = ((), (), s32[]{:S(2)}) async-start(), calls=%async_computation | async-start | bytes 20004864 | tf_op jit(solution)/shard_map/all_gather | solution.py:1300
  92.4 3.6 copy-start.38
  94.8 4.7 slice-start.2
  95.4 4.1 copy-start.32
  95.4 4.1 slice-start.3
  99.5 9.0 %copy-start.1 = (s32[4]{0:T(128)S(1)}, s32[4]{0:T(128)}, u32[]{:S(2)}) copy-start(s32[4]{0:T(128)} %prefix_ref.1) | copy-start | bytes 52
  108.5 105.9 %copy-start = (f32[8,256]{1,0:T(8,128)}, f32[8,256]{1,0:T(8,128)S(1)}, u32[]{:S(2)}) copy-start(f32[8,256]{1,0:T(8,128)S(1)} %broadcast_in_dim.53.refs_3_.gain_ref) | copy-start | bytes 24580
  108.5 106.0 %copy-start.12 = (bf16[4,256,1024]{2,1,0:T(8,128)(2,1)S(1)}, bf16[4,256,1024]{2,1,0:T(8,128)(2,1)}, u32[]{:S(2)}) copy-start(bf16[4,256,1024]{2,1,0:T(8,128)(2,1)} %param.33) | copy-start | bytes 6291460
  308.8 4.1 copy-start.14
  317.2 8.1 %copy-start.15 = (f32[1024,1024]{1,0:T(8,128)}, f32[1024,1024]{1,0:T(8,128)S(1)}, u32[]{:S(2)}) copy-start(f32[1024,1024]{1,0:T(8,128)S(1)} %get-tuple-element.126) | copy-start | bytes 12582916
  318.4 6.8 %collective-permute-start = (bf16[512,1024]{1,0:T(8,128)(2,1)S(1)}, bf16[512,1024]{1,0:T(8,128)(2,1)S(1)}, u32[]{:S(2)}, u32[]{:S(2)}) collective-permute-start(bf16[512,1024]{1,0:T(8,128)(2,1)S(1)} %convolution_convert_fusion.3), channel_id=1, source_target_pairs={{0,4},{4,0},{1,5},{5,1},{2,6},{6,2},{3,7},{7,3},{8,12},{12,8},{9,1... | collective-permute-start | bytes 3145736 | tf_op jit(solution)/shard_map/ppermute | solution.py:1062
  319.4 5.4 copy-start.22
  328.5 4.0 copy-start.8
  330.3 81.0 %collective-permute-start.1 = (bf16[2,4,32,4736]{3,2,1,0:T(8,128)(2,1)}, bf16[2,4,32,4736]{3,2,1,0:T(8,128)(2,1)}, u32[]{:S(2)}, u32[]{:S(2)}) collective-permute-start(bf16[2,4,32,4736]{3,2,1,0:T(8,128)(2,1)} %dynamic-slice_bitcast_fusion), channel_id=1, source_target_pairs={{0,16},{16,0},{1,17},{17,1},{2,18},{18,2},{3,19},{19,3},{4,20},{20... | collective-permute-start | bytes 7274504 | tf_op jit(solution)/shard_map/ppermute | solution.py:1088
  334.0 77.3 %collective-permute-start.2 = (bf16[2,4,32,4736]{3,2,0,1:T(8,128)(2,1)}, bf16[2,4,32,4736]{3,2,0,1:T(8,128)(2,1)}, u32[]{:S(2)}, u32[]{:S(2)}) collective-permute-start(bf16[2,4,32,4736]{3,2,0,1:T(8,128)(2,1)} %bitcast.97), channel_id=1, source_target_pairs={{0,8},{8,0},{1,9},{9,1},{2,10},{10,2},{3,11},{11,3},{4,12},{12,4},... | collective-permute-start | bytes 7274504 | tf_op jit(solution)/shard_map/ppermute | solution.py:1088
  414.3 11.5 %copy-start.40 = (bf16[1024,3072]{1,0:T(8,128)(2,1)S(1)}, bf16[1024,3072]{1,0:T(8,128)(2,1)}, u32[]{:S(2)}) copy-start(bf16[1024,3072]{1,0:T(8,128)(2,1)} %get-tuple-element.70) | copy-start | bytes 18874372
  415.4 48.6 %collective-permute-start.3 = (bf16[4,32,4736]{2,1,0:T(8,128)(2,1)}, bf16[4,32,4736]{2,1,0:T(8,128)(2,1)}, u32[]{:S(2)}, u32[]{:S(2)}) collective-permute-start(bf16[4,32,4736]{2,1,0:T(8,128)(2,1)} %dynamic-slice_bitcast_fusion.1), channel_id=1, source_target_pairs={{0,8},{8,0},{1,9},{9,1},{2,10},{10,2},{3,11},{11,3},{4,12},{12,4},... | collective-permute-start | bytes 3637256 | tf_op jit(solution)/shard_map/ppermute | solution.py:1088
  416.1 20.8 %slice-start.4 = ((s8[6291456]{0:T(1024)(128)(4,1)}), s8[4194304]{0:T(1024)(128)(4,1)S(1)}, s32[]{:S(2)}) async-start(s8[6291456]{0:T(1024)(128)(4,1)} %bitcast.133), calls=%async_computation.5 | async-start | bytes 8388608
  420.6 5.2 copy-start.10
  421.9 41.8 %collective-permute-start.4 = (bf16[2,32,4736]{2,1,0:T(8,128)(2,1)}, bf16[2,32,4736]{2,1,0:T(8,128)(2,1)}, u32[]{:S(2)}, u32[]{:S(2)}) collective-permute-start(bf16[2,32,4736]{2,1,0:T(8,128)(2,1)} %get-tuple-element.130), channel_id=1, source_target_pairs={{0,1},{1,2},{2,3},{3,0},{4,5},{5,6},{6,7},{7,4},{8,9},{9,10},{10,1... | collective-permute-start | bytes 1818632 | tf_op jit(solution)/shard_map/ppermute | solution.py:1088
  421.9 42.1 %collective-permute-start.5 = (bf16[2,32,4736]{2,1,0:T(8,128)(2,1)}, bf16[2,32,4736]{2,1,0:T(8,128)(2,1)}, u32[]{:S(2)}, u32[]{:S(2)}) collective-permute-start(bf16[2,32,4736]{2,1,0:T(8,128)(2,1)} %get-tuple-element.129), channel_id=1, source_target_pairs={{0,2},{1,3},{2,0},{3,1},{4,6},{5,7},{6,4},{7,5},{8,10},{9,11},{10,... | collective-permute-start | bytes 1818632 | tf_op jit(solution)/shard_map/ppermute | solution.py:1088
  421.9 13.0 %copy-start.23 = (f32[1024,512]{1,0:T(8,128)S(1)}, f32[1024,512]{1,0:T(8,128)}, u32[]{:S(2)}) copy-start(f32[1024,512]{1,0:T(8,128)} %get-tuple-element.162) | copy-start | bytes 6291460
  421.9 13.0 %copy-start.24 = (f32[1024,512]{1,0:T(8,128)S(1)}, f32[1024,512]{1,0:T(8,128)}, u32[]{:S(2)}) copy-start(f32[1024,512]{1,0:T(8,128)} %get-tuple-element.71) | copy-start | bytes 6291460
  421.9 13.0 %copy-start.39 = (f32[512]{0:T(512)S(1)}, f32[512]{0:T(512)}, u32[]{:S(2)}) copy-start(f32[512]{0:T(512)} %copy-done.38) | copy-start | bytes 6148
  421.9 15.1 %slice-start.5 = ((s8[6291456]{0:T(1024)(128)(4,1)}), s8[2097152]{0:T(1024)(128)(4,1)S(1)}, s32[]{:S(2)}) async-start(s8[6291456]{0:T(1024)(128)(4,1)} %bitcast.133), calls=%async_computation.6 | async-start | bytes 4194304
  421.9 42.1 %collective-permute-start.6 = (bf16[2,32,4736]{2,1,0:T(8,128)(2,1)}, bf16[2,32,4736]{2,1,0:T(8,128)(2,1)}, u32[]{:S(2)}, u32[]{:S(2)}) collective-permute-start(bf16[2,32,4736]{2,1,0:T(8,128)(2,1)} %get-tuple-element.128), channel_id=1, source_target_pairs={{0,3},{1,0},{2,1},{3,2},{4,7},{5,4},{6,5},{7,6},{8,11},{9,8},{10,9... | collective-permute-start | bytes 1818632 | tf_op jit(solution)/shard_map/ppermute | solution.py:1088
  437.8 10.8 %copy-start.33 = (bf16[1024,16]{0,1:T(8,128)(2,1)S(1)}, bf16[1024,16]{0,1:T(8,128)(2,1)}, u32[]{:S(2)}) copy-start(bf16[1024,16]{0,1:T(8,128)(2,1)} %copy-done.32) | copy-start | bytes 98308
  448.6 4.9 copy-start.25
  453.5 14.1 %slice-start = ((s8[6291456]{0:T(1024)(128)(4,1)}), s8[2097152]{0:T(1024)(128)(4,1)S(1)}, s32[]{:S(2)}) async-start(s8[6291456]{0:T(1024)(128)(4,1)} %bitcast.99), calls=%async_computation.1 | async-start | bytes 4194304
  457.5 6.5 %copy-start.18 = (bf16[2,4,32,4736]{3,2,1,0:T(8,128)(2,1)S(1)}, bf16[2,4,32,4736]{3,2,1,0:T(8,128)(2,1)}, u32[]{:S(2)}) copy-start(bf16[2,4,32,4736]{3,2,1,0:T(8,128)(2,1)} %copy-done.17) | copy-start | bytes 7274500
  457.5 10.1 %slice-start.1 = ((s8[6291456]{0:T(1024)(128)(4,1)}), s8[4194304]{0:T(1024)(128)(4,1)S(1)}, s32[]{:S(2)}) async-start(s8[6291456]{0:T(1024)(128)(4,1)} %bitcast.99), calls=%async_computation.2 | async-start | bytes 8388608
  (23 other events, 41.4 us)
Sparse Core Ops, SparseCore 0:
  11.4 169.1 all-gather.1

commit v6 on v5

--- a/solution.py
+++ b/solution.py
@@ -69,6 +69,10 @@
     second = low(left)
     third = low(left - wide(second))
     return nn(ones, first) + nn(ones, second) + nn(ones, third)
+
+
+def logistic_of(values):
+    return 0.5 * jnp.tanh(0.5 * values) + 0.5
 
 
 def iota(shape, dim):
@@ -281,6 +285,25 @@
     return iota((count, HEAD_K), 0)
 
 
+def both_ways(seqs, place, count, go_right, go_left):
+    behind = count - 1 - place
+
+    def step(seq, carry):
+        for head in range(HEADS):
+
+            @pl.when(seq < seqs)
+            def _():
+                go_right(seq, head)
+
+            @pl.when(jnp.logical_and(seq >= behind, seq < behind + seqs))
+            def _():
+                go_left(seq - behind, head)
+
+        return carry
+
+    lax.fori_loop(0, seqs + count - 1, step, 0)
+
+
 def prefix_weights(cum, end_local, count):
     rows = row_places(count)
     owner = jnp.logical_and(end_local >= 0, end_local < count)
@@ -339,10 +362,10 @@
     def states_of(seq, carry):
         rows = pl.ds(pl.multiple_of(seq * toks, toks), toks)
         end_local = prefix_ref[seq] - 1 - place * toks
+        locals_ = []
         for head in range(HEADS):
             i = seq * HEADS + head
-            keys = slice(head * HEAD_K, (head + 1) * HEAD_K)
-            vals = slice(head * HEAD_V, (head + 1) * HEAD_V)
+            keys = query_columns(head)
             before = jnp.zeros((1, HEAD_K), jnp.float32)
             key = wide(proj_ref[rows, key_columns(head)])
             value = proj_ref[rows, value_columns(head)]
@@ -363,10 +386,13 @@
             weights, edge = prefix_weights(cum, end_local, toks)
             part_ref[i] = tn(value, low(key * weights))
             edge_ref[i] = jnp.broadcast_to(edge, (8, HEAD_K))
-
-            @pl.when(place == 0)
-            def _():
-                right_out[i] = low(local)
+            locals_.append(low(local))
+
+        @pl.when(place == 0)
+        def _():
+            for head in range(HEADS):
+                i = seq * HEADS + head
+                right_out[i] = locals_[head]
                 if count > 1:
                     to_right(i).start()
 
@@ -374,101 +400,91 @@
 
     lax.fori_loop(0, seqs, states_of, 0)
 
-    def outputs_of(seq, carry):
+    def go_right(seq, head):
         rows = pl.ds(pl.multiple_of(seq * toks, toks), toks)
-        for head in range(HEADS):
-            i = seq * HEADS + head
-            keys = slice(head * HEAD_K, (head + 1) * HEAD_K)
-            vals = slice(head * HEAD_V, (head + 1) * HEAD_V)
-            cum = cum_ref[rows, keys]
-            query = wide(proj_ref[rows, query_columns(head)])
-            key = wide(proj_ref[rows, key_columns(head)])
-            value = proj_ref[rows, value_columns(head)]
-            scores = []
-            for chunk in range(chunks):
-                at = slice(chunk * CHUNK, (chunk + 1) * CHUNK)
-                piece, total, middle = chunk_parts(cum, chunk)
-                raw = nt(
-                    low(query[at] * jnp.exp(piece - middle)), low(key[at] * jnp.exp(middle - piece))
-                )
-                scores.append(low(jnp.where(causal, raw, 0.0)))
-
-            @pl.when(place == 0)
+        i = seq * HEADS + head
+        vals = slice(head * HEAD_V, (head + 1) * HEAD_V)
+        cum = cum_ref[rows, query_columns(head)]
+
+        @pl.when(place == 0)
+        def _():
+            right_in[i] = jnp.zeros((HEAD_V, HEAD_K), jnp.bfloat16)
+
+        @pl.when(place > 0)
+        def _():
+            send(
+                right_out.at[i], right_in.at[i], right_sent.at[i], right_got.at[i], axes, place - 1
+            ).wait_recv()
+
+        state = wide(right_in[i])
+        part = part_ref[i] + edge_ref[i][:1] * state
+        part_ref[i] = part
+        for chunk in range(chunks):
+            state_ref[i, chunk] = low(state)
+            state = jnp.exp(chunk_parts(cum, chunk)[1]) * state + kv_ref[i, chunk]
+        state_ref[i, chunks] = low(state)
+
+        @pl.when(jnp.logical_and(place > 0, place < count - 1))
+        def _():
+            right_out[i] = low(state)
+            to_right(i).start()
+
+        if count > 1:
+
+            @pl.when(place == count - 1)
             def _():
-                right_in[i] = jnp.zeros((HEAD_V, HEAD_K), jnp.bfloat16)
-
-            @pl.when(place > 0)
-            def _():
-                send(right_out.at[i], right_in.at[i], right_sent.at[i], right_got.at[i], axes, place - 1).wait_recv()
-
-            state = wide(right_in[i])
-            part = part_ref[i] + edge_ref[i][:1] * state
-            part_ref[i] = part
-            for chunk in range(chunks):
-                at = slice(chunk * CHUNK, (chunk + 1) * CHUNK)
-                piece, total, middle = chunk_parts(cum, chunk)
-                narrow = low(state)
-                state_ref[i, chunk] = narrow
-                output = nn(scores[chunk], value[at]) + nt(
-                    low(query[at] * jnp.exp(piece)), narrow
-                )
-                mixed_ref[pl.ds(seq * toks + chunk * CHUNK, CHUNK), vals] = output
-                state = jnp.exp(total) * state + kv_ref[i, chunk]
-            state_ref[i, chunks] = low(state)
-
-            @pl.when(jnp.logical_and(place > 0, place < count - 1))
-            def _():
-                right_out[i] = low(state)
-                to_right(i).start()
-
-            if count > 1:
-
-                @pl.when(place == count - 1)
-                def _():
-                    left_out[i] = low(part)
-                    to_left(i).start()
-
-        return carry
-
-    lax.fori_loop(0, seqs, outputs_of, 0)
-
-    def prefix_of(seq, carry):
+                left_out[i] = low(part)
+                to_left(i).start()
+
+        query = wide(proj_ref[rows, query_columns(head)])
+        key = wide(proj_ref[rows, key_columns(head)])
+        value = proj_ref[rows, value_columns(head)]
+        for chunk in range(chunks):
+            at = slice(chunk * CHUNK, (chunk + 1) * CHUNK)
+            piece, total, middle = chunk_parts(cum, chunk)
+            raw = nt(
+                low(query[at] * jnp.exp(piece - middle)), low(key[at] * jnp.exp(middle - piece))
+            )
+            mixed_ref[pl.ds(seq * toks + chunk * CHUNK, CHUNK), vals] = nn(
+                low(jnp.where(causal, raw, 0.0)), value[at]
+            ) + nt(low(query[at] * jnp.exp(piece)), state_ref[i, chunk])
+
+    def go_left(seq, head):
         rows = pl.ds(pl.multiple_of(seq * toks, toks), toks)
         end_local = prefix_ref[seq] - 1 - place * toks
         inside = iota((toks, HEAD_V), 0) <= end_local
-        for head in range(HEADS):
-            i = seq * HEADS + head
-            keys = slice(head * HEAD_K, (head + 1) * HEAD_K)
-            vals = slice(head * HEAD_V, (head + 1) * HEAD_V)
-
-            @pl.when(place < count - 1)
-            def _():
-                send(left_out.at[i], left_in.at[i], left_sent.at[i], left_got.at[i], axes, place + 1).wait_recv()
-
-            @pl.when(place == count - 1)
-            def _():
-                left_in[i] = jnp.zeros((HEAD_V, HEAD_K), jnp.bfloat16)
-
-            whole = low(part_ref[i] + wide(left_in[i]))
-
-            @pl.when(jnp.logical_and(place > 0, place < count - 1))
-            def _():
-                left_out[i] = whole
-                to_left(i).start()
-
-            prefix_state_ref[i] = whole
-            mixed = jnp.where(
-                inside, nt(proj_ref[rows, query_columns(head)], whole), mixed_ref[rows, vals]
-            )
-            scale = lax.rsqrt(jnp.mean(mixed * mixed, axis=1, keepdims=True) + norm_eps)
-            unit = mixed * scale
-            gate = wide(proj_ref[rows, gate_columns(head)])
-            gated_ref[rows, vals] = low(unit * gain_ref[:1] * (gate / (1.0 + jnp.exp(-gate))))
-            unit_ref[rows, vals] = low(unit)
-            scale_ref[rows, slice(head, head + 1)] = scale
-        return carry
-
-    lax.fori_loop(0, seqs, prefix_of, 0)
+        i = seq * HEADS + head
+        vals = slice(head * HEAD_V, (head + 1) * HEAD_V)
+
+        @pl.when(place < count - 1)
+        def _():
+            send(
+                left_out.at[i], left_in.at[i], left_sent.at[i], left_got.at[i], axes, place + 1
+            ).wait_recv()
+
+        @pl.when(place == count - 1)
+        def _():
+            left_in[i] = jnp.zeros((HEAD_V, HEAD_K), jnp.bfloat16)
+
+        whole = low(part_ref[i] + wide(left_in[i]))
+
+        @pl.when(jnp.logical_and(place > 0, place < count - 1))
+        def _():
+            left_out[i] = whole
+            to_left(i).start()
+
+        prefix_state_ref[i] = whole
+        mixed = jnp.where(
+            inside, nt(proj_ref[rows, query_columns(head)], whole), mixed_ref[rows, vals]
+        )
+        scale = lax.rsqrt(jnp.mean(mixed * mixed, axis=1, keepdims=True) + norm_eps)
+        unit = mixed * scale
+        gate = wide(proj_ref[rows, gate_columns(head)])
+        gated_ref[rows, vals] = low(unit * gain_ref[:1] * gate * logistic_of(gate))
+        unit_ref[rows, vals] = low(unit)
+        scale_ref[rows, slice(head, head + 1)] = scale
+
+    both_ways(seqs, place, count, go_right, go_left)
 
     def finish(i, carry):
         @pl.when(place < count - 1)
@@ -532,23 +548,24 @@
         rows = pl.ds(pl.multiple_of(seq * toks, toks), toks)
         end_local = prefix_ref[seq] - 1 - place * toks
         inside = iota((toks, HEAD_V), 0) <= end_local
+        shares = []
+        gain = gain_ref[:1]
+        gain_grad = jnp.zeros((1, HEAD_V), jnp.float32)
         for head in range(HEADS):
             i = seq * HEADS + head
-            keys = slice(head * HEAD_K, (head + 1) * HEAD_K)
             vals = slice(head * HEAD_V, (head + 1) * HEAD_V)
-            cum = cum_ref[rows, keys]
+            cum = cum_ref[rows, query_columns(head)]
             query = proj_ref[rows, query_columns(head)]
             gate = wide(proj_ref[rows, gate_columns(head)])
-            logistic = 1.0 / (1.0 + jnp.exp(-gate))
+            logistic = logistic_of(gate)
             unit = wide(unit_ref[rows, vals])
-            gain = gain_ref[:1]
             gated_grad = wide(gated_grad_ref[rows, vals])
             through = gated_grad * unit
             active = gate * logistic
             dproj_ref[rows, gate_columns(head)] = low(
                 through * gain * (logistic + active * (1.0 - logistic))
             )
-            gain_grad_ref[:1] += jnp.sum(through * active, axis=0, keepdims=True)
+            gain_grad = gain_grad + jnp.sum(through * active, axis=0, keepdims=True)
             weighted = gated_grad * active * gain
             grad = scale_ref[rows, slice(head, head + 1)] * (
                 weighted - unit * jnp.mean(weighted * unit, axis=1, keepdims=True)
@@ -556,155 +573,152 @@
             grad_ref[rows, vals] = low(grad)
             share = tn(low(jnp.where(inside, grad, 0.0)), query)
             acc_ref[i] = share
-
-            @pl.when(place == 0)
-            def _():
-                right_out[i] = low(share)
-                if count > 1:
-                    to_right(i).start()
-
+            shares.append(low(share))
             later = low(jnp.where(inside, 0.0, grad))
             for chunk in range(chunks):
                 at = slice(chunk * CHUNK, (chunk + 1) * CHUNK)
                 piece, total, middle = chunk_parts(cum, chunk)
                 local_ref[i, chunk] = tn(later[at], low(wide(query[at]) * jnp.exp(piece)))
+        gain_grad_ref[:1] += gain_grad
+
+        @pl.when(place == 0)
+        def _():
+            for head in range(HEADS):
+                i = seq * HEADS + head
+                right_out[i] = shares[head]
+                if count > 1:
+                    to_right(i).start()
+
         return carry
 
     gain_grad_ref[...] = jnp.zeros_like(gain_grad_ref)
     lax.fori_loop(0, seqs, shares_of, 0)
 
-    def local_of(seq, carry):
+    def go_right(seq, head):
         rows = pl.ds(pl.multiple_of(seq * toks, toks), toks)
         end_local = prefix_ref[seq] - 1 - place * toks
         inside = iota((toks, HEAD_V), 0) <= end_local
-        inside_keys = iota((toks, HEAD_K), 0) <= end_local
         at_end = iota((toks, HEAD_K), 0) == end_local
-        for head in range(HEADS):
-            i = seq * HEADS + head
-            keys = slice(head * HEAD_K, (head + 1) * HEAD_K)
-            vals = slice(head * HEAD_V, (head + 1) * HEAD_V)
-            cum = cum_ref[rows, keys]
-            query = wide(proj_ref[rows, query_columns(head)])
-            key = wide(proj_ref[rows, key_columns(head)])
-            value = proj_ref[rows, value_columns(head)]
-            grad = wide(grad_ref[rows, vals])
-            later = low(jnp.where(inside, 0.0, grad))
-            weights, edge = prefix_weights(cum, end_local, toks)
-            prefix_state = prefix_state_ref[i]
-
-            @pl.when(place == 0)
-            def _():
-                right_in[i] = jnp.zeros((HEAD_V, HEAD_K), jnp.bfloat16)
-
-            @pl.when(place > 0)
-            def _():
-                send(right_out.at[i], right_in.at[i], right_sent.at[i], right_got.at[i], axes, place - 1).wait_recv()
-
-            acc = acc_ref[i] + wide(right_in[i])
-            narrow_acc = low(acc)
-
-            @pl.when(jnp.logical_and(place > 0, place < count - 1))
-            def _():
-                right_out[i] = narrow_acc
-                to_right(i).start()
-
-            local = jnp.zeros((HEAD_V, HEAD_K), jnp.float32)
-            starts = []
-            for chunk in reversed(range(chunks)):
-                piece, total, middle = chunk_parts(cum, chunk)
-                starts.append(local)
-                local = jnp.exp(total) * local + local_ref[i, chunk]
-            starts = starts[::-1]
-            local = local + edge * acc
-            acc_ref[i] = local
-            if count > 1:
-
-                @pl.when(place == count - 1)
-                def _():
-                    left_out[i] = low(local)
-                    to_left(i).start()
-
-            weighted = low(key * weights)
-            dk_all = weights * nn(value, narrow_acc)
-            dv_all = nt(weighted, narrow_acc)
-            dq_all = nn(low(jnp.where(inside, grad, 0.0)), prefix_state)
-            dqs, dks, dvs, dcs = [], [], [], []
-            for chunk in range(chunks):
-                at = slice(chunk * CHUNK, (chunk + 1) * CHUNK)
-                piece, total, middle = chunk_parts(cum, chunk)
-                rise = jnp.exp(piece - middle)
-                fall = jnp.exp(middle - piece)
-                q_in = low(query[at] * rise)
-                k_in = low(key[at] * fall)
-                scores = low(jnp.where(causal, nt(q_in, k_in), 0.0))
-                d_scores = low(jnp.where(causal, nt(later[at], value[at]), 0.0))
-                dq_in = nn(d_scores, k_in)
-                dk_in = tn(d_scores, q_in)
-                dq_state = jnp.exp(piece) * nn(later[at], state_ref[i, chunk])
-                to_end = jnp.exp(total - piece)
-                after = low(starts[chunk])
-                dk_state = to_end * nn(value[at], after) + dk_all[at]
-                dv = tn(scores, later[at]) + dv_all[at]
-                if chunk < chunks - 1:
-                    dv = dv + nt(low(key[at] * to_end), after)
-                dqs.append(rise * dq_in + dq_state + dq_all[at])
-                dks.append(fall * dk_in + dk_state)
-                dvs.append(dv)
-                dcs.append(
-                    wide(q_in) * dq_in
-                    - wide(k_in) * dk_in
-                    + query[at] * dq_state
-                    - key[at] * dk_state
-                )
-            dproj_ref[rows, query_columns(head)] = low(jnp.concatenate(dqs, axis=0))
-            dk_part[rows, keys] = jnp.concatenate(dks, axis=0)
-            dv_part[rows, vals] = jnp.concatenate(dvs, axis=0)
-            turn = jnp.sum(wide(narrow_acc) * wide(prefix_state), axis=0, keepdims=True)
-            dcum_part[rows, keys] = jnp.concatenate(dcs, axis=0) + jnp.where(at_end, turn, 0.0)
-        return carry
-
-    lax.fori_loop(0, seqs, local_of, 0)
-
-    def rest_of(seq, carry):
-        rows = pl.ds(pl.multiple_of(seq * toks, toks), toks)
-        for head in range(HEADS):
-            i = seq * HEADS + head
-            keys = slice(head * HEAD_K, (head + 1) * HEAD_K)
-            vals = slice(head * HEAD_V, (head + 1) * HEAD_V)
-            cum = cum_ref[rows, keys]
-            key = wide(proj_ref[rows, key_columns(head)])
-            value = proj_ref[rows, value_columns(head)]
-
-            @pl.when(place < count - 1)
-            def _():
-                send(left_out.at[i], left_in.at[i], left_sent.at[i], left_got.at[i], axes, place + 1).wait_recv()
+        i = seq * HEADS + head
+        cum = cum_ref[rows, query_columns(head)]
+
+        @pl.when(place == 0)
+        def _():
+            right_in[i] = jnp.zeros((HEAD_V, HEAD_K), jnp.bfloat16)
+
+        @pl.when(place > 0)
+        def _():
+            send(
+                right_out.at[i], right_in.at[i], right_sent.at[i], right_got.at[i], axes, place - 1
+            ).wait_recv()
+
+        acc = acc_ref[i] + wide(right_in[i])
+        narrow_acc = low(acc)
+
+        @pl.when(jnp.logical_and(place > 0, place < count - 1))
+        def _():
+            right_out[i] = narrow_acc
+            to_right(i).start()
+
+        weights, edge = prefix_weights(cum, end_local, toks)
+        local = jnp.zeros((HEAD_V, HEAD_K), jnp.float32)
+        starts = []
+        for chunk in reversed(range(chunks)):
+            starts.append(low(local))
+            local = jnp.exp(chunk_parts(cum, chunk)[1]) * local + local_ref[i, chunk]
+        starts = starts[::-1]
+        local = local + edge * acc
+        acc_ref[i] = local
+        if count > 1:
 
             @pl.when(place == count - 1)
             def _():
-                left_in[i] = jnp.zeros((HEAD_V, HEAD_K), jnp.bfloat16)
-
-            after = left_in[i]
-            last = cum[toks - 1 :]
-
-            @pl.when(jnp.logical_and(place > 0, place < count - 1))
-            def _():
-                left_out[i] = low(jnp.exp(last) * wide(after) + acc_ref[i])
+                left_out[i] = low(local)
                 to_left(i).start()
 
-            to_end = jnp.exp(last - cum)
-            dk_more = to_end * nn(value, after)
-            dproj_ref[rows, key_columns(head)] = low(
-                dk_part[rows, keys] + dk_more
+        keys = query_columns(head)
+        vals = slice(head * HEAD_V, (head + 1) * HEAD_V)
+        query = wide(proj_ref[rows, query_columns(head)])
+        key = wide(proj_ref[rows, key_columns(head)])
+        value = proj_ref[rows, value_columns(head)]
+        grad = wide(grad_ref[rows, vals])
+        later = low(jnp.where(inside, 0.0, grad))
+        prefix_state = prefix_state_ref[i]
+        weighted = low(key * weights)
+        dk_all = weights * nn(value, narrow_acc)
+        dv_all = nt(weighted, narrow_acc)
+        dq_all = nn(low(jnp.where(inside, grad, 0.0)), prefix_state)
+        dqs, dks, dvs, dcs = [], [], [], []
+        for chunk in range(chunks):
+            at = slice(chunk * CHUNK, (chunk + 1) * CHUNK)
+            piece, total, middle = chunk_parts(cum, chunk)
+            rise = jnp.exp(piece - middle)
+            fall = jnp.exp(middle - piece)
+            q_in = low(query[at] * rise)
+            k_in = low(key[at] * fall)
+            scores = low(jnp.where(causal, nt(q_in, k_in), 0.0))
+            d_scores = low(jnp.where(causal, nt(later[at], value[at]), 0.0))
+            dq_in = nn(d_scores, k_in)
+            dk_in = tn(d_scores, q_in)
+            dq_state = jnp.exp(piece) * nn(later[at], state_ref[i, chunk])
+            dk_state = dk_all[at]
+            dv = tn(scores, later[at]) + dv_all[at]
+            if chunk < chunks - 1:
+                to_end = jnp.exp(total - piece)
+                dk_state = to_end * nn(value[at], starts[chunk]) + dk_state
+                dv = dv + nt(low(key[at] * to_end), starts[chunk])
+            dqs.append(rise * dq_in + dq_state + dq_all[at])
+            dks.append(fall * dk_in + dk_state)
+            dvs.append(dv)
+            dcs.append(
+                wide(q_in) * dq_in
+                - wide(k_in) * dk_in
+                + query[at] * dq_state
+                - key[at] * dk_state
             )
-            dproj_ref[rows, value_columns(head)] = low(
-                dv_part[rows, vals] + nt(low(key * to_end), after)
-            )
-            carry_row = jnp.sum(wide(after) * wide(state_ref[i, chunks]), axis=0, keepdims=True)
-            dcum = dcum_part[rows, keys] - key * dk_more
-            ddecay_ref[rows, keys] = three_way(upper, dcum) + carry_row
-        return carry
-
-    lax.fori_loop(0, seqs, rest_of, 0)
+        dproj_ref[rows, query_columns(head)] = low(jnp.concatenate(dqs, axis=0))
+        dk_part[rows, keys] = jnp.concatenate(dks, axis=0)
+        dv_part[rows, vals] = jnp.concatenate(dvs, axis=0)
+        turn = jnp.sum(wide(narrow_acc) * wide(prefix_state), axis=0, keepdims=True)
+        dcum_part[rows, keys] = jnp.concatenate(dcs, axis=0) + jnp.where(at_end, turn, 0.0)
+
+    def go_left(seq, head):
+        rows = pl.ds(pl.multiple_of(seq * toks, toks), toks)
+        i = seq * HEADS + head
+        keys = query_columns(head)
+        vals = slice(head * HEAD_V, (head + 1) * HEAD_V)
+
+        @pl.when(place < count - 1)
+        def _():
+            send(
+                left_out.at[i], left_in.at[i], left_sent.at[i], left_got.at[i], axes, place + 1
+            ).wait_recv()
+
+        @pl.when(place == count - 1)
+        def _():
+            left_in[i] = jnp.zeros((HEAD_V, HEAD_K), jnp.bfloat16)
+
+        @pl.when(jnp.logical_and(place > 0, place < count - 1))
+        def _():
+            last = cum_ref[rows, keys][toks - 1 :]
+            left_out[i] = low(jnp.exp(last) * wide(left_in[i]) + acc_ref[i])
+            to_left(i).start()
+
+        cum = cum_ref[rows, keys]
+        key = wide(proj_ref[rows, key_columns(head)])
+        value = proj_ref[rows, value_columns(head)]
+        after = left_in[i]
+        to_end = jnp.exp(cum[toks - 1 :] - cum)
+        dk_more = to_end * nn(value, after)
+        dproj_ref[rows, key_columns(head)] = low(dk_part[rows, keys] + dk_more)
+        dproj_ref[rows, value_columns(head)] = low(
+            dv_part[rows, vals] + nt(low(key * to_end), after)
+        )
+        carry_row = jnp.sum(wide(after) * wide(state_ref[i, chunks]), axis=0, keepdims=True)
+        dcum = dcum_part[rows, keys] - key * dk_more
+        ddecay_ref[rows, keys] = three_way(upper, dcum) + carry_row
+
+    both_ways(seqs, place, count, go_right, go_left)
 
     def finish(i, carry):
         @pl.when(place < count - 1)

time: 556 us -> 524 us (0.942)
  Pallas kernels: 400 us -> 368 us
    pallas_call x1, Pallas kernels: 74.4 us -> 59.7 us  [mix_backward(): pl.pallas_call(partial(backward_kernel, axes), out_shape=(jax.ShapeDtypeS...]
    pallas_call x1, Pallas kernels: 106 us -> 91.5 us  [mix_forward(): pl.pallas_call(partial(forward_kernel, axes), out_shape=(jax.ShapeDtypeSt...]
  transfers between devices with their start and end apart: 8 -> 8, of which waited for: 1 -> 0; matrix products, arithmetic and copies ran while one was open for 14% -> 15% of each run, Pallas kernels for 47% -> 44%
where the time goes in v6:
time: 524 us; the launch traced here: 517 us
  Pallas kernels  368 us (70%)
  matrix products  47.4 us (9%)
  local copies, waits for them, and re-layouts  44.4 us (8%)
  other arithmetic  34.5 us (7%)
  between operations  15.3 us (3%)
  starting transfers between devices  7.79 us (1%)
    pallas_call x1, Pallas kernels, mix_forward(): pl.pallas_call(partial(forward_kernel, axes), out_shape=(jax.ShapeDtypeSt...  91.5 us
    pallas_call x1, Pallas kernels, ffn_both(): pl.pallas_call(ffn_kernel, out_shape=(total, total, share, share, share),...  78 us
    pallas_call x1, Pallas kernels, gather_first(): pl.pallas_call(partial(gather_kernel, (names, sizes, len(shards), len(wid...  75.2 us
    pallas_call x1, Pallas kernels, reduce_rest(): pl.pallas_call(partial(reduce_kernel, (len(arrays), jobs, sizes, slots)),...  63.4 us
    pallas_call x1, Pallas kernels, mix_backward(): pl.pallas_call(partial(backward_kernel, axes), out_shape=(jax.ShapeDtypeS...  59.7 us
    dot_general x4, matrix products, project(): jnp.einsum('td,de->te', inputs, weight, preferred_element_type=jnp.float32)  17.7 us
    dot_general x4, matrix products, back_project(): jnp.einsum('te,de->td', gradient, weight, preferred_element_type=jnp.floa...  17.3 us
    dot_general x5, matrix products, flat_grad(): jnp.einsum('td,te->de', inputs, gradient, preferred_element_type=jnp.floa...  12.3 us
  transfers between devices with their start and end apart: 8, of which 0 were waited for; matrix products, arithmetic and copies ran while one was open for 15% of the time, Pallas kernels for 44%

profile of v6, /device:TPU:0, one launch (start us, length us, event | category | flops | bytes accessed | tf_op | source)
XLA Modules:
  0.0 517.1 jit_solution(2896969612732569723)
XLA Ops:
  7.2 2.1 pad_maximum_fusion.6
  14.8 75.2 %gather_first.1 = (bf16[2,2,2,4,32,3072]{5,4,3,2,1,0:T(8,128)(2,1)}, bf16[2,2,2,4,32,128]{5,4,3,2,1,0:T(8,128)(2,1)}) custom-call(bf16[32,512]{1,0:T(8,128)(2,1)} %refs_0_.2, bf16[32,512]{1,0:T(8,128)(2,1)} %refs_1_.1, bf16[32,1024]{1,0:T(8,128)(2,1)} %refs_2_.1, bf16[32,1024]{1,0:T(8,128)(2,1)} %refs_3_.1, bf16[32,128]{1,0:T(8,128)(2,1)} %concatenate.37.refs_4_), custom_call_target="tpu_custom_call" | custom-call | tf_op jit(solution)/shard_map/gather_first/pallas_call | solution.py:271
  96.1 3.4 fusion.17
  99.5 9.0 %convolution_convert_fusion.1.refs_1_.proj_ref = bf16[1024,3072]{1,0:T(8,128)(2,1)} fusion(bf16[1024,1024]{1,0:T(8,128)(2,1)S(1)} %bitcast.117, bf16[1024,3072]{1,0:T(8,128)(2,1)S(1)} %bitcast.132), kind=kOutput, calls=%fused_computation.2 | convolution fusion | flops 6445596672 | bytes 14680064 | tf_op jit(solution)/shard_map/td,de->te/dot_general | solution.py:25
  108.5 91.5 %mix_forward.1 = (bf16[1024,1024]{1,0:T(8,128)(2,1)S(1)}, bf16[1024,1024]{1,0:T(8,128)(2,1)}, f32[1024,128]{1,0:T(8,128)S(1)}, f32[1024,512]{1,0:T(8,128)}, bf16...) custom-call(s32[4]{0:T(128)S(1)} %copy-done.1, ...), custom_call_target="tpu_custom_call" | custom-call | flops 60000002048 | bytes 220000000 | tf_op jit(solution)/shard_map/mix_forward/pallas_call | solution.py:752
  200.0 2.0 constant_dynamic-slice_fusion.9
  204.2 4.7 multiply_reduce_fusion.2
  209.3 1.6 copy-done.4
  211.4 1.6 pad_maximum_fusion.2
  213.0 78.0 %ffn_both.1 = (f32[1024,1024]{1,0:T(8,128)}, f32[1024,1024]{1,0:T(8,128)}, bf16[512,2816]{1,0:T(8,128)(2,1)}, bf16[512,2816]{1,0:T(8,128)(2,1)}, bf16[512,2816]{1,0:T(8,128)(2,1)}) custom-call(bf16[1024,1024]{1,0:T(8,128)(2,1)} %copy-done.11, bf16[1024,1024]{1,0:T(8,128)(2,1)} %bitcast.107, bf16[1024,512]{1,0:T(8,128)(2,1)} %get-tuple-element.174.mine_ref, ...), custom_call_target="tpu_custom_call" | custom-call | tf_op jit(solution)/shard_map/ffn_both/pallas_call | solution.py:958
  291.0 1.4 slice.83
  292.4 1.8 slice.84
  294.3 3.5 multiply_reduce_fusion
  298.4 4.3 multiply_add_fusion
  302.7 1.3 convolution_convert_fusion.3
  305.0 5.4 %convolution_convert_fusion.2.gated_grad_ref = bf16[1024,1024]{1,0:T(8,128)(2,1)} fusion(bf16[1024,9472]{1,0:T(8,128)(2,1)} %all-gather.2.cloned.1.call-done.weight_ref, f32[1024,1024]{1,0:T(8,128)S(1)} %get-tuple-element.126), kind=kOutput, calls=%fused_computation.42 | convolution fusion | flops 2149580800 | bytes 8388608 | tf_op jit(solution)/shard_map/te,de->td/dot_general | solution.py:29
  314.0 1.8 dynamic-slice_bitcast_fusion
  315.8 1.8 collective-permute-start.1
  318.0 1.6 copy.71
  319.6 1.4 collective-permute-start.2
  321.1 59.7 %mix_backward.1 = (bf16[1024,3072]{1,0:T(8,128)(2,1)}, f32[1024,512]{1,0:T(8,128)}, f32[8,256]{1,0:T(8,128)}) custom-call(s32[4]{0:T(128)} %prefix_ref.1, bf16[1024,3072]{1,0:T(8,128)(2,1)} %convolution_convert_fusion.1.refs_1_.proj_ref, f32[1024,512]{1,0:T(8,128)} %get-tuple-element.60.cum_ref, bf16[16,3,256,128]{3,2,1,0:T(8,128)(2,1)} %get-tuple-element.61.state_ref, ...), custom_call_target="tpu_custom_call" | custom-call | flops 60000002048 | bytes 220000000 | tf_op jit(solution)/shard_map/mix_backward/pallas_call | solution.py:789
  382.2 3.0 fusion.1
  387.1 3.0 fusion
  390.2 1.4 copy-done.16
  392.9 3.9 collective-permute-start.6
  396.7 9.1 %convolution_convert_fusion = bf16[1024,3072]{1,0:T(8,128)(2,1)} fusion(bf16[1024,1024]{1,0:T(8,128)(2,1)S(1)} %copy-done.10, bf16[1024,3072]{1,0:T(8,128)(2,1)S(1)} %copy-done.40), kind=kOutput, calls=%fused_computation.1 | convolution fusion | flops 6445596672 | bytes 14680064 | tf_op jit(solution)/shard_map/td,te->de/dot_general | solution.py:1086
  408.8 10.8 %fusion.8 = (f32[1024]{0:T(1024)S(1)}, bf16[1024]{0:T(1024)(128)(2,1)S(1)}, f32[1024,1024]{1,0:T(8,128)}) fusion(bf16[4,256,1024]{2,1,0:T(8,128)(2,1)S(1)} %copy-done.7, f32[1024]{0:T(1024)S(1)} %copy-done.35, f32[1024]{0:T(1024)S(1)} %bitcast.124, f32[1024,1024]{1,0:T(8,128)S(1)} %fusion.40, bf16[1024,3072]{1,0:T(8,128)(2,1)} %get-tuple-element.70, ...), kind=kOutput, calls=%fused_computation.19 | convolution fusion | flops 6450837504 | bytes 23083008 | tf_op jit(solution)/shard_map/te,de->td/dot_general | solution.py:29
  424.4 4.0 concatenate.47
  428.4 6.1 %fusion.11 = f32[1024,1024]{1,0:T(8,128)} fusion(f32[1024,1024]{1,0:T(8,128)} %copy-done.15, bf16[4,256,1024]{2,1,0:T(8,128)(2,1)} %param.17, f32[1024,1024]{1,0:T(8,128)} %get-tuple-element.165, f32[1024]{0:T(1024)S(1)} %broadcast_multiply_fusion, f32[1024]{0:T(1024)S(1)} %copy-done.35, f32[1024]{0:T(1024)S(1)} %bitcast.125), kind=kLoop, calls=%fused_computation.22 | loop fusion | flops 7340032 | bytes 14692352 | tf_op jit(solution)/shard_map/add | solution.py:1398
  434.6 1.9 fusion.15.refs_0_
  436.5 1.9 fusion.22.refs_1_
  438.5 63.4 %reduce_rest.1 = (f32[32,4736]{1,0:T(8,128)S(1)}, f32[32,4736]{1,0:T(8,128)S(1)}, f32[32,3072]{1,0:T(8,128)S(1)}, f32[32,128]{1,0:T(8,128)S(1)}) custom-call(bf16[4,32,4736]{2,1,0:T(8,128)(2,1)S(1)} %fusion.15.refs_0_, bf16[2,32,4736]{2,1,0:T(8,128)(2,1)S(1)} %fusion.22.refs_1_, bf16[2,2,2,4,32,3072]{5,4,3,2,1,0:T(8,128)(2,1)S(1)} %bitcast.101, ...), custom_call_target="tpu_custom_call" | custom-call | tf_op jit(solution)/shard_map/reduce_rest/pallas_call | solution.py:1244
  (186 shorter events, 40.1 us)
Async XLA Ops:
  7.2 85.2 %copy-start.6 = (bf16[4,256,1024]{2,1,0:T(8,128)(2,1)S(1)}, bf16[4,256,1024]{2,1,0:T(8,128)(2,1)}, u32[]{:S(2)}) copy-start(bf16[4,256,1024]{2,1,0:T(8,128)(2,1)} %param.17) | copy-start | bytes 6291460
  7.2 197.0 %all-gather.2.cloned.1.call-start = ((), (), s32[]{:S(2)}) async-start(), calls=%async_computation | async-start | bytes 20004864 | tf_op jit(solution)/shard_map/all_gather | solution.py:1314
  92.4 3.6 copy-start.38
  94.8 4.7 slice-start.2
  95.4 4.1 copy-start.32
  95.4 4.1 slice-start.3
  99.5 9.0 %copy-start.1 = (s32[4]{0:T(128)S(1)}, s32[4]{0:T(128)}, u32[]{:S(2)}) copy-start(s32[4]{0:T(128)} %prefix_ref.1) | copy-start | bytes 52
  108.5 91.5 %copy-start = (f32[8,256]{1,0:T(8,128)}, f32[8,256]{1,0:T(8,128)S(1)}, u32[]{:S(2)}) copy-start(f32[8,256]{1,0:T(8,128)S(1)} %broadcast_in_dim.53.refs_3_.gain_ref) | copy-start | bytes 24580
  108.5 91.5 %copy-start.12 = (bf16[4,256,1024]{2,1,0:T(8,128)(2,1)S(1)}, bf16[4,256,1024]{2,1,0:T(8,128)(2,1)}, u32[]{:S(2)}) copy-start(bf16[4,256,1024]{2,1,0:T(8,128)(2,1)} %param.33) | copy-start | bytes 6291460
  294.3 4.1 copy-start.14
  302.7 8.1 %copy-start.15 = (f32[1024,1024]{1,0:T(8,128)}, f32[1024,1024]{1,0:T(8,128)S(1)}, u32[]{:S(2)}) copy-start(f32[1024,1024]{1,0:T(8,128)S(1)} %get-tuple-element.126) | copy-start | bytes 12582916
  304.0 6.8 %collective-permute-start = (bf16[512,1024]{1,0:T(8,128)(2,1)S(1)}, bf16[512,1024]{1,0:T(8,128)(2,1)S(1)}, u32[]{:S(2)}, u32[]{:S(2)}) collective-permute-start(bf16[512,1024]{1,0:T(8,128)(2,1)S(1)} %convolution_convert_fusion.3), channel_id=1, source_target_pairs={{0,4},{4,0},{1,5},{5,1},{2,6},{6,2},{3,7},{7,3},{8,12},{12,8},{9,1... | collective-permute-start | bytes 3145736 | tf_op jit(solution)/shard_map/ppermute | solution.py:1076
  305.0 5.4 %copy-start.22 = (bf16[512,2816]{1,0:T(8,128)(2,1)S(1)}, bf16[512,2816]{1,0:T(8,128)(2,1)}, u32[]{:S(2)}) copy-start(bf16[512,2816]{1,0:T(8,128)(2,1)} %get-tuple-element.57) | copy-start | bytes 8650756
  314.0 4.0 copy-start.8
  315.8 66.4 %collective-permute-start.1 = (bf16[2,4,32,4736]{3,2,1,0:T(8,128)(2,1)}, bf16[2,4,32,4736]{3,2,1,0:T(8,128)(2,1)}, u32[]{:S(2)}, u32[]{:S(2)}) collective-permute-start(bf16[2,4,32,4736]{3,2,1,0:T(8,128)(2,1)} %dynamic-slice_bitcast_fusion), channel_id=1, source_target_pairs={{0,16},{16,0},{1,17},{17,1},{2,18},{18,2},{3,19},{19,3},{4,20},{20... | collective-permute-start | bytes 7274504 | tf_op jit(solution)/shard_map/ppermute | solution.py:1102
  319.6 62.6 %collective-permute-start.2 = (bf16[2,4,32,4736]{3,2,0,1:T(8,128)(2,1)}, bf16[2,4,32,4736]{3,2,0,1:T(8,128)(2,1)}, u32[]{:S(2)}, u32[]{:S(2)}) collective-permute-start(bf16[2,4,32,4736]{3,2,0,1:T(8,128)(2,1)} %bitcast.97), channel_id=1, source_target_pairs={{0,8},{8,0},{1,9},{9,1},{2,10},{10,2},{3,11},{11,3},{4,12},{12,4},... | collective-permute-start | bytes 7274504 | tf_op jit(solution)/shard_map/ppermute | solution.py:1102
  385.2 11.5 %copy-start.40 = (bf16[1024,3072]{1,0:T(8,128)(2,1)S(1)}, bf16[1024,3072]{1,0:T(8,128)(2,1)}, u32[]{:S(2)}) copy-start(bf16[1024,3072]{1,0:T(8,128)(2,1)} %get-tuple-element.70) | copy-start | bytes 18874372
  386.4 48.2 %collective-permute-start.3 = (bf16[4,32,4736]{2,1,0:T(8,128)(2,1)}, bf16[4,32,4736]{2,1,0:T(8,128)(2,1)}, u32[]{:S(2)}, u32[]{:S(2)}) collective-permute-start(bf16[4,32,4736]{2,1,0:T(8,128)(2,1)} %dynamic-slice_bitcast_fusion.1), channel_id=1, source_target_pairs={{0,8},{8,0},{1,9},{9,1},{2,10},{10,2},{3,11},{11,3},{4,12},{12,4},... | collective-permute-start | bytes 3637256 | tf_op jit(solution)/shard_map/ppermute | solution.py:1102
  387.1 20.8 %slice-start.4 = ((s8[6291456]{0:T(1024)(128)(4,1)}), s8[4194304]{0:T(1024)(128)(4,1)S(1)}, s32[]{:S(2)}) async-start(s8[6291456]{0:T(1024)(128)(4,1)} %bitcast.133), calls=%async_computation.5 | async-start | bytes 8388608
  391.6 5.2 copy-start.10
  392.8 41.8 %collective-permute-start.4 = (bf16[2,32,4736]{2,1,0:T(8,128)(2,1)}, bf16[2,32,4736]{2,1,0:T(8,128)(2,1)}, u32[]{:S(2)}, u32[]{:S(2)}) collective-permute-start(bf16[2,32,4736]{2,1,0:T(8,128)(2,1)} %get-tuple-element.130), channel_id=1, source_target_pairs={{0,1},{1,2},{2,3},{3,0},{4,5},{5,6},{6,7},{7,4},{8,9},{9,10},{10,1... | collective-permute-start | bytes 1818632 | tf_op jit(solution)/shard_map/ppermute | solution.py:1102
  392.8 41.8 %collective-permute-start.5 = (bf16[2,32,4736]{2,1,0:T(8,128)(2,1)}, bf16[2,32,4736]{2,1,0:T(8,128)(2,1)}, u32[]{:S(2)}, u32[]{:S(2)}) collective-permute-start(bf16[2,32,4736]{2,1,0:T(8,128)(2,1)} %get-tuple-element.129), channel_id=1, source_target_pairs={{0,2},{1,3},{2,0},{3,1},{4,6},{5,7},{6,4},{7,5},{8,10},{9,11},{10,... | collective-permute-start | bytes 1818632 | tf_op jit(solution)/shard_map/ppermute | solution.py:1102
  392.8 13.0 %copy-start.23 = (f32[1024,512]{1,0:T(8,128)S(1)}, f32[1024,512]{1,0:T(8,128)}, u32[]{:S(2)}) copy-start(f32[1024,512]{1,0:T(8,128)} %get-tuple-element.162) | copy-start | bytes 6291460
  392.8 13.0 %copy-start.24 = (f32[1024,512]{1,0:T(8,128)S(1)}, f32[1024,512]{1,0:T(8,128)}, u32[]{:S(2)}) copy-start(f32[1024,512]{1,0:T(8,128)} %get-tuple-element.71) | copy-start | bytes 6291460
  392.8 13.0 %copy-start.39 = (f32[512]{0:T(512)S(1)}, f32[512]{0:T(512)}, u32[]{:S(2)}) copy-start(f32[512]{0:T(512)} %copy-done.38) | copy-start | bytes 6148
  392.9 15.1 %slice-start.5 = ((s8[6291456]{0:T(1024)(128)(4,1)}), s8[2097152]{0:T(1024)(128)(4,1)S(1)}, s32[]{:S(2)}) async-start(s8[6291456]{0:T(1024)(128)(4,1)} %bitcast.133), calls=%async_computation.6 | async-start | bytes 4194304
  392.9 41.7 %collective-permute-start.6 = (bf16[2,32,4736]{2,1,0:T(8,128)(2,1)}, bf16[2,32,4736]{2,1,0:T(8,128)(2,1)}, u32[]{:S(2)}, u32[]{:S(2)}) collective-permute-start(bf16[2,32,4736]{2,1,0:T(8,128)(2,1)} %get-tuple-element.128), channel_id=1, source_target_pairs={{0,3},{1,0},{2,1},{3,2},{4,7},{5,4},{6,5},{7,6},{8,11},{9,8},{10,9... | collective-permute-start | bytes 1818632 | tf_op jit(solution)/shard_map/ppermute | solution.py:1102
  408.8 10.8 %copy-start.33 = (bf16[1024,16]{0,1:T(8,128)(2,1)S(1)}, bf16[1024,16]{0,1:T(8,128)(2,1)}, u32[]{:S(2)}) copy-start(bf16[1024,16]{0,1:T(8,128)(2,1)} %copy-done.32) | copy-start | bytes 98308
  419.6 4.9 copy-start.25
  424.4 14.1 %slice-start = ((s8[6291456]{0:T(1024)(128)(4,1)}), s8[2097152]{0:T(1024)(128)(4,1)S(1)}, s32[]{:S(2)}) async-start(s8[6291456]{0:T(1024)(128)(4,1)} %bitcast.99), calls=%async_computation.1 | async-start | bytes 4194304
  428.4 6.2 %copy-start.18 = (bf16[2,4,32,4736]{3,2,1,0:T(8,128)(2,1)S(1)}, bf16[2,4,32,4736]{3,2,1,0:T(8,128)(2,1)}, u32[]{:S(2)}) copy-start(bf16[2,4,32,4736]{3,2,1,0:T(8,128)(2,1)} %copy-done.17) | copy-start | bytes 7274500
  428.4 10.1 %slice-start.1 = ((s8[6291456]{0:T(1024)(128)(4,1)}), s8[4194304]{0:T(1024)(128)(4,1)S(1)}, s32[]{:S(2)}) async-start(s8[6291456]{0:T(1024)(128)(4,1)} %bitcast.99), calls=%async_computation.2 | async-start | bytes 8388608
  (23 other events, 41.4 us)
Sparse Core Ops, SparseCore 0:
  11.4 169.1 all-gather.1

commit v7 on v6

--- a/solution.py
+++ b/solution.py
@@ -1420,12 +1420,10 @@
     size_of = dict(zip(names, sizes))
     ends = last_orders(names)
     jobs = [
-        (which, columns, names, ("core", *order), which, columns)
-        for which, columns, order in (
-            (2, (0, 1536), ends[0]),
-            (2, (1536, 3072), ends[1]),
-            (3, (0, EXTRA), ends[0]),
-        )
+        (2, (begin, begin + 768), names, ("core", *order), 2, (begin, begin + 768))
+        for begin, order in zip(range(0, 3072, 768), ends * 2)
+    ] + [
+        (3, (0, EXTRA), names, ("core", *ends[0]), 3, (0, EXTRA)),
     ] + [
         (i, (0, groups[i].shape[-1]), (order[2],), (order[2],), i, (0, groups[i].shape[-1]))
         for i, order in enumerate(orders)

time: 524 us -> 520 us (level)
  no operation moved by 1% of the time
where the time goes in v7:
time: 520 us; the launch traced here: 513 us
  Pallas kernels  364 us (70%)
  matrix products  47.4 us (9%)
  local copies, waits for them, and re-layouts  44.4 us (9%)
  other arithmetic  34.5 us (7%)
  between operations  15.3 us (3%)
  starting transfers between devices  7.79 us (1%)
    pallas_call x1, Pallas kernels, mix_forward(): pl.pallas_call(partial(forward_kernel, axes), out_shape=(jax.ShapeDtypeSt...  91.5 us
    pallas_call x1, Pallas kernels, ffn_both(): pl.pallas_call(ffn_kernel, out_shape=(total, total, share, share, share),...  78 us
    pallas_call x1, Pallas kernels, gather_first(): pl.pallas_call(partial(gather_kernel, (names, sizes, len(shards), len(wid...  75.2 us
    pallas_call x1, Pallas kernels, mix_backward(): pl.pallas_call(partial(backward_kernel, axes), out_shape=(jax.ShapeDtypeS...  59.7 us
    pallas_call x1, Pallas kernels, reduce_rest(): pl.pallas_call(partial(reduce_kernel, (len(arrays), jobs, sizes, slots)),...  59.6 us
    dot_general x4, matrix products, project(): jnp.einsum('td,de->te', inputs, weight, preferred_element_type=jnp.float32)  17.7 us
    dot_general x4, matrix products, back_project(): jnp.einsum('te,de->td', gradient, weight, preferred_element_type=jnp.floa...  17.3 us
    dot_general x5, matrix products, flat_grad(): jnp.einsum('td,te->de', inputs, gradient, preferred_element_type=jnp.floa...  12.3 us
  transfers between devices with their start and end apart: 8, of which 0 were waited for; matrix products, arithmetic and copies ran while one was open for 15% of the time, Pallas kernels for 44%

profile of v7, /device:TPU:0, one launch (start us, length us, event | category | flops | bytes accessed | tf_op | source)
XLA Modules:
  0.0 513.3 jit_solution(14934231082053790741)
XLA Ops:
  7.2 2.1 pad_maximum_fusion.6
  14.8 75.2 %gather_first.1 = (bf16[2,2,2,4,32,3072]{5,4,3,2,1,0:T(8,128)(2,1)}, bf16[2,2,2,4,32,128]{5,4,3,2,1,0:T(8,128)(2,1)}) custom-call(bf16[32,512]{1,0:T(8,128)(2,1)} %refs_0_.2, bf16[32,512]{1,0:T(8,128)(2,1)} %refs_1_.1, bf16[32,1024]{1,0:T(8,128)(2,1)} %refs_2_.1, bf16[32,1024]{1,0:T(8,128)(2,1)} %refs_3_.1, bf16[32,128]{1,0:T(8,128)(2,1)} %concatenate.37.refs_4_), custom_call_target="tpu_custom_call" | custom-call | tf_op jit(solution)/shard_map/gather_first/pallas_call | solution.py:271
  96.1 3.4 fusion.17
  99.5 9.0 %convolution_convert_fusion.1.refs_1_.proj_ref = bf16[1024,3072]{1,0:T(8,128)(2,1)} fusion(bf16[1024,1024]{1,0:T(8,128)(2,1)S(1)} %bitcast.117, bf16[1024,3072]{1,0:T(8,128)(2,1)S(1)} %bitcast.132), kind=kOutput, calls=%fused_computation.2 | convolution fusion | flops 6445596672 | bytes 14680064 | tf_op jit(solution)/shard_map/td,de->te/dot_general | solution.py:25
  108.5 91.5 %mix_forward.1 = (bf16[1024,1024]{1,0:T(8,128)(2,1)S(1)}, bf16[1024,1024]{1,0:T(8,128)(2,1)}, f32[1024,128]{1,0:T(8,128)S(1)}, f32[1024,512]{1,0:T(8,128)}, bf16...) custom-call(s32[4]{0:T(128)S(1)} %copy-done.1, ...), custom_call_target="tpu_custom_call" | custom-call | flops 60000002048 | bytes 220000000 | tf_op jit(solution)/shard_map/mix_forward/pallas_call | solution.py:752
  200.0 2.0 constant_dynamic-slice_fusion.9
  204.2 4.7 multiply_reduce_fusion.2
  209.3 1.6 copy-done.4
  211.4 1.6 pad_maximum_fusion.2
  213.0 78.0 %ffn_both.1 = (f32[1024,1024]{1,0:T(8,128)}, f32[1024,1024]{1,0:T(8,128)}, bf16[512,2816]{1,0:T(8,128)(2,1)}, bf16[512,2816]{1,0:T(8,128)(2,1)}, bf16[512,2816]{1,0:T(8,128)(2,1)}) custom-call(bf16[1024,1024]{1,0:T(8,128)(2,1)} %copy-done.11, bf16[1024,1024]{1,0:T(8,128)(2,1)} %bitcast.107, bf16[1024,512]{1,0:T(8,128)(2,1)} %get-tuple-element.174.mine_ref, ...), custom_call_target="tpu_custom_call" | custom-call | tf_op jit(solution)/shard_map/ffn_both/pallas_call | solution.py:958
  291.0 1.4 slice.83
  292.4 1.8 slice.84
  294.3 3.5 multiply_reduce_fusion
  298.4 4.3 multiply_add_fusion
  302.7 1.3 convolution_convert_fusion.3
  305.0 5.4 %convolution_convert_fusion.2.gated_grad_ref = bf16[1024,1024]{1,0:T(8,128)(2,1)} fusion(bf16[1024,9472]{1,0:T(8,128)(2,1)} %all-gather.2.cloned.1.call-done.weight_ref, f32[1024,1024]{1,0:T(8,128)S(1)} %get-tuple-element.126), kind=kOutput, calls=%fused_computation.42 | convolution fusion | flops 2149580800 | bytes 8388608 | tf_op jit(solution)/shard_map/te,de->td/dot_general | solution.py:29
  314.0 1.8 dynamic-slice_bitcast_fusion
  315.8 1.8 collective-permute-start.1
  318.0 1.6 copy.71
  319.6 1.4 collective-permute-start.2
  321.1 59.7 %mix_backward.1 = (bf16[1024,3072]{1,0:T(8,128)(2,1)}, f32[1024,512]{1,0:T(8,128)}, f32[8,256]{1,0:T(8,128)}) custom-call(s32[4]{0:T(128)} %prefix_ref.1, bf16[1024,3072]{1,0:T(8,128)(2,1)} %convolution_convert_fusion.1.refs_1_.proj_ref, f32[1024,512]{1,0:T(8,128)} %get-tuple-element.60.cum_ref, bf16[16,3,256,128]{3,2,1,0:T(8,128)(2,1)} %get-tuple-element.61.state_ref, ...), custom_call_target="tpu_custom_call" | custom-call | flops 60000002048 | bytes 220000000 | tf_op jit(solution)/shard_map/mix_backward/pallas_call | solution.py:789
  382.2 3.0 fusion.1
  387.1 3.0 fusion
  390.2 1.4 copy-done.16
  392.9 3.9 collective-permute-start.6
  396.7 9.1 %convolution_convert_fusion = bf16[1024,3072]{1,0:T(8,128)(2,1)} fusion(bf16[1024,1024]{1,0:T(8,128)(2,1)S(1)} %copy-done.10, bf16[1024,3072]{1,0:T(8,128)(2,1)S(1)} %copy-done.40), kind=kOutput, calls=%fused_computation.1 | convolution fusion | flops 6445596672 | bytes 14680064 | tf_op jit(solution)/shard_map/td,te->de/dot_general | solution.py:1086
  408.8 10.8 %fusion.8 = (f32[1024]{0:T(1024)S(1)}, bf16[1024]{0:T(1024)(128)(2,1)S(1)}, f32[1024,1024]{1,0:T(8,128)}) fusion(bf16[4,256,1024]{2,1,0:T(8,128)(2,1)S(1)} %copy-done.7, f32[1024]{0:T(1024)S(1)} %copy-done.35, f32[1024]{0:T(1024)S(1)} %bitcast.124, f32[1024,1024]{1,0:T(8,128)S(1)} %fusion.40, bf16[1024,3072]{1,0:T(8,128)(2,1)} %get-tuple-element.70, ...), kind=kOutput, calls=%fused_computation.19 | convolution fusion | flops 6450837504 | bytes 23083008 | tf_op jit(solution)/shard_map/te,de->td/dot_general | solution.py:29
  424.4 4.0 concatenate.47
  428.4 6.1 %fusion.11 = f32[1024,1024]{1,0:T(8,128)} fusion(f32[1024,1024]{1,0:T(8,128)} %copy-done.15, bf16[4,256,1024]{2,1,0:T(8,128)(2,1)} %param.17, f32[1024,1024]{1,0:T(8,128)} %get-tuple-element.165, f32[1024]{0:T(1024)S(1)} %broadcast_multiply_fusion, f32[1024]{0:T(1024)S(1)} %copy-done.35, f32[1024]{0:T(1024)S(1)} %bitcast.125), kind=kLoop, calls=%fused_computation.22 | loop fusion | flops 7340032 | bytes 14692352 | tf_op jit(solution)/shard_map/add | solution.py:1398
  434.6 1.9 fusion.15.refs_0_
  436.5 1.9 fusion.22.refs_1_
  438.5 59.6 %reduce_rest.1 = (f32[32,4736]{1,0:T(8,128)S(1)}, f32[32,4736]{1,0:T(8,128)S(1)}, f32[32,3072]{1,0:T(8,128)S(1)}, f32[32,128]{1,0:T(8,128)S(1)}) custom-call(bf16[4,32,4736]{2,1,0:T(8,128)(2,1)S(1)} %fusion.15.refs_0_, bf16[2,32,4736]{2,1,0:T(8,128)(2,1)S(1)} %fusion.22.refs_1_, bf16[2,2,2,4,32,3072]{5,4,3,2,1,0:T(8,128)(2,1)S(1)} %bitcast.101, ...), custom_call_target="tpu_custom_call" | custom-call | tf_op jit(solution)/shard_map/reduce_rest/pallas_call | solution.py:1244
  (186 shorter events, 40.1 us)
Async XLA Ops:
  7.2 85.2 %copy-start.6 = (bf16[4,256,1024]{2,1,0:T(8,128)(2,1)S(1)}, bf16[4,256,1024]{2,1,0:T(8,128)(2,1)}, u32[]{:S(2)}) copy-start(bf16[4,256,1024]{2,1,0:T(8,128)(2,1)} %param.17) | copy-start | bytes 6291460
  7.2 197.0 %all-gather.2.cloned.1.call-start = ((), (), s32[]{:S(2)}) async-start(), calls=%async_computation | async-start | bytes 20004864 | tf_op jit(solution)/shard_map/all_gather | solution.py:1314
  92.4 3.6 copy-start.38
  94.8 4.7 slice-start.2
  95.4 4.1 copy-start.32
  95.4 4.1 slice-start.3
  99.5 9.0 %copy-start.1 = (s32[4]{0:T(128)S(1)}, s32[4]{0:T(128)}, u32[]{:S(2)}) copy-start(s32[4]{0:T(128)} %prefix_ref.1) | copy-start | bytes 52
  108.5 91.5 %copy-start = (f32[8,256]{1,0:T(8,128)}, f32[8,256]{1,0:T(8,128)S(1)}, u32[]{:S(2)}) copy-start(f32[8,256]{1,0:T(8,128)S(1)} %broadcast_in_dim.53.refs_3_.gain_ref) | copy-start | bytes 24580
  108.5 91.5 %copy-start.12 = (bf16[4,256,1024]{2,1,0:T(8,128)(2,1)S(1)}, bf16[4,256,1024]{2,1,0:T(8,128)(2,1)}, u32[]{:S(2)}) copy-start(bf16[4,256,1024]{2,1,0:T(8,128)(2,1)} %param.33) | copy-start | bytes 6291460
  294.3 4.1 copy-start.14
  302.7 8.1 %copy-start.15 = (f32[1024,1024]{1,0:T(8,128)}, f32[1024,1024]{1,0:T(8,128)S(1)}, u32[]{:S(2)}) copy-start(f32[1024,1024]{1,0:T(8,128)S(1)} %get-tuple-element.126) | copy-start | bytes 12582916
  304.0 6.8 %collective-permute-start = (bf16[512,1024]{1,0:T(8,128)(2,1)S(1)}, bf16[512,1024]{1,0:T(8,128)(2,1)S(1)}, u32[]{:S(2)}, u32[]{:S(2)}) collective-permute-start(bf16[512,1024]{1,0:T(8,128)(2,1)S(1)} %convolution_convert_fusion.3), channel_id=1, source_target_pairs={{0,4},{4,0},{1,5},{5,1},{2,6},{6,2},{3,7},{7,3},{8,12},{12,8},{9,1... | collective-permute-start | bytes 3145736 | tf_op jit(solution)/shard_map/ppermute | solution.py:1076
  305.0 5.4 %copy-start.22 = (bf16[512,2816]{1,0:T(8,128)(2,1)S(1)}, bf16[512,2816]{1,0:T(8,128)(2,1)}, u32[]{:S(2)}) copy-start(bf16[512,2816]{1,0:T(8,128)(2,1)} %get-tuple-element.57) | copy-start | bytes 8650756
  314.0 4.0 copy-start.8
  315.8 66.4 %collective-permute-start.1 = (bf16[2,4,32,4736]{3,2,1,0:T(8,128)(2,1)}, bf16[2,4,32,4736]{3,2,1,0:T(8,128)(2,1)}, u32[]{:S(2)}, u32[]{:S(2)}) collective-permute-start(bf16[2,4,32,4736]{3,2,1,0:T(8,128)(2,1)} %dynamic-slice_bitcast_fusion), channel_id=1, source_target_pairs={{0,16},{16,0},{1,17},{17,1},{2,18},{18,2},{3,19},{19,3},{4,20},{20... | collective-permute-start | bytes 7274504 | tf_op jit(solution)/shard_map/ppermute | solution.py:1102
  319.6 62.6 %collective-permute-start.2 = (bf16[2,4,32,4736]{3,2,0,1:T(8,128)(2,1)}, bf16[2,4,32,4736]{3,2,0,1:T(8,128)(2,1)}, u32[]{:S(2)}, u32[]{:S(2)}) collective-permute-start(bf16[2,4,32,4736]{3,2,0,1:T(8,128)(2,1)} %bitcast.97), channel_id=1, source_target_pairs={{0,8},{8,0},{1,9},{9,1},{2,10},{10,2},{3,11},{11,3},{4,12},{12,4},... | collective-permute-start | bytes 7274504 | tf_op jit(solution)/shard_map/ppermute | solution.py:1102
  385.2 11.5 %copy-start.40 = (bf16[1024,3072]{1,0:T(8,128)(2,1)S(1)}, bf16[1024,3072]{1,0:T(8,128)(2,1)}, u32[]{:S(2)}) copy-start(bf16[1024,3072]{1,0:T(8,128)(2,1)} %get-tuple-element.70) | copy-start | bytes 18874372
  386.4 48.2 %collective-permute-start.3 = (bf16[4,32,4736]{2,1,0:T(8,128)(2,1)}, bf16[4,32,4736]{2,1,0:T(8,128)(2,1)}, u32[]{:S(2)}, u32[]{:S(2)}) collective-permute-start(bf16[4,32,4736]{2,1,0:T(8,128)(2,1)} %dynamic-slice_bitcast_fusion.1), channel_id=1, source_target_pairs={{0,8},{8,0},{1,9},{9,1},{2,10},{10,2},{3,11},{11,3},{4,12},{12,4},... | collective-permute-start | bytes 3637256 | tf_op jit(solution)/shard_map/ppermute | solution.py:1102
  387.1 20.8 %slice-start.4 = ((s8[6291456]{0:T(1024)(128)(4,1)}), s8[4194304]{0:T(1024)(128)(4,1)S(1)}, s32[]{:S(2)}) async-start(s8[6291456]{0:T(1024)(128)(4,1)} %bitcast.133), calls=%async_computation.5 | async-start | bytes 8388608
  391.6 5.2 %copy-start.10 = (bf16[1024,1024]{1,0:T(8,128)(2,1)S(1)}, bf16[1024,1024]{1,0:T(8,128)(2,1)}, u32[]{:S(2)}) copy-start(bf16[1024,1024]{1,0:T(8,128)(2,1)} %copy-done.9) | copy-start | bytes 6291460
  392.8 41.8 %collective-permute-start.4 = (bf16[2,32,4736]{2,1,0:T(8,128)(2,1)}, bf16[2,32,4736]{2,1,0:T(8,128)(2,1)}, u32[]{:S(2)}, u32[]{:S(2)}) collective-permute-start(bf16[2,32,4736]{2,1,0:T(8,128)(2,1)} %get-tuple-element.130), channel_id=1, source_target_pairs={{0,1},{1,2},{2,3},{3,0},{4,5},{5,6},{6,7},{7,4},{8,9},{9,10},{10,1... | collective-permute-start | bytes 1818632 | tf_op jit(solution)/shard_map/ppermute | solution.py:1102
  392.8 41.8 %collective-permute-start.5 = (bf16[2,32,4736]{2,1,0:T(8,128)(2,1)}, bf16[2,32,4736]{2,1,0:T(8,128)(2,1)}, u32[]{:S(2)}, u32[]{:S(2)}) collective-permute-start(bf16[2,32,4736]{2,1,0:T(8,128)(2,1)} %get-tuple-element.129), channel_id=1, source_target_pairs={{0,2},{1,3},{2,0},{3,1},{4,6},{5,7},{6,4},{7,5},{8,10},{9,11},{10,... | collective-permute-start | bytes 1818632 | tf_op jit(solution)/shard_map/ppermute | solution.py:1102
  392.8 13.0 %copy-start.23 = (f32[1024,512]{1,0:T(8,128)S(1)}, f32[1024,512]{1,0:T(8,128)}, u32[]{:S(2)}) copy-start(f32[1024,512]{1,0:T(8,128)} %get-tuple-element.162) | copy-start | bytes 6291460
  392.8 13.0 %copy-start.24 = (f32[1024,512]{1,0:T(8,128)S(1)}, f32[1024,512]{1,0:T(8,128)}, u32[]{:S(2)}) copy-start(f32[1024,512]{1,0:T(8,128)} %get-tuple-element.71) | copy-start | bytes 6291460
  392.8 13.0 %copy-start.39 = (f32[512]{0:T(512)S(1)}, f32[512]{0:T(512)}, u32[]{:S(2)}) copy-start(f32[512]{0:T(512)} %copy-done.38) | copy-start | bytes 6148
  392.9 15.1 %slice-start.5 = ((s8[6291456]{0:T(1024)(128)(4,1)}), s8[2097152]{0:T(1024)(128)(4,1)S(1)}, s32[]{:S(2)}) async-start(s8[6291456]{0:T(1024)(128)(4,1)} %bitcast.133), calls=%async_computation.6 | async-start | bytes 4194304
  392.9 41.7 %collective-permute-start.6 = (bf16[2,32,4736]{2,1,0:T(8,128)(2,1)}, bf16[2,32,4736]{2,1,0:T(8,128)(2,1)}, u32[]{:S(2)}, u32[]{:S(2)}) collective-permute-start(bf16[2,32,4736]{2,1,0:T(8,128)(2,1)} %get-tuple-element.128), channel_id=1, source_target_pairs={{0,3},{1,0},{2,1},{3,2},{4,7},{5,4},{6,5},{7,6},{8,11},{9,8},{10,9... | collective-permute-start | bytes 1818632 | tf_op jit(solution)/shard_map/ppermute | solution.py:1102
  408.8 10.8 %copy-start.33 = (bf16[1024,16]{0,1:T(8,128)(2,1)S(1)}, bf16[1024,16]{0,1:T(8,128)(2,1)}, u32[]{:S(2)}) copy-start(bf16[1024,16]{0,1:T(8,128)(2,1)} %copy-done.32) | copy-start | bytes 98308
  419.6 4.9 copy-start.25
  424.4 14.1 %slice-start = ((s8[6291456]{0:T(1024)(128)(4,1)}), s8[2097152]{0:T(1024)(128)(4,1)S(1)}, s32[]{:S(2)}) async-start(s8[6291456]{0:T(1024)(128)(4,1)} %bitcast.99), calls=%async_computation.1 | async-start | bytes 4194304
  428.4 6.2 %copy-start.18 = (bf16[2,4,32,4736]{3,2,1,0:T(8,128)(2,1)S(1)}, bf16[2,4,32,4736]{3,2,1,0:T(8,128)(2,1)}, u32[]{:S(2)}) copy-start(bf16[2,4,32,4736]{3,2,1,0:T(8,128)(2,1)} %copy-done.17) | copy-start | bytes 7274500
  428.4 10.1 %slice-start.1 = ((s8[6291456]{0:T(1024)(128)(4,1)}), s8[4194304]{0:T(1024)(128)(4,1)S(1)}, s32[]{:S(2)}) async-start(s8[6291456]{0:T(1024)(128)(4,1)} %bitcast.99), calls=%async_computation.2 | async-start | bytes 8388608
  (23 other events, 41.4 us)
Sparse Core Ops, SparseCore 0:
  11.4 169.1 all-gather.1
